TPU v7x, 32 devices: a whole 2x2x4 slice. The times are simulated.
32 devices in a mesh: gx: 2 (over x), gy: 4 (over y, core), gz: 4 (over z).
Axes of the slice: x: 2, y: 2, z: 4, core: 2. Of those that a mesh axis runs over, the one named last changes fastest.
Arguments:
- t_matrix: float32 [1, 2, 4, 16, 1024], P(None, 'gx', 'gy', 'gz'), may hold values from -3 to 3
- structure: float32 [1, 1440, 1440], replicated, may hold values from -0.0390625 to 0.0390625
- species: int32 [2, 4, 16], P('gx', 'gy', 'gz'), may hold values from 0 to 3
- members: int32 [2, 4, 16, 45], P('gx', 'gy', 'gz'), may hold values from -1 to 44, as said below
- delta_table: float32 [4, 1024], replicated, may hold values from -4 to 4
Outputs:
- site_tau: float32 [1, 2, 4, 16, 1024], P(None, 'gx', 'gy', 'gz')
- pair_terms: float32 [2, 4, 16, 45], P('gx', 'gy', 'gz')
Inputs may be any that keep to these rules, and one draw needn't show every extreme that they name: `members`: each site's list names distinct window cells, the centre cell first, 27 to 45 of them, then -1 in the remaining slots; in every draw some site lists all 45 cells.
All inputs are finite; a program needn't handle non-finite values.
Results may differ from a plain program's by a relative error of at most 0.00013.
Values sent between devices are 32-bit elements; how exact they have to be, the bound alone decides.
No kernel may reach another device: no remote copies, remote signals or barrier semaphores. Data moves between devices by JAX's collectives and lax.ppermute only.
A program may use at most 192 MiB of HBM per device.

v0:
```python
import functools

import jax
import jax.numpy as jnp
import numpy as np
from jax import lax
from jax.experimental import pallas as pl
from jax.experimental.pallas import tpu as pltpu
from jax.sharding import PartitionSpec as P

L2 = 32
WINDOW = 45
ITERS = 4
SPECIES = 4
DEPTH = 4
LANES = DEPTH * L2
ROWS = WINDOW * L2
CENTRE = WINDOW // 2
GROUP = 9
CHUNK = GROUP * L2
CHUNKS = WINDOW // GROUP
MESH_AXES = ("gx", "gy", "gz")

bf16 = jnp.bfloat16
f32 = jnp.float32
highest = lax.Precision.HIGHEST
MIB = 1 << 20


def shifted(x, shift):
    sizes = [lax.axis_size(axis) for axis in MESH_AXES]
    pairs = []
    for source in np.ndindex(*sizes):
        target = [(i + d) % n for i, d, n in zip(source, shift, sizes)]
        pairs.append(
            (int(np.ravel_multi_index(source, sizes)), int(np.ravel_multi_index(target, sizes)))
        )
    return lax.ppermute(x, MESH_AXES, pairs)


def in_vmem(count):
    return [pl.BlockSpec(memory_space=pltpu.VMEM)] * count


def halves(x):
    high = x.astype(bf16)
    return high, (x - high.astype(f32)).astype(bf16)


def lane_index(shape):
    return lax.broadcasted_iota(jnp.int32, shape, len(shape) - 1)


def tile_kernel(flat_ref, tile_ref):
    row = lax.broadcasted_iota(jnp.int32, (DEPTH, LANES), 0)
    diagonal = lane_index((DEPTH, LANES)) // L2 == row
    for j in range(L2 // DEPTH):
        part = flat_ref[:, j * LANES : (j + 1) * LANES]
        rolled = [part] + [pltpu.roll(part, m * L2, 1) for m in range(1, DEPTH)]
        for k in range(DEPTH):
            picked = jnp.zeros((DEPTH, LANES), f32)
            for m in range(DEPTH):
                picked = jnp.where(diagonal & (row == (m + k) % DEPTH), rolled[m], picked)
            a = j * DEPTH + k
            tile_ref[a : a + 1, :] = jnp.sum(picked, axis=0, keepdims=True)


def own_tile(flat):
    return pl.pallas_call(
        tile_kernel,
        out_shape=jax.ShapeDtypeStruct((L2, LANES), f32),
        in_specs=in_vmem(1),
        out_specs=in_vmem(1)[0],
        compiler_params=pltpu.CompilerParams(vmem_limit_bytes=4 * MIB),
        name="own_tile",
    )(flat)


def split_kernel(structure_ref, own_ref, high_ref, low_ref, image_ref, buffer, sems):
    def fetch(step):
        return pltpu.make_async_copy(
            structure_ref.at[pl.ds(step * CHUNK, CHUNK), :],
            buffer.at[step % 2],
            sems.at[step % 2],
        )

    fetch(0).start()
    own_high, own_low = halves(own_ref[...])
    for step in range(CHUNKS):
        if step + 1 < CHUNKS:
            fetch(step + 1).start()
        fetch(step).wait()
        rows = pl.ds(step * CHUNK, CHUNK)
        for q in range(GROUP):
            part = pl.ds(q * L2, L2)
            high, low = halves(buffer[step % 2, part, :])
            high_ref[pl.ds(step * CHUNK + q * L2, L2), :] = high
            low_ref[pl.ds(step * CHUNK + q * L2, L2), :] = low
        columns = pl.ds(CENTRE * L2, L2)
        centre_high, centre_low = halves(buffer[step % 2, :, columns])
        image_ref[rows, :] = (
            jnp.dot(centre_high, own_high, preferred_element_type=f32)
            + jnp.dot(centre_high, own_low, preferred_element_type=f32)
            + jnp.dot(centre_low, own_high, preferred_element_type=f32)
        )


def split_structure(structure, own):
    return pl.pallas_call(
        split_kernel,
        out_shape=(
            jax.ShapeDtypeStruct((ROWS, ROWS), bf16),
            jax.ShapeDtypeStruct((ROWS, ROWS), bf16),
            jax.ShapeDtypeStruct((ROWS, LANES), f32),
        ),
        in_specs=[pl.BlockSpec(memory_space=pl.ANY)] + in_vmem(1),
        out_specs=tuple(in_vmem(3)),
        scratch_shapes=[pltpu.VMEM((2, CHUNK, ROWS), f32), pltpu.SemaphoreType.DMA((2,))],
        compiler_params=pltpu.CompilerParams(vmem_limit_bytes=24 * MIB),
        cost_estimate=pl.CostEstimate(
            flops=2 * 3 * ROWS * L2 * LANES, bytes_accessed=4 * ROWS * ROWS, transcendentals=0
        ),
        name="split_structure",
    )(structure, own)


def window_tile(near_ref, cell):
    dx, dy, dz = cell // 15, cell // 5 % 3, cell % 5 - 2
    dx = dx % near_ref.shape[1]
    own = near_ref[dy, dx, 0]
    if dz == 0:
        return own
    lane = lane_index((L2, LANES))
    if dz > 0:
        joined = jnp.where(lane < dz * L2, near_ref[dy, dx, 2], own)
        return pltpu.roll(joined, LANES - dz * L2, 1)
    joined = jnp.where(lane >= LANES + dz * L2, near_ref[dy, dx, 1], own)
    return pltpu.roll(joined, -dz * L2, 1)


def sweep_kernel(
    groups, high_ref, low_ref, image_ref, near_ref, member_ref, own_ref, delta_ref, *rest
):
    sent = rest[: len(groups)]
    tau_ref, window, column = rest[len(groups) :]
    lane = lane_index((L2, LANES))
    masks = [(lane // L2 == s).astype(f32).astype(bf16) for s in range(DEPTH)]

    def apply(cell, image):
        high, low = halves(image)
        high_blocks = jnp.concatenate([high * mask for mask in masks], axis=0)
        low_blocks = jnp.concatenate([low * mask for mask in masks], axis=0)
        both = jnp.concatenate([high_blocks, low_blocks], axis=1)
        rows = pl.ds(cell * L2, L2)
        first = jnp.dot(window[rows, :LANES], both, preferred_element_type=f32)
        second = jnp.dot(window[rows, LANES:], high_blocks, preferred_element_type=f32)
        return first[:, :LANES] + first[:, LANES:] + second

    def keep(slot, cell, value):
        high, low = halves(value)
        rows = pl.ds(cell * L2, L2)
        column[slot, rows, :LANES] = high
        column[slot, rows, LANES:] = low

    for cell in range(WINDOW):
        value = window_tile(near_ref, cell) * member_ref[cell : cell + 1, :]
        high, low = halves(value)
        window[cell * L2 : (cell + 1) * L2, :LANES] = high
        window[cell * L2 : (cell + 1) * L2, LANES:] = low
    for cell in range(WINDOW):
        value = apply(cell, image_ref[cell * L2 : (cell + 1) * L2, :])
        if cell == CENTRE:
            value = value + own_ref[...]
        keep(0, cell, value)

    for sweep in range(1, ITERS):
        now, later = (sweep - 1) % 2, sweep % 2

        def chunk_step(chunk, carry, now=now, later=later, last=sweep == ITERS - 1):
            rows = pl.ds(pl.multiple_of(chunk * CHUNK, CHUNK), CHUNK)
            first = jnp.dot(high_ref[rows, :], column[now], preferred_element_type=f32)
            second = jnp.dot(low_ref[rows, :], column[now, :, :LANES], preferred_element_type=f32)
            image = first[:, :LANES] + first[:, LANES:] + second
            for q in range(GROUP):
                cell = chunk * GROUP + q
                value = apply(cell, image[q * L2 : (q + 1) * L2])
                if q == CENTRE % GROUP:
                    value = value + jnp.where(chunk == CENTRE // GROUP, own_ref[...], 0.0)
                    if last:
                        @pl.when(chunk == CENTRE // GROUP)
                        def _():
                            tau_ref[...] = value
                keep(later, cell, value)
            return carry

        lax.fori_loop(0, CHUNKS, chunk_step, 0)

    final = (ITERS - 1) % 2
    high, low = halves(delta_ref[...])
    delta = jnp.concatenate(
        [
            jnp.concatenate([high, low], axis=1),
            jnp.concatenate([high, jnp.zeros_like(high)], axis=1),
        ],
        axis=0,
    )
    for group, ref in zip(groups, sent):
        for place, (ox, oy) in enumerate(group):
            base = ((ox + 1) * 3 + oy + 1) * 5 * L2
            rows = slice(base, base + 5 * L2)
            product = jnp.dot(column[final, rows, :], delta, preferred_element_type=f32)
            value = product[:, :LANES] + product[:, LANES:]
            ref[place * 5 : place * 5 + 5] = value.reshape(5, L2, LANES)


def sweeps(groups, high, low, image, near, member, own, delta):
    out_shape = [jax.ShapeDtypeStruct((5 * len(group), L2, LANES), f32) for group in groups]
    out_shape.append(jax.ShapeDtypeStruct((L2, LANES), f32))
    flops = 2 * 3 * (ITERS - 1) * ROWS * ROWS * LANES
    return pl.pallas_call(
        functools.partial(sweep_kernel, groups),
        out_shape=tuple(out_shape),
        in_specs=in_vmem(7),
        out_specs=tuple(in_vmem(len(out_shape))),
        scratch_shapes=[
            pltpu.VMEM((ROWS, 2 * LANES), bf16),
            pltpu.VMEM((2, ROWS, 2 * LANES), bf16),
        ],
        compiler_params=pltpu.CompilerParams(vmem_limit_bytes=32 * MIB),
        cost_estimate=pl.CostEstimate(flops=flops, bytes_accessed=10 * MIB, transcendentals=0),
        name="sweeps",
    )(high, low, image, near, member, own, delta)


def find_tile(groups, refs, ox, oy, oz):
    for group, ref in zip(groups, refs):
        if (ox, oy) in group:
            return ref[group.index((ox, oy)) * 5 + oz + 2]
    raise ValueError("no tile")


def turn_kernel(groups, *refs):
    own, out = refs[:-1], refs[-1]
    lane = lane_index((L2, LANES))

    def cell_tile(cell):
        cell = min(cell, WINDOW - 1)
        return find_tile(groups, own, cell // 15 - 1, cell // 5 % 3 - 1, cell % 5 - 2)

    for base in range(0, WINDOW, DEPTH):
        block = jnp.concatenate([cell_tile(base + k) for k in range(DEPTH)], axis=0)
        turned = block.T
        pieces = [turned[s * L2 : (s + 1) * L2] for s in range(DEPTH)]
        for k in range(min(DEPTH, WINDOW - base)):
            value = pieces[0] if k == 0 else pltpu.roll(pieces[0], (-k % DEPTH) * L2, 1)
            for s in range(1, DEPTH):
                move = (s - k) % DEPTH
                piece = pieces[s] if move == 0 else pltpu.roll(pieces[s], move * L2, 1)
                value = jnp.where(lane // L2 == s, piece, value)
            out[base + k] = value


def turned_tiles(groups, own):
    return pl.pallas_call(
        functools.partial(turn_kernel, groups),
        out_shape=jax.ShapeDtypeStruct((WINDOW, L2, LANES), f32),
        in_specs=in_vmem(len(own)),
        out_specs=in_vmem(1)[0],
        compiler_params=pltpu.CompilerParams(vmem_limit_bytes=8 * MIB),
        cost_estimate=pl.CostEstimate(flops=MIB, bytes_accessed=2 * MIB, transcendentals=0),
        name="turned_tiles",
    )(*own)


def plane_offsets():
    return [(ox, oy) for ox in (-1, 0, 1) for oy in (-1, 0, 1)]


def pack_kernel(groups, *refs):
    got = refs[:-2]
    down_ref, up_ref = refs[-2:]
    lane = lane_index((L2, LANES))
    for place, (ox, oy) in enumerate(plane_offsets()):
        far = pltpu.roll(find_tile(groups, got, ox, oy, -2), 2 * L2, 1)
        down_ref[place] = jnp.where(lane >= 2 * L2, far, find_tile(groups, got, ox, oy, -1))
        far = pltpu.roll(find_tile(groups, got, ox, oy, 2), 2 * L2, 1)
        up_ref[place] = jnp.where(lane < 2 * L2, far, find_tile(groups, got, ox, oy, 1))


def packed_edges(groups, got):
    shape = jax.ShapeDtypeStruct((9, L2, LANES), f32)
    return pl.pallas_call(
        functools.partial(pack_kernel, groups),
        out_shape=(shape, shape),
        in_specs=in_vmem(len(got)),
        out_specs=tuple(in_vmem(2)),
        compiler_params=pltpu.CompilerParams(vmem_limit_bytes=8 * MIB),
        name="packed_edges",
    )(*got)


def pair_kernel(groups, *refs):
    got = refs[: len(groups)]
    above_ref, below_ref, turned_ref, out_ref, sums = refs[len(groups) :]
    lane = lane_index((L2, LANES))
    for place, (ox, oy) in enumerate(plane_offsets()):
        above, below = above_ref[place], below_ref[place]
        for dz in range(-2, 3):
            tile = find_tile(groups, got, ox, oy, -dz)
            if dz == 1:
                tile = pltpu.roll(jnp.where(lane >= L2, tile, above), 3 * L2, 1)
            elif dz == 2:
                tile = jnp.where(lane < 2 * L2, pltpu.roll(tile, 2 * L2, 1), above)
            elif dz == -1:
                tile = pltpu.roll(jnp.where(lane < 3 * L2, tile, below), L2, 1)
            elif dz == -2:
                tile = jnp.where(lane >= 2 * L2, pltpu.roll(tile, 2 * L2, 1), below)
            cell = ((1 - ox) * 3 + 1 - oy) * 5 + dz + 2
            sums[cell : cell + 1, :] = jnp.sum(tile * turned_ref[cell], axis=0, keepdims=True)
    site = lax.broadcasted_iota(jnp.int32, (8, LANES), 0)
    pick = (lane_index((8, LANES)) // L2 == site).astype(f32)
    total = lax.dot_general(
        pick, sums[...], (((1,), (1,)), ((), ())), precision=highest, preferred_element_type=f32
    )
    out_ref[...] = total[:DEPTH, :WINDOW]


def pair_sums(groups, got, above, below, turned):
    return pl.pallas_call(
        functools.partial(pair_kernel, groups),
        out_shape=jax.ShapeDtypeStruct((DEPTH, WINDOW), f32),
        in_specs=in_vmem(len(got) + 3),
        out_specs=in_vmem(1)[0],
        scratch_shapes=[pltpu.VMEM((48, LANES), f32)],
        compiler_params=pltpu.CompilerParams(vmem_limit_bytes=8 * MIB),
        name="pair_sums",
    )(*got, above, below, turned)


def plane_groups():
    counts = (lax.axis_size("gx"), lax.axis_size("gy"))
    groups = {}
    for ox, oy in plane_offsets():
        groups.setdefault((ox % counts[0], oy % counts[1]), []).append((ox, oy))
    return groups


def near_tiles(own):
    column = jnp.stack([own, shifted(own, (0, 0, 1)), shifted(own, (0, 0, -1))])
    if lax.axis_size("gx") == 2:
        sides = [shifted(column, (1, 0, 0)), column]
    else:
        sides = [shifted(column, (1, 0, 0)), column, shifted(column, (-1, 0, 0))]
    plane = jnp.stack(sides)
    planes = [shifted(plane, (0, 1, 0)), plane, shifted(plane, (0, -1, 0))]
    return jnp.stack(planes)


def body(t_matrix, structure, species, members, delta_table):
    own = own_tile(t_matrix.reshape(DEPTH, L2 * L2))
    near = near_tiles(own)
    high, low, image = split_structure(structure[0], own)

    window_cells = jnp.arange(WINDOW, dtype=jnp.int32)
    member = jnp.any(members[0, 0][..., None] == window_cells, axis=-2).astype(f32).T
    member = jnp.repeat(member, L2, axis=1)
    onehot = (species.reshape(DEPTH, 1) == jnp.arange(SPECIES, dtype=jnp.int32)).astype(f32)
    delta = jnp.dot(onehot, delta_table, precision=highest, preferred_element_type=f32)
    delta = delta.reshape(DEPTH, L2, 1, L2) * jnp.eye(DEPTH, dtype=f32)[:, None, :, None]
    delta = delta.reshape(LANES, LANES)

    table = plane_groups()
    shifts, groups = list(table), list(table.values())
    *sent, tau = sweeps(groups, high, low, image, near, member, own, delta)
    got = [
        block if shift == (0, 0) else shifted(block, shift + (0,))
        for shift, block in zip(shifts, sent)
    ]
    turned = turned_tiles(groups, sent)
    down, up = packed_edges(groups, got)
    above = shifted(down, (0, 0, -1))
    below = shifted(up, (0, 0, 1))
    pairs = pair_sums(groups, got, above, below, turned)
    site_tau = jnp.transpose(tau.reshape(L2, DEPTH, L2), (1, 0, 2))
    return (
        site_tau.reshape(1, 1, 1, DEPTH, L2 * L2),
        pairs.reshape(1, 1, DEPTH, WINDOW),
    )


def solution(mesh):
    placed = (
        P(None, "gx", "gy", "gz", None),
        P(),
        P("gx", "gy", "gz"),
        P("gx", "gy", "gz", None),
        P(),
    )
    return jax.shard_map(
        body,
        mesh=mesh,
        in_specs=placed,
        out_specs=(P(None, "gx", "gy", "gz", None), P("gx", "gy", "gz", None)),
        check_vma=False,
    )
```

profile of v0, /device:TPU:0, one launch (start us, length us, event | category | flops | bytes accessed | tf_op | source)
XLA Modules:
  0.0 64.6 jit_solution(17242247511813813615)
XLA Ops:
  0.6 0.0 copy-start
  0.6 0.0 copy-start.2
  0.7 0.7 %copy-done.2 = f32[1,1,1,4,1024]{4,3,2,1,0:T(4,128)S(1)} copy-done((f32[1,1,1,4,1024]{4,3,2,1,0:T(4,128)S(1)}, f32[1,1,1,4,1024]{4,3,2,1,0:T(4,128)}, u32[]{:S(2)}) %copy-start.2) | copy-done | bytes 16408
  1.4 0.1 own_tile.1.own_ref
  1.5 5.1 %collective-permute-start.1 = (f32[32,128]{1,0:T(8,128)S(1)}, f32[32,128]{1,0:T(8,128)S(1)}, u32[]{:S(2)}, u32[]{:S(2)}) collective-permute-start(f32[32,128]{1,0:T(8,128)S(1)} %own_tile.1.own_ref), channel_id=1, source_target_pairs={{0,3},{1,0},{2,1},{3,2},{4,7},{5,4},{6,5},{7,6},{8,11},{9,8},{10,9... | collective-permute-start | bytes 49160 | tf_op jit(solution)/shard_map/ppermute | solution.py:38
  6.6 0.0 collective-permute-start
  6.6 0.0 copy-done
  6.6 0.9 %fusion.1 = f32[4,1024]{1,0:T(4,128)S(1)} fusion(f32[4,1024]{1,0:T(4,128)S(1)} %copy-done, s32[4]{0:T(128)} %bitcast.30), kind=kOutput, calls=%fused_computation.9 | convolution fusion | flops 196624 | bytes 32784 | tf_op jit(solution)/shard_map/dot_general | solution.py:368
  7.5 0.1 mul.19
  7.6 0.1 broadcast_multiply_fusion
  7.7 0.8 %copy.9 = s32[4,45]{0,1:T(8,128)S(1)} copy(s32[4,45]{1,0:T(4,128)} %bitcast.28) | data formatting | bytes 1440 | tf_op jit(solution)/shard_map/eq | solution.py:365
  8.5 0.0 collective-permute-done.1
  8.5 3.7 %collective-permute-done = f32[32,128]{1,0:T(8,128)S(1)} collective-permute-done((f32[32,128]{1,0:T(8,128)S(1)}, f32[32,128]{1,0:T(8,128)S(1)}, u32[]{:S(2)}, u32[]{:S(2)}) %collective-permute-start) | collective-permute-done | bytes 16416 | tf_op jit(solution)/shard_map/ppermute | solution.py:38
  12.2 1.6 %collective-permute-start.2 = (f32[3,32,128]{2,1,0:T(8,128)S(1)}, f32[3,32,128]{2,1,0:T(8,128)S(1)}, u32[]{:S(2)}, u32[]{:S(2)}) collective-permute-start(f32[3,32,128]{2,1,0:T(8,128)S(1)} %get-tuple-element.28), channel_id=1, source_target_pairs={{0,16},{1,17},{2,18},{3,19},{4,20},{5,21},{6,22},{7,23},{8,24},{9,... | collective-permute-start | bytes 147464 | tf_op jit(solution)/shard_map/ppermute | solution.py:38
  13.7 0.1 fusion
  13.9 2.5 %collective-permute-done.2 = f32[3,32,128]{2,1,0:T(8,128)S(1)} collective-permute-done((f32[3,32,128]{2,1,0:T(8,128)S(1)}, f32[3,32,128]{2,1,0:T(8,128)S(1)}, u32[]{:S(2)}, u32[]{:S(2)}) %collective-permute-start.2) | collective-permute-done | bytes 49184 | tf_op jit(solution)/shard_map/ppermute | solution.py:38
  16.3 0.1 collective-permute-start.4
  16.4 0.5 collective-permute-start.3
  16.9 0.1 copy.10
  17.0 0.1 broadcast_in_dim.2
  17.1 0.1 reshape.37.member_ref
  17.2 0.2 mul.23.delta_ref
  17.4 0.0 copy-start.1
  17.4 3.5 %copy-done.1 = f32[1,1440,1440]{2,1,0:T(8,128)S(1)} copy-done((f32[1,1440,1440]{2,1,0:T(8,128)S(1)}, f32[1,1440,1440]{2,1,0:T(8,128)}, u32[]{:S(2)}) %copy-start.1) | copy-done | bytes 8294424
  20.9 5.0 %split_structure.1 = (bf16[1440,1440]{1,0:T(8,128)(2,1)S(1)}, bf16[1440,1440]{1,0:T(8,128)(2,1)S(1)}, f32[1440,128]{1,0:T(8,128)S(1)}) custom-call(f32[1440,1440]{1,0:T(8,128)S(1)} %bitcast.19, f32[32,128]{1,0:T(8,128)S(1)} %own_tile.1.own_ref), custom_call_target="tpu_custom_call" | custom-call | flops 35389440 | bytes 8294400 | tf_op jit(solution)/shard_map/split_structure/pallas_call | solution.py:109
  26.0 0.0 collective-permute-done.4
  26.0 0.0 collective-permute-done.3
  26.0 14.6 %sweeps.1 = (f32[10,32,128]{2,1,0:T(8,128)S(1)}, f32[10,32,128]{2,1,0:T(8,128)S(1)}, f32[10,32,128]{2,1,0:T(8,128)S(1)}, f32[5,32,128]{2,1,0:T(8,128)S(1)}, f32[...) custom-call(bf16[1440,1440]{1,0:T(8,128)(2,1)S(1)} %get-tuple-element.14.high_ref, ...), custom_call_target="tpu_custom_call" | custom-call | flops 4777574400 | bytes 10485760 | tf_op jit(solution)/shard_map/sweeps/pallas_call | solution.py:220
  40.6 2.3 %collective-permute-start.5 = (f32[10,32,128]{2,1,0:T(8,128)S(1)}, f32[10,32,128]{2,1,0:T(8,128)S(1)}, u32[]{:S(2)}, u32[]{:S(2)}) collective-permute-start(f32[10,32,128]{2,1,0:T(8,128)S(1)} %get-tuple-element.18.refs_0_), channel_id=1, source_target_pairs={{0,28},{1,29},{2,30},{3,31},{4,16},{5,17},{6,18},{7,19},{8,20},{9,... | collective-permute-start | bytes 491528 | tf_op jit(solution)/shard_map/ppermute | solution.py:38
  42.9 0.5 collective-permute-start.6
  43.4 0.2 collective-permute-start.7
  43.6 2.5 %collective-permute-start.8 = (f32[5,32,128]{2,1,0:T(8,128)S(1)}, f32[5,32,128]{2,1,0:T(8,128)S(1)}, u32[]{:S(2)}, u32[]{:S(2)}) collective-permute-start(f32[5,32,128]{2,1,0:T(8,128)S(1)} %get-tuple-element.21.refs_3_), channel_id=1, source_target_pairs={{0,12},{1,13},{2,14},{3,15},{4,0},{5,1},{6,2},{7,3},{8,4},{9,5},{1... | collective-permute-start | bytes 245768 | tf_op jit(solution)/shard_map/ppermute | solution.py:38
  46.1 0.0 collective-permute-start.9
  46.1 2.1 %collective-permute-done.8.refs_3_ = f32[5,32,128]{2,1,0:T(8,128)S(1)} collective-permute-done((f32[5,32,128]{2,1,0:T(8,128)S(1)}, f32[5,32,128]{2,1,0:T(8,128)S(1)}, u32[]{:S(2)}, u32[]{:S(2)}) %collective-permute-start.8) | collective-permute-done | bytes 81952 | tf_op jit(solution)/shard_map/ppermute | solution.py:38
  48.2 3.4 %collective-permute-done.9.refs_5_ = f32[5,32,128]{2,1,0:T(8,128)S(1)} collective-permute-done((f32[5,32,128]{2,1,0:T(8,128)S(1)}, f32[5,32,128]{2,1,0:T(8,128)S(1)}, u32[]{:S(2)}, u32[]{:S(2)}) %collective-permute-start.9) | collective-permute-done | bytes 81952 | tf_op jit(solution)/shard_map/ppermute | solution.py:38
  51.6 0.0 collective-permute-done.5.refs_0_
  51.7 0.3 collective-permute-done.6.refs_1_
  52.0 1.9 %collective-permute-done.7.refs_2_ = f32[10,32,128]{2,1,0:T(8,128)S(1)} collective-permute-done((f32[10,32,128]{2,1,0:T(8,128)S(1)}, f32[10,32,128]{2,1,0:T(8,128)S(1)}, u32[]{:S(2)}, u32[]{:S(2)}) %collective-permute-start.7) | collective-permute-done | bytes 163872 | tf_op jit(solution)/shard_map/ppermute | solution.py:38
  53.8 0.1 packed_edges.1
  54.0 0.2 collective-permute-start.10
  54.2 1.9 %collective-permute-start.11 = (f32[9,32,128]{2,1,0:T(8,128)S(1)}, f32[9,32,128]{2,1,0:T(8,128)S(1)}, u32[]{:S(2)}, u32[]{:S(2)}) collective-permute-start(f32[9,32,128]{2,1,0:T(8,128)S(1)} %get-tuple-element.25), channel_id=1, source_target_pairs={{0,1},{1,2},{2,3},{3,0},{4,5},{5,6},{6,7},{7,4},{8,9},{9,10},{10,1... | collective-permute-start | bytes 442376 | tf_op jit(solution)/shard_map/ppermute | solution.py:38
  56.1 0.1 reshape.38
  56.2 0.7 %reshape.39 = f32[1,1,1,4,1024]{4,3,2,1,0:T(4,128)} reshape(f32[4,32,32]{2,1,0:T(8,128)S(1)} %copy.11) | data formatting | bytes 32768 | tf_op jit(solution)/shard_map/reshape | solution.py:386
  56.9 0.9 %turned_tiles.1.refs_8_ = f32[45,32,128]{2,1,0:T(8,128)S(1)} custom-call(f32[10,32,128]{2,1,0:T(8,128)S(1)} %get-tuple-element.18.refs_0_, f32[10,32,128]{2,1,0:T(8,128)S(1)} %get-tuple-element.19.refs_1_, f32[10,32,128]{2,1,0:T(8,128)S(1)} %get-tuple-element.20.refs_2_, f32[5,32,128]{2,1,0:T(8,128)S(1)} %get-tuple-element.21.refs_3_, ...), custom_call_target="tpu_custom_call" | custom-call | flops 1048576 | bytes 2097152 | tf_op jit(solution)/shard_map/turned_tiles/pallas_call | solution.py:264
  57.8 5.9 %collective-permute-done.10.refs_6_ = f32[9,32,128]{2,1,0:T(8,128)S(1)} collective-permute-done((f32[9,32,128]{2,1,0:T(8,128)S(1)}, f32[9,32,128]{2,1,0:T(8,128)S(1)}, u32[]{:S(2)}, u32[]{:S(2)}) %collective-permute-start.10) | collective-permute-done | bytes 147488 | tf_op jit(solution)/shard_map/ppermute | solution.py:38
  63.7 0.0 collective-permute-done.11.refs_7_
  63.7 1.0 %pair_sums.1 = f32[4,45]{1,0:T(4,128)} custom-call(f32[10,32,128]{2,1,0:T(8,128)S(1)} %collective-permute-done.5.refs_0_, f32[10,32,128]{2,1,0:T(8,128)S(1)} %collective-permute-done.6.refs_1_, f32[10,32,128]{2,1,0:T(8,128)S(1)} %collective-permute-done.7.refs_2_, f32[5,32,128]{2,1,0:T(8,128)S(1)} %collective-permute-done.8.refs_3_, ...), custom_call_target="tpu_custom_call" | custom-call | tf_op jit(solution)/shard_map/pair_sums/pallas_call | solution.py:329
  (6 shorter events, 0.1 us)
Async XLA Ops:
  0.6 6.0 %copy-start = (f32[4,1024]{1,0:T(4,128)S(1)}, f32[4,1024]{1,0:T(4,128)}, u32[]{:S(2)}) copy-start(f32[4,1024]{1,0:T(4,128)} %param.9) | copy-start | bytes 49156
  0.6 0.7 %copy-start.2 = (f32[1,1,1,4,1024]{4,3,2,1,0:T(4,128)S(1)}, f32[1,1,1,4,1024]{4,3,2,1,0:T(4,128)}, u32[]{:S(2)}) copy-start(f32[1,1,1,4,1024]{4,3,2,1,0:T(4,128)} %param.5) | copy-start | bytes 49156
  1.5 7.0 %collective-permute-start.1 = (f32[32,128]{1,0:T(8,128)S(1)}, f32[32,128]{1,0:T(8,128)S(1)}, u32[]{:S(2)}, u32[]{:S(2)}) collective-permute-start(f32[32,128]{1,0:T(8,128)S(1)} %own_tile.1.own_ref), channel_id=1, source_target_pairs={{0,3},{1,0},{2,1},{3,2},{4,7},{5,4},{6,5},{7,6},{8,11},{9,8},{10,9... | collective-permute-start | bytes 49160 | tf_op jit(solution)/shard_map/ppermute | solution.py:38
  6.6 5.5 %collective-permute-start = (f32[32,128]{1,0:T(8,128)S(1)}, f32[32,128]{1,0:T(8,128)S(1)}, u32[]{:S(2)}, u32[]{:S(2)}) collective-permute-start(f32[32,128]{1,0:T(8,128)S(1)} %own_tile.1.own_ref), channel_id=1, source_target_pairs={{0,1},{1,2},{2,3},{3,0},{4,5},{5,6},{6,7},{7,4},{8,9},{9,10},{10,1... | collective-permute-start | bytes 49160 | tf_op jit(solution)/shard_map/ppermute | solution.py:38
  12.2 4.2 %collective-permute-start.2 = (f32[3,32,128]{2,1,0:T(8,128)S(1)}, f32[3,32,128]{2,1,0:T(8,128)S(1)}, u32[]{:S(2)}, u32[]{:S(2)}) collective-permute-start(f32[3,32,128]{2,1,0:T(8,128)S(1)} %get-tuple-element.28), channel_id=1, source_target_pairs={{0,16},{1,17},{2,18},{3,19},{4,20},{5,21},{6,22},{7,23},{8,24},{9,... | collective-permute-start | bytes 147464 | tf_op jit(solution)/shard_map/ppermute | solution.py:38
  16.3 9.6 %collective-permute-start.4 = (f32[2,3,32,128]{3,2,1,0:T(8,128)S(1)}, f32[2,3,32,128]{3,2,1,0:T(8,128)S(1)}, u32[]{:S(2)}, u32[]{:S(2)}) collective-permute-start(f32[2,3,32,128]{3,2,1,0:T(8,128)S(1)} %get-tuple-element.27), channel_id=1, source_target_pairs={{0,12},{1,13},{2,14},{3,15},{4,0},{5,1},{6,2},{7,3},{8,4},{9,5},{1... | collective-permute-start | bytes 294920 | tf_op jit(solution)/shard_map/ppermute | solution.py:38
  16.4 9.6 %collective-permute-start.3 = (f32[2,3,32,128]{3,2,1,0:T(8,128)S(1)}, f32[2,3,32,128]{3,2,1,0:T(8,128)S(1)}, u32[]{:S(2)}, u32[]{:S(2)}) collective-permute-start(f32[2,3,32,128]{3,2,1,0:T(8,128)S(1)} %get-tuple-element.27), channel_id=1, source_target_pairs={{0,4},{1,5},{2,6},{3,7},{4,8},{5,9},{6,10},{7,11},{8,12},{9,13},{1... | collective-permute-start | bytes 294920 | tf_op jit(solution)/shard_map/ppermute | solution.py:38
  17.4 3.5 %copy-start.1 = (f32[1,1440,1440]{2,1,0:T(8,128)S(1)}, f32[1,1440,1440]{2,1,0:T(8,128)}, u32[]{:S(2)}) copy-start(f32[1,1440,1440]{2,1,0:T(8,128)} %param.6) | copy-start | bytes 24883204
  40.6 11.0 %collective-permute-start.5 = (f32[10,32,128]{2,1,0:T(8,128)S(1)}, f32[10,32,128]{2,1,0:T(8,128)S(1)}, u32[]{:S(2)}, u32[]{:S(2)}) collective-permute-start(f32[10,32,128]{2,1,0:T(8,128)S(1)} %get-tuple-element.18.refs_0_), channel_id=1, source_target_pairs={{0,28},{1,29},{2,30},{3,31},{4,16},{5,17},{6,18},{7,19},{8,20},{9,... | collective-permute-start | bytes 491528 | tf_op jit(solution)/shard_map/ppermute | solution.py:38
  42.9 9.1 %collective-permute-start.6 = (f32[10,32,128]{2,1,0:T(8,128)S(1)}, f32[10,32,128]{2,1,0:T(8,128)S(1)}, u32[]{:S(2)}, u32[]{:S(2)}) collective-permute-start(f32[10,32,128]{2,1,0:T(8,128)S(1)} %get-tuple-element.19.refs_1_), channel_id=1, source_target_pairs={{0,16},{1,17},{2,18},{3,19},{4,20},{5,21},{6,22},{7,23},{8,24},{9,... | collective-permute-start | bytes 491528 | tf_op jit(solution)/shard_map/ppermute | solution.py:38
  43.4 10.4 %collective-permute-start.7 = (f32[10,32,128]{2,1,0:T(8,128)S(1)}, f32[10,32,128]{2,1,0:T(8,128)S(1)}, u32[]{:S(2)}, u32[]{:S(2)}) collective-permute-start(f32[10,32,128]{2,1,0:T(8,128)S(1)} %get-tuple-element.20.refs_2_), channel_id=1, source_target_pairs={{0,20},{1,21},{2,22},{3,23},{4,24},{5,25},{6,26},{7,27},{8,28},{9,... | collective-permute-start | bytes 491528 | tf_op jit(solution)/shard_map/ppermute | solution.py:38
  43.6 4.6 %collective-permute-start.8 = (f32[5,32,128]{2,1,0:T(8,128)S(1)}, f32[5,32,128]{2,1,0:T(8,128)S(1)}, u32[]{:S(2)}, u32[]{:S(2)}) collective-permute-start(f32[5,32,128]{2,1,0:T(8,128)S(1)} %get-tuple-element.21.refs_3_), channel_id=1, source_target_pairs={{0,12},{1,13},{2,14},{3,15},{4,0},{5,1},{6,2},{7,3},{8,4},{9,5},{1... | collective-permute-start | bytes 245768 | tf_op jit(solution)/shard_map/ppermute | solution.py:38
  46.1 5.5 %collective-permute-start.9 = (f32[5,32,128]{2,1,0:T(8,128)S(1)}, f32[5,32,128]{2,1,0:T(8,128)S(1)}, u32[]{:S(2)}, u32[]{:S(2)}) collective-permute-start(f32[5,32,128]{2,1,0:T(8,128)S(1)} %get-tuple-element.23.refs_5_), channel_id=1, source_target_pairs={{0,4},{1,5},{2,6},{3,7},{4,8},{5,9},{6,10},{7,11},{8,12},{9,13},{1... | collective-permute-start | bytes 245768 | tf_op jit(solution)/shard_map/ppermute | solution.py:38
  54.0 9.7 %collective-permute-start.10 = (f32[9,32,128]{2,1,0:T(8,128)S(1)}, f32[9,32,128]{2,1,0:T(8,128)S(1)}, u32[]{:S(2)}, u32[]{:S(2)}) collective-permute-start(f32[9,32,128]{2,1,0:T(8,128)S(1)} %get-tuple-element.24), channel_id=1, source_target_pairs={{0,3},{1,0},{2,1},{3,2},{4,7},{5,4},{6,5},{7,6},{8,11},{9,8},{10,9... | collective-permute-start | bytes 442376 | tf_op jit(solution)/shard_map/ppermute | solution.py:38
  54.2 9.5 %collective-permute-start.11 = (f32[9,32,128]{2,1,0:T(8,128)S(1)}, f32[9,32,128]{2,1,0:T(8,128)S(1)}, u32[]{:S(2)}, u32[]{:S(2)}) collective-permute-start(f32[9,32,128]{2,1,0:T(8,128)S(1)} %get-tuple-element.25), channel_id=1, source_target_pairs={{0,1},{1,2},{2,3},{3,0},{4,5},{5,6},{6,7},{7,4},{8,9},{9,10},{10,1... | collective-permute-start | bytes 442376 | tf_op jit(solution)/shard_map/ppermute | solution.py:38
where the time goes:
time: 64.9 us; the launch traced here: 64.6 us
  Pallas kernels  21.7 us (33%)
  waiting for transfers between devices  19.8 us (31%)
  starting transfers between devices  14.8 us (23%)
  local copies, waits for them, and re-layouts  6.38 us (10%)
  matrix products  0.85 us (1%)
  between operations  0.79 us (1%)
    ppermute x12, waiting for transfers between devices, shifted(): return lax.ppermute(x, MESH_AXES, pairs)  19.8 us
    ppermute x12, starting transfers between devices, shifted(): return lax.ppermute(x, MESH_AXES, pairs)  14.8 us
    pallas_call x1, Pallas kernels, sweeps(): pl.pallas_call(functools.partial(sweep_kernel, groups), out_shape=tuple(o...  14.6 us
    pallas_call x1, Pallas kernels, split_structure(): pl.pallas_call(split_kernel, out_shape=(jax.ShapeDtypeStruct((ROWS, ROWS)...  5.03 us
    unnamed x6, local copies, waits for them, and re-layouts  4.23 us
  transfers between devices with their start and end apart: 12, of which 7 were waited for; matrix products, arithmetic and copies ran while one was open for 5% of the time, Pallas kernels for 9%

commit v1 on v0

--- a/solution.py
+++ b/solution.py
@@ -42,6 +42,10 @@
     return [pl.BlockSpec(memory_space=pltpu.VMEM)] * count
 
 
+def in_hbm(x):
+    return pltpu.with_memory_space_constraint(x, pltpu.HBM)
+
+
 def halves(x):
     high = x.astype(bf16)
     return high, (x - high.astype(f32)).astype(bf16)
@@ -65,6 +69,24 @@
             tile_ref[a : a + 1, :] = jnp.sum(picked, axis=0, keepdims=True)
 
 
+def flat_kernel(tile_ref, flat_ref):
+    row = lax.broadcasted_iota(jnp.int32, (DEPTH, LANES), 0)
+    diagonal = lane_index((DEPTH, LANES)) // L2 == row
+    for j in range(L2 // DEPTH):
+        spread = []
+        for k in range(DEPTH):
+            a = j * DEPTH + k
+            line = jnp.broadcast_to(tile_ref[a : a + 1, :], (DEPTH, LANES))
+            spread.append(jnp.where(diagonal, line, 0.0))
+        value = jnp.zeros((DEPTH, LANES), f32)
+        for m in range(DEPTH):
+            picked = jnp.zeros((DEPTH, LANES), f32)
+            for k in range(DEPTH):
+                picked = jnp.where(row == (k - m) % DEPTH, spread[k], picked)
+            value = value + (picked if m == 0 else pltpu.roll(picked, m * L2, 1))
+        flat_ref[:, j * LANES : (j + 1) * LANES] = value
+
+
 def own_tile(flat):
     return pl.pallas_call(
         tile_kernel,
@@ -76,52 +98,120 @@
     )(flat)
 
 
-def split_kernel(structure_ref, own_ref, high_ref, low_ref, image_ref, buffer, sems):
+def split_kernel(
+    structure_hbm,
+    own_ref,
+    species_hbm,
+    members_hbm,
+    table_hbm,
+    high_ref,
+    low_ref,
+    image_ref,
+    member_ref,
+    delta_ref,
+    buffer,
+    species_ref,
+    members_ref,
+    table_ref,
+    table_tile,
+    sems,
+    small_sems,
+):
     def fetch(step):
         return pltpu.make_async_copy(
-            structure_ref.at[pl.ds(step * CHUNK, CHUNK), :],
-            buffer.at[step % 2],
-            sems.at[step % 2],
+            structure_hbm.at[pl.ds(step * CHUNK, CHUNK), :], buffer.at[step], sems.at[step]
         )
 
-    fetch(0).start()
+    small = [
+        pltpu.make_async_copy(source, target, small_sems.at[i])
+        for i, (source, target) in enumerate(
+            [
+                (species_hbm, species_ref),
+                (members_hbm, members_ref),
+                (table_hbm, table_ref),
+            ]
+        )
+    ]
+    for step in range(CHUNKS):
+        fetch(step).start()
+    for copy in small:
+        copy.start()
     own_high, own_low = halves(own_ref[...])
+    for copy in small:
+        copy.wait()
+    split_small(species_ref, members_ref, table_ref, table_tile, member_ref, delta_ref)
+
     for step in range(CHUNKS):
-        if step + 1 < CHUNKS:
-            fetch(step + 1).start()
         fetch(step).wait()
-        rows = pl.ds(step * CHUNK, CHUNK)
-        for q in range(GROUP):
-            part = pl.ds(q * L2, L2)
-            high, low = halves(buffer[step % 2, part, :])
-            high_ref[pl.ds(step * CHUNK + q * L2, L2), :] = high
-            low_ref[pl.ds(step * CHUNK + q * L2, L2), :] = low
-        columns = pl.ds(CENTRE * L2, L2)
-        centre_high, centre_low = halves(buffer[step % 2, :, columns])
-        image_ref[rows, :] = (
-            jnp.dot(centre_high, own_high, preferred_element_type=f32)
-            + jnp.dot(centre_high, own_low, preferred_element_type=f32)
-            + jnp.dot(centre_low, own_high, preferred_element_type=f32)
-        )
-
-
-def split_structure(structure, own):
+
+        def cell_step(q, carry, step=step):
+            source = pl.ds(pl.multiple_of(q * L2, L2), L2)
+            rows = pl.ds(pl.multiple_of(step * CHUNK + q * L2, L2), L2)
+            high, low = halves(buffer[step, source, :])
+            high_ref[rows, :] = high
+            low_ref[rows, :] = low
+            columns = slice(CENTRE * L2, CENTRE * L2 + L2)
+            image_ref[rows, :] = (
+                jnp.dot(high[:, columns], own_high, preferred_element_type=f32)
+                + jnp.dot(high[:, columns], own_low, preferred_element_type=f32)
+                + jnp.dot(low[:, columns], own_high, preferred_element_type=f32)
+            )
+            return carry
+
+        lax.fori_loop(0, GROUP, cell_step, 0, unroll=3)
+
+
+def split_small(species_ref, members_ref, table_ref, table_tile, member_ref, delta_ref):
+    tile_kernel(table_ref, table_tile)
+    table = table_tile[...]
+    moved = [table] + [pltpu.roll(table, m * L2, 1) for m in range(1, SPECIES)]
+    group = lane_index((L2, LANES)) // L2
+    delta = jnp.zeros((L2, LANES), f32)
+    for s in range(DEPTH):
+        for kind in range(SPECIES):
+            here = (group == s) & (species_ref[0, s] == kind)
+            delta = jnp.where(here, moved[(s - kind) % SPECIES], delta)
+    delta_ref[...] = delta
+
+    cells = lax.broadcasted_iota(jnp.int32, (WINDOW, WINDOW), 0)
+    group = lane_index((WINDOW, LANES)) // L2
+    member = jnp.zeros((WINDOW, LANES), f32)
+    for s in range(DEPTH):
+        found = (members_ref[s : s + 1, :] == cells).astype(f32)
+        found = jnp.max(found, axis=1, keepdims=True)
+        member = jnp.where(group == s, found, member)
+    member_ref[...] = member
+
+
+def split_structure(structure, own, species, members, table):
+    specs = [pl.BlockSpec(memory_space=pltpu.HBM)] * 5
+    specs[1] = in_vmem(1)[0]
     return pl.pallas_call(
         split_kernel,
         out_shape=(
             jax.ShapeDtypeStruct((ROWS, ROWS), bf16),
             jax.ShapeDtypeStruct((ROWS, ROWS), bf16),
             jax.ShapeDtypeStruct((ROWS, LANES), f32),
+            jax.ShapeDtypeStruct((WINDOW, LANES), f32),
+            jax.ShapeDtypeStruct((L2, LANES), f32),
         ),
-        in_specs=[pl.BlockSpec(memory_space=pl.ANY)] + in_vmem(1),
-        out_specs=tuple(in_vmem(3)),
-        scratch_shapes=[pltpu.VMEM((2, CHUNK, ROWS), f32), pltpu.SemaphoreType.DMA((2,))],
-        compiler_params=pltpu.CompilerParams(vmem_limit_bytes=24 * MIB),
+        in_specs=specs,
+        out_specs=tuple(in_vmem(5)),
+        scratch_shapes=[
+            pltpu.VMEM((CHUNKS, CHUNK, ROWS), f32),
+            pltpu.SMEM((1, DEPTH), jnp.int32),
+            pltpu.VMEM((DEPTH, WINDOW), jnp.int32),
+            pltpu.VMEM((SPECIES, L2 * L2), f32),
+            pltpu.VMEM((L2, LANES), f32),
+            pltpu.SemaphoreType.DMA((CHUNKS,)),
+            pltpu.SemaphoreType.DMA((3,)),
+        ],
+        compiler_params=pltpu.CompilerParams(vmem_limit_bytes=16 * MIB),
         cost_estimate=pl.CostEstimate(
             flops=2 * 3 * ROWS * L2 * LANES, bytes_accessed=4 * ROWS * ROWS, transcendentals=0
         ),
         name="split_structure",
-    )(structure, own)
+    )(in_hbm(structure), own, in_hbm(species), in_hbm(members), in_hbm(table))
 
 
 def window_tile(near_ref, cell):
@@ -146,10 +236,11 @@
     lane = lane_index((L2, LANES))
     masks = [(lane // L2 == s).astype(f32).astype(bf16) for s in range(DEPTH)]
 
+    def site_blocks(tile):
+        return jnp.concatenate([tile * mask for mask in masks], axis=0)
+
     def apply(cell, image):
-        high, low = halves(image)
-        high_blocks = jnp.concatenate([high * mask for mask in masks], axis=0)
-        low_blocks = jnp.concatenate([low * mask for mask in masks], axis=0)
+        high_blocks, low_blocks = (site_blocks(part) for part in halves(image))
         both = jnp.concatenate([high_blocks, low_blocks], axis=1)
         rows = pl.ds(cell * L2, L2)
         first = jnp.dot(window[rows, :LANES], both, preferred_element_type=f32)
@@ -196,7 +287,7 @@
         lax.fori_loop(0, CHUNKS, chunk_step, 0)
 
     final = (ITERS - 1) % 2
-    high, low = halves(delta_ref[...])
+    high, low = (site_blocks(part) for part in halves(delta_ref[...]))
     delta = jnp.concatenate(
         [
             jnp.concatenate([high, low], axis=1),
@@ -239,8 +330,17 @@
     raise ValueError("no tile")
 
 
+def plane_offsets():
+    return [(ox, oy) for ox in (-1, 0, 1) for oy in (-1, 0, 1)]
+
+
+def cell_of(dx, dy, dz):
+    return ((dx + 1) * 3 + dy + 1) * 5 + dz + 2
+
+
 def turn_kernel(groups, *refs):
-    own, out = refs[:-1], refs[-1]
+    own = refs[: len(groups)]
+    out, up_ref, down_ref = refs[len(groups) :]
     lane = lane_index((L2, LANES))
 
     def cell_tile(cell):
@@ -258,65 +358,105 @@
                 piece = pieces[s] if move == 0 else pltpu.roll(pieces[s], move * L2, 1)
                 value = jnp.where(lane // L2 == s, piece, value)
             out[base + k] = value
+    for place, (dx, dy) in enumerate(plane_offsets()):
+        far = pltpu.roll(out[cell_of(dx, dy, 2)], 2 * L2, 1)
+        up_ref[place] = jnp.where(lane < 2 * L2, far, out[cell_of(dx, dy, 1)])
+        far = pltpu.roll(out[cell_of(dx, dy, -2)], 2 * L2, 1)
+        down_ref[place] = jnp.where(lane >= 2 * L2, far, out[cell_of(dx, dy, -1)])
 
 
 def turned_tiles(groups, own):
+    edge = jax.ShapeDtypeStruct((9, L2, LANES), f32)
     return pl.pallas_call(
         functools.partial(turn_kernel, groups),
-        out_shape=jax.ShapeDtypeStruct((WINDOW, L2, LANES), f32),
+        out_shape=(jax.ShapeDtypeStruct((WINDOW, L2, LANES), f32), edge, edge),
         in_specs=in_vmem(len(own)),
-        out_specs=in_vmem(1)[0],
+        out_specs=tuple(in_vmem(3)),
         compiler_params=pltpu.CompilerParams(vmem_limit_bytes=8 * MIB),
         cost_estimate=pl.CostEstimate(flops=MIB, bytes_accessed=2 * MIB, transcendentals=0),
         name="turned_tiles",
     )(*own)
 
 
-def plane_offsets():
-    return [(ox, oy) for ox in (-1, 0, 1) for oy in (-1, 0, 1)]
-
-
-def pack_kernel(groups, *refs):
-    got = refs[:-2]
-    down_ref, up_ref = refs[-2:]
+def edge_kernel(groups, *refs):
+    got = refs[: len(groups)]
+    from_below, from_above, to_below, to_above = refs[len(groups) :]
     lane = lane_index((L2, LANES))
-    for place, (ox, oy) in enumerate(plane_offsets()):
-        far = pltpu.roll(find_tile(groups, got, ox, oy, -2), 2 * L2, 1)
-        down_ref[place] = jnp.where(lane >= 2 * L2, far, find_tile(groups, got, ox, oy, -1))
-        far = pltpu.roll(find_tile(groups, got, ox, oy, 2), 2 * L2, 1)
-        up_ref[place] = jnp.where(lane < 2 * L2, far, find_tile(groups, got, ox, oy, 1))
-
-
-def packed_edges(groups, got):
-    shape = jax.ShapeDtypeStruct((9, L2, LANES), f32)
-    return pl.pallas_call(
-        functools.partial(pack_kernel, groups),
+    for ref in (to_below, to_above):
+        ref[...] = jnp.zeros_like(ref)
+    for place, (dx, dy) in enumerate(plane_offsets()):
+        far = find_tile(groups, got, -dx, -dy, -2)
+        close = pltpu.roll(find_tile(groups, got, -dx, -dy, -1), 3 * L2, 1)
+        value = jnp.where(lane < 2 * L2, far, close) * from_below[place]
+        to_below[place : place + 1, :] = jnp.sum(value, axis=0, keepdims=True)
+        far = find_tile(groups, got, -dx, -dy, 2)
+        close = pltpu.roll(find_tile(groups, got, -dx, -dy, 1), L2, 1)
+        value = jnp.where(lane >= 2 * L2, far, close) * from_above[place]
+        to_above[place : place + 1, :] = jnp.sum(value, axis=0, keepdims=True)
+
+
+def edge_sums(groups, got, from_below, from_above):
+    shape = jax.ShapeDtypeStruct((16, LANES), f32)
+    return pl.pallas_call(
+        functools.partial(edge_kernel, groups),
         out_shape=(shape, shape),
-        in_specs=in_vmem(len(got)),
+        in_specs=in_vmem(len(got) + 2),
         out_specs=tuple(in_vmem(2)),
         compiler_params=pltpu.CompilerParams(vmem_limit_bytes=8 * MIB),
-        name="packed_edges",
-    )(*got)
-
-
-def pair_kernel(groups, *refs):
+        name="edge_sums",
+    )(*got, from_below, from_above)
+
+
+def slab_kernel(groups, *refs):
     got = refs[: len(groups)]
-    above_ref, below_ref, turned_ref, out_ref, sums = refs[len(groups) :]
-    lane = lane_index((L2, LANES))
-    for place, (ox, oy) in enumerate(plane_offsets()):
-        above, below = above_ref[place], below_ref[place]
+    turned_ref, tau_ref, sums, flat_ref = refs[len(groups) :]
+    flat_kernel(tau_ref, flat_ref)
+    lane = lane_index((1, LANES))
+    for dx, dy in plane_offsets():
         for dz in range(-2, 3):
-            tile = find_tile(groups, got, ox, oy, -dz)
-            if dz == 1:
-                tile = pltpu.roll(jnp.where(lane >= L2, tile, above), 3 * L2, 1)
-            elif dz == 2:
-                tile = jnp.where(lane < 2 * L2, pltpu.roll(tile, 2 * L2, 1), above)
-            elif dz == -1:
-                tile = pltpu.roll(jnp.where(lane < 3 * L2, tile, below), L2, 1)
-            elif dz == -2:
-                tile = jnp.where(lane >= 2 * L2, pltpu.roll(tile, 2 * L2, 1), below)
-            cell = ((1 - ox) * 3 + 1 - oy) * 5 + dz + 2
-            sums[cell : cell + 1, :] = jnp.sum(tile * turned_ref[cell], axis=0, keepdims=True)
+            cell = cell_of(dx, dy, dz)
+            tile = find_tile(groups, got, -dx, -dy, -dz)
+            if dz != 0:
+                tile = pltpu.roll(tile, -dz % DEPTH * L2, 1)
+            row = jnp.sum(tile * turned_ref[cell], axis=0, keepdims=True)
+            if dz > 0:
+                row = jnp.where(lane < (DEPTH - dz) * L2, row, 0.0)
+            elif dz < 0:
+                row = jnp.where(lane >= -dz * L2, row, 0.0)
+            sums[cell : cell + 1, :] = row
+
+
+def slab_sums(groups, got, turned, tau):
+    return pl.pallas_call(
+        functools.partial(slab_kernel, groups),
+        out_shape=(
+            jax.ShapeDtypeStruct((WINDOW, LANES), f32),
+            jax.ShapeDtypeStruct((DEPTH, L2 * L2), f32),
+        ),
+        in_specs=in_vmem(len(got) + 2),
+        out_specs=tuple(in_vmem(2)),
+        compiler_params=pltpu.CompilerParams(vmem_limit_bytes=8 * MIB),
+        cost_estimate=pl.CostEstimate(flops=MIB, bytes_accessed=2 * MIB, transcendentals=0),
+        name="slab_sums",
+    )(*got, turned, tau)
+
+
+def total_kernel(slab_ref, above_ref, below_ref, out_ref, sums):
+    lane = lane_index((1, LANES))
+    sums[...] = jnp.zeros_like(sums)
+    sums[:WINDOW, :] = slab_ref[...]
+    for place, (dx, dy) in enumerate(plane_offsets()):
+        above = above_ref[place : place + 1, :]
+        below = below_ref[place : place + 1, :]
+        edges = {
+            1: jnp.where(lane >= 3 * L2, above, 0.0),
+            2: jnp.where(lane >= 2 * L2, pltpu.roll(above, 2 * L2, 1), 0.0),
+            -1: jnp.where(lane < L2, below, 0.0),
+            -2: jnp.where(lane < 2 * L2, pltpu.roll(below, 2 * L2, 1), 0.0),
+        }
+        for dz, row in edges.items():
+            cell = cell_of(dx, dy, dz)
+            sums[cell : cell + 1, :] = sums[cell : cell + 1, :] + row
     site = lax.broadcasted_iota(jnp.int32, (8, LANES), 0)
     pick = (lane_index((8, LANES)) // L2 == site).astype(f32)
     total = lax.dot_general(
@@ -325,16 +465,16 @@
     out_ref[...] = total[:DEPTH, :WINDOW]
 
 
-def pair_sums(groups, got, above, below, turned):
-    return pl.pallas_call(
-        functools.partial(pair_kernel, groups),
+def total_sums(slab, above, below):
+    return pl.pallas_call(
+        total_kernel,
         out_shape=jax.ShapeDtypeStruct((DEPTH, WINDOW), f32),
-        in_specs=in_vmem(len(got) + 3),
+        in_specs=in_vmem(3),
         out_specs=in_vmem(1)[0],
         scratch_shapes=[pltpu.VMEM((48, LANES), f32)],
-        compiler_params=pltpu.CompilerParams(vmem_limit_bytes=8 * MIB),
-        name="pair_sums",
-    )(*got, above, below, turned)
+        compiler_params=pltpu.CompilerParams(vmem_limit_bytes=4 * MIB),
+        name="total_sums",
+    )(slab, above, below)
 
 
 def plane_groups():
@@ -345,30 +485,30 @@
     return groups
 
 
-def near_tiles(own):
+def near_tiles(own, ready):
     column = jnp.stack([own, shifted(own, (0, 0, 1)), shifted(own, (0, 0, -1))])
+    column, *ready = lax.optimization_barrier((column, *ready))
     if lax.axis_size("gx") == 2:
         sides = [shifted(column, (1, 0, 0)), column]
     else:
         sides = [shifted(column, (1, 0, 0)), column, shifted(column, (-1, 0, 0))]
     plane = jnp.stack(sides)
     planes = [shifted(plane, (0, 1, 0)), plane, shifted(plane, (0, -1, 0))]
-    return jnp.stack(planes)
+    return jnp.stack(planes), ready
 
 
 def body(t_matrix, structure, species, members, delta_table):
     own = own_tile(t_matrix.reshape(DEPTH, L2 * L2))
-    near = near_tiles(own)
-    high, low, image = split_structure(structure[0], own)
-
-    window_cells = jnp.arange(WINDOW, dtype=jnp.int32)
-    member = jnp.any(members[0, 0][..., None] == window_cells, axis=-2).astype(f32).T
-    member = jnp.repeat(member, L2, axis=1)
-    onehot = (species.reshape(DEPTH, 1) == jnp.arange(SPECIES, dtype=jnp.int32)).astype(f32)
-    delta = jnp.dot(onehot, delta_table, precision=highest, preferred_element_type=f32)
-    delta = delta.reshape(DEPTH, L2, 1, L2) * jnp.eye(DEPTH, dtype=f32)[:, None, :, None]
-    delta = delta.reshape(LANES, LANES)
-
+    near, (high, low, image, member, delta) = near_tiles(
+        own,
+        split_structure(
+            structure[0],
+            own,
+            species.reshape(1, DEPTH),
+            members.reshape(DEPTH, WINDOW),
+            delta_table,
+        ),
+    )
     table = plane_groups()
     shifts, groups = list(table), list(table.values())
     *sent, tau = sweeps(groups, high, low, image, near, member, own, delta)
@@ -376,12 +516,14 @@
         block if shift == (0, 0) else shifted(block, shift + (0,))
         for shift, block in zip(shifts, sent)
     ]
-    turned = turned_tiles(groups, sent)
-    down, up = packed_edges(groups, got)
-    above = shifted(down, (0, 0, -1))
-    below = shifted(up, (0, 0, 1))
-    pairs = pair_sums(groups, got, above, below, turned)
-    site_tau = jnp.transpose(tau.reshape(L2, DEPTH, L2), (1, 0, 2))
+    turned, up, down = turned_tiles(groups, sent)
+    from_below = shifted(up, (0, 0, 1))
+    from_above = shifted(down, (0, 0, -1))
+    to_below, to_above = edge_sums(groups, got, from_below, from_above)
+    above = shifted(to_below, (0, 0, -1))
+    below = shifted(to_above, (0, 0, 1))
+    slab, site_tau = slab_sums(groups, got, turned, tau)
+    pairs = total_sums(slab, above, below)
     return (
         site_tau.reshape(1, 1, 1, DEPTH, L2 * L2),
         pairs.reshape(1, 1, DEPTH, WINDOW),

time: 64.9 us -> 62.4 us (0.961)
  local copies, waits for them, and re-layouts: 6.38 us -> 0.71 us
  Pallas kernels: 21.7 us -> 25.4 us
  starting transfers between devices: 14.8 us -> 18.5 us
  waiting for transfers between devices: 19.8 us -> 16.7 us
  matrix products: 0.85 us -> 0 us
    ppermute x12 -> x14, starting transfers between devices: 14.8 us -> 18.5 us  [shifted(): return lax.ppermute(x, MESH_AXES, pairs)]
    unnamed x6 -> x2, local copies, waits for them, and re-layouts: 4.23 us -> 0.71 us
    ppermute x12 -> x14, waiting for transfers between devices: 19.8 us -> 16.7 us  [shifted(): return lax.ppermute(x, MESH_AXES, pairs)]
    pallas_call x1, Pallas kernels: 5.03 us -> 8.05 us  [split_structure(): pl.pallas_call(split_kernel, out_shape=(jax.ShapeDtypeStruct((ROWS, ROWS)...]
    reshape x3 -> x0, local copies, waits for them, and re-layouts: 0.9 us -> none  [the longest x1 0.7 us: body(): site_tau.reshape(1, 1, 1, DEPTH, L2 * L2)]
    dot_general x1 -> x0, matrix products: 0.85 us -> none  [body(): jnp.dot(onehot, delta_table, precision=highest, preferred_element_type=f32)]
    eq x1 -> x0, local copies, waits for them, and re-layouts: 0.78 us -> none  [body(): members[0, 0][..., None] == window_cells]
    pallas_call x3 -> x4, Pallas kernels: 1.97 us -> 2.63 us  [the longest x1 0.95 us: turned_tiles(): pl.pallas_call(functools.partial(turn_kernel, groups), out_shape=(jax.Sha...]
  transfers between devices with their start and end apart: 12 -> 14, of which waited for: 7 -> 9; matrix products, arithmetic and copies ran while one was open for 5% -> 0% of each run, Pallas kernels for 9% -> 16%
where the time goes in v1:
time: 62.4 us; the launch traced here: 62.1 us
  Pallas kernels  25.4 us (41%)
  starting transfers between devices  18.5 us (30%)
  waiting for transfers between devices  16.7 us (27%)
  between operations  0.75 us (1%)
  local copies, waits for them, and re-layouts  0.71 us (1%)
    ppermute x14, starting transfers between devices, shifted(): return lax.ppermute(x, MESH_AXES, pairs)  18.5 us
    ppermute x14, waiting for transfers between devices, shifted(): return lax.ppermute(x, MESH_AXES, pairs)  16.7 us
    pallas_call x1, Pallas kernels, sweeps(): pl.pallas_call(functools.partial(sweep_kernel, groups), out_shape=tuple(o...  14.6 us
    pallas_call x1, Pallas kernels, split_structure(): pl.pallas_call(split_kernel, out_shape=(jax.ShapeDtypeStruct((ROWS, ROWS)...  8.05 us
  transfers between devices with their start and end apart: 14, of which 9 were waited for; matrix products, arithmetic and copies ran while one was open for 0% of the time, Pallas kernels for 16%

profile of v1, /device:TPU:0, one launch (start us, length us, event | category | flops | bytes accessed | tf_op | source)
XLA Modules:
  0.0 62.1 jit_solution(1825662001177728227)
XLA Ops:
  0.6 0.0 copy-start
  0.6 0.7 %copy-done = f32[1,1,1,4,1024]{4,3,2,1,0:T(4,128)S(1)} copy-done((f32[1,1,1,4,1024]{4,3,2,1,0:T(4,128)S(1)}, f32[1,1,1,4,1024]{4,3,2,1,0:T(4,128)}, u32[]{:S(2)}) %copy-start) | copy-done | bytes 16408
  1.3 0.1 own_tile.1.own_ref
  1.5 5.1 %collective-permute-start.1 = (f32[32,128]{1,0:T(8,128)S(1)}, f32[32,128]{1,0:T(8,128)S(1)}, u32[]{:S(2)}, u32[]{:S(2)}) collective-permute-start(f32[32,128]{1,0:T(8,128)S(1)} %own_tile.1.own_ref), channel_id=1, source_target_pairs={{0,3},{1,0},{2,1},{3,2},{4,7},{5,4},{6,5},{7,6},{8,11},{9,8},{10,9... | collective-permute-start | bytes 49160 | tf_op jit(solution)/shard_map/ppermute | solution.py:38
  6.6 0.0 collective-permute-start
  6.6 8.0 %split_structure.1 = (bf16[1440,1440]{1,0:T(8,128)(2,1)S(1)}, bf16[1440,1440]{1,0:T(8,128)(2,1)S(1)}, f32[1440,128]{1,0:T(8,128)S(1)}, f32[45,128]{1,0:T(8,128)S(1)}, f32[32,128]{1,0:T(8,128)S(1)}) custom-call(f32[1440,1440]{1,0:T(8,128)} %bitcast.17, f32[32,128]{1,0:T(8,128)S(1)} %own_tile.1.own_ref, s32[1,4]{1,0:T(1,128)} %bitcast.26, s32[4,45]{1,0:T(4,128)} %bitcast.24, ...), custom_call_target="tpu_custom_call" | custom-call | flops 35389440 | bytes 8294400 | tf_op jit(solution)/shard_map/split_structure/pallas_call | solution.py:189
  14.7 0.0 collective-permute-done.1
  14.7 0.0 collective-permute-done
  14.7 1.6 %collective-permute-start.2 = (f32[3,32,128]{2,1,0:T(8,128)S(1)}, f32[3,32,128]{2,1,0:T(8,128)S(1)}, u32[]{:S(2)}, u32[]{:S(2)}) collective-permute-start(f32[3,32,128]{2,1,0:T(8,128)S(1)} %pad_maximum_fusion.2), channel_id=1, source_target_pairs={{0,16},{1,17},{2,18},{3,19},{4,20},{5,21},{6,22},{7,23},{8,24},{9,... | collective-permute-start | bytes 147464 | tf_op jit(solution)/shard_map/ppermute | solution.py:38
  16.3 2.6 %collective-permute-done.2 = f32[3,32,128]{2,1,0:T(8,128)S(1)} collective-permute-done((f32[3,32,128]{2,1,0:T(8,128)S(1)}, f32[3,32,128]{2,1,0:T(8,128)S(1)}, u32[]{:S(2)}, u32[]{:S(2)}) %collective-permute-start.2) | collective-permute-done | bytes 49184 | tf_op jit(solution)/shard_map/ppermute | solution.py:38
  18.9 0.1 collective-permute-start.4
  18.9 0.5 collective-permute-start.3
  19.4 1.7 %collective-permute-done.4 = f32[2,3,32,128]{3,2,1,0:T(8,128)S(1)} collective-permute-done((f32[2,3,32,128]{3,2,1,0:T(8,128)S(1)}, f32[2,3,32,128]{3,2,1,0:T(8,128)S(1)}, u32[]{:S(2)}, u32[]{:S(2)}) %collective-permute-start.4) | collective-permute-done | bytes 98336 | tf_op jit(solution)/shard_map/ppermute | solution.py:38
  21.1 2.9 %collective-permute-done.3 = f32[2,3,32,128]{3,2,1,0:T(8,128)S(1)} collective-permute-done((f32[2,3,32,128]{3,2,1,0:T(8,128)S(1)}, f32[2,3,32,128]{3,2,1,0:T(8,128)S(1)}, u32[]{:S(2)}, u32[]{:S(2)}) %collective-permute-start.3) | collective-permute-done | bytes 98336 | tf_op jit(solution)/shard_map/ppermute | solution.py:38
  24.1 14.6 %sweeps.1 = (f32[10,32,128]{2,1,0:T(8,128)S(1)}, f32[10,32,128]{2,1,0:T(8,128)S(1)}, f32[10,32,128]{2,1,0:T(8,128)S(1)}, f32[5,32,128]{2,1,0:T(8,128)S(1)}, f32[...) custom-call(bf16[1440,1440]{1,0:T(8,128)(2,1)S(1)} %get-tuple-element.32.high_ref, ...), custom_call_target="tpu_custom_call" | custom-call | flops 4777574400 | bytes 10485760 | tf_op jit(solution)/shard_map/sweeps/pallas_call | solution.py:311
  38.7 0.1 collective-permute-start.8
  38.8 0.5 collective-permute-start.9
  39.3 2.2 %collective-permute-start.5 = (f32[10,32,128]{2,1,0:T(8,128)S(1)}, f32[10,32,128]{2,1,0:T(8,128)S(1)}, u32[]{:S(2)}, u32[]{:S(2)}) collective-permute-start(f32[10,32,128]{2,1,0:T(8,128)S(1)} %get-tuple-element.38.refs_0_), channel_id=1, source_target_pairs={{0,28},{1,29},{2,30},{3,31},{4,16},{5,17},{6,18},{7,19},{8,20},{9,... | collective-permute-start | bytes 491528 | tf_op jit(solution)/shard_map/ppermute | solution.py:38
  41.5 0.5 collective-permute-start.6
  42.0 0.2 collective-permute-start.7
  42.2 0.9 %turned_tiles.1 = (f32[45,32,128]{2,1,0:T(8,128)S(1)}, f32[9,32,128]{2,1,0:T(8,128)S(1)}, f32[9,32,128]{2,1,0:T(8,128)S(1)}) custom-call(f32[10,32,128]{2,1,0:T(8,128)S(1)} %get-tuple-element.38.refs_0_, f32[10,32,128]{2,1,0:T(8,128)S(1)} %get-tuple-element.39.refs_1_, f32[10,32,128]{2,1,0:T(8,128)S(1)} %get-tuple-element.40.refs_2_, ...), custom_call_target="tpu_custom_call" | custom-call | flops 1048576 | bytes 2097152 | tf_op jit(solution)/shard_map/turned_tiles/pallas_call | solution.py:370
  43.2 0.0 collective-permute-done.8.refs_3_
  43.2 0.1 collective-permute-start.10
  43.3 0.1 collective-permute-done.9.refs_5_
  43.3 3.8 %collective-permute-start.11 = (f32[9,32,128]{2,1,0:T(8,128)S(1)}, f32[9,32,128]{2,1,0:T(8,128)S(1)}, u32[]{:S(2)}, u32[]{:S(2)}) collective-permute-start(f32[9,32,128]{2,1,0:T(8,128)S(1)} %get-tuple-element.49), channel_id=1, source_target_pairs={{0,3},{1,0},{2,1},{3,2},{4,7},{5,4},{6,5},{7,6},{8,11},{9,8},{10,9... | collective-permute-start | bytes 442376 | tf_op jit(solution)/shard_map/ppermute | solution.py:38
  47.2 3.1 %collective-permute-done.10.refs_6_ = f32[9,32,128]{2,1,0:T(8,128)S(1)} collective-permute-done((f32[9,32,128]{2,1,0:T(8,128)S(1)}, f32[9,32,128]{2,1,0:T(8,128)S(1)}, u32[]{:S(2)}, u32[]{:S(2)}) %collective-permute-start.10) | collective-permute-done | bytes 147488 | tf_op jit(solution)/shard_map/ppermute | solution.py:38
  50.3 0.0 collective-permute-done.11.refs_7_
  50.3 0.0 collective-permute-done.5.refs_0_
  50.3 0.3 collective-permute-done.6.refs_1_
  50.6 1.2 %collective-permute-done.7.refs_2_ = f32[10,32,128]{2,1,0:T(8,128)S(1)} collective-permute-done((f32[10,32,128]{2,1,0:T(8,128)S(1)}, f32[10,32,128]{2,1,0:T(8,128)S(1)}, u32[]{:S(2)}, u32[]{:S(2)}) %collective-permute-start.7) | collective-permute-done | bytes 163872 | tf_op jit(solution)/shard_map/ppermute | solution.py:38
  51.8 0.2 edge_sums.1
  52.0 3.9 %collective-permute-start.12 = (f32[16,128]{1,0:T(8,128)S(1)}, f32[16,128]{1,0:T(8,128)S(1)}, u32[]{:S(2)}, u32[]{:S(2)}) collective-permute-start(f32[16,128]{1,0:T(8,128)S(1)} %get-tuple-element.50), channel_id=1, source_target_pairs={{0,3},{1,0},{2,1},{3,2},{4,7},{5,4},{6,5},{7,6},{8,11},{9,8},{10,9... | collective-permute-start | bytes 24584 | tf_op jit(solution)/shard_map/ppermute | solution.py:38
  55.8 0.0 collective-permute-start.13
  55.8 0.7 %slab_sums.1 = (f32[45,128]{1,0:T(8,128)S(1)}, f32[4,1024]{1,0:T(4,128)}) custom-call(f32[10,32,128]{2,1,0:T(8,128)S(1)} %collective-permute-done.5.refs_0_, f32[10,32,128]{2,1,0:T(8,128)S(1)} %collective-permute-done.6.refs_1_, f32[10,32,128]{2,1,0:T(8,128)S(1)} %collective-permute-done.7.refs_2_, f32[5,32,128]{2,1,0:T(8,128)S(1)} %collective-permute-done.8.refs_3_, ...), custom_call_target="tpu_custom_call" | custom-call | flops 1048576 | bytes 2097152 | tf_op jit(solution)/shard_map/slab_sums/pallas_call | solution.py:430
  56.5 0.7 %collective-permute-done.12.above_ref = f32[16,128]{1,0:T(8,128)S(1)} collective-permute-done((f32[16,128]{1,0:T(8,128)S(1)}, f32[16,128]{1,0:T(8,128)S(1)}, u32[]{:S(2)}, u32[]{:S(2)}) %collective-permute-start.12) | collective-permute-done | bytes 8224 | tf_op jit(solution)/shard_map/ppermute | solution.py:38
  57.2 4.1 %collective-permute-done.13.below_ref = f32[16,128]{1,0:T(8,128)S(1)} collective-permute-done((f32[16,128]{1,0:T(8,128)S(1)}, f32[16,128]{1,0:T(8,128)S(1)}, u32[]{:S(2)}, u32[]{:S(2)}) %collective-permute-start.13) | collective-permute-done | bytes 8224 | tf_op jit(solution)/shard_map/ppermute | solution.py:38
  61.3 0.8 %total_sums.1 = f32[4,45]{1,0:T(4,128)} custom-call(f32[45,128]{1,0:T(8,128)S(1)} %get-tuple-element.47.slab_ref, f32[16,128]{1,0:T(8,128)S(1)} %collective-permute-done.12.above_ref, f32[16,128]{1,0:T(8,128)S(1)} %collective-permute-done.13.below_ref), custom_call_target="tpu_custom_call" | custom-call | tf_op jit(solution)/shard_map/total_sums/pallas_call | solution.py:469
  (3 shorter events, 0.0 us)
Async XLA Ops:
  0.6 0.7 %copy-start = (f32[1,1,1,4,1024]{4,3,2,1,0:T(4,128)S(1)}, f32[1,1,1,4,1024]{4,3,2,1,0:T(4,128)}, u32[]{:S(2)}) copy-start(f32[1,1,1,4,1024]{4,3,2,1,0:T(4,128)} %param.5) | copy-start | bytes 49156
  1.5 13.2 %collective-permute-start.1 = (f32[32,128]{1,0:T(8,128)S(1)}, f32[32,128]{1,0:T(8,128)S(1)}, u32[]{:S(2)}, u32[]{:S(2)}) collective-permute-start(f32[32,128]{1,0:T(8,128)S(1)} %own_tile.1.own_ref), channel_id=1, source_target_pairs={{0,3},{1,0},{2,1},{3,2},{4,7},{5,4},{6,5},{7,6},{8,11},{9,8},{10,9... | collective-permute-start | bytes 49160 | tf_op jit(solution)/shard_map/ppermute | solution.py:38
  6.6 8.1 %collective-permute-start = (f32[32,128]{1,0:T(8,128)S(1)}, f32[32,128]{1,0:T(8,128)S(1)}, u32[]{:S(2)}, u32[]{:S(2)}) collective-permute-start(f32[32,128]{1,0:T(8,128)S(1)} %own_tile.1.own_ref), channel_id=1, source_target_pairs={{0,1},{1,2},{2,3},{3,0},{4,5},{5,6},{6,7},{7,4},{8,9},{9,10},{10,1... | collective-permute-start | bytes 49160 | tf_op jit(solution)/shard_map/ppermute | solution.py:38
  14.7 4.2 %collective-permute-start.2 = (f32[3,32,128]{2,1,0:T(8,128)S(1)}, f32[3,32,128]{2,1,0:T(8,128)S(1)}, u32[]{:S(2)}, u32[]{:S(2)}) collective-permute-start(f32[3,32,128]{2,1,0:T(8,128)S(1)} %pad_maximum_fusion.2), channel_id=1, source_target_pairs={{0,16},{1,17},{2,18},{3,19},{4,20},{5,21},{6,22},{7,23},{8,24},{9,... | collective-permute-start | bytes 147464 | tf_op jit(solution)/shard_map/ppermute | solution.py:38
  18.9 2.3 %collective-permute-start.4 = (f32[2,3,32,128]{3,2,1,0:T(8,128)S(1)}, f32[2,3,32,128]{3,2,1,0:T(8,128)S(1)}, u32[]{:S(2)}, u32[]{:S(2)}) collective-permute-start(f32[2,3,32,128]{3,2,1,0:T(8,128)S(1)} %get-tuple-element.53), channel_id=1, source_target_pairs={{0,12},{1,13},{2,14},{3,15},{4,0},{5,1},{6,2},{7,3},{8,4},{9,5},{1... | collective-permute-start | bytes 294920 | tf_op jit(solution)/shard_map/ppermute | solution.py:38
  18.9 5.1 %collective-permute-start.3 = (f32[2,3,32,128]{3,2,1,0:T(8,128)S(1)}, f32[2,3,32,128]{3,2,1,0:T(8,128)S(1)}, u32[]{:S(2)}, u32[]{:S(2)}) collective-permute-start(f32[2,3,32,128]{3,2,1,0:T(8,128)S(1)} %get-tuple-element.53), channel_id=1, source_target_pairs={{0,4},{1,5},{2,6},{3,7},{4,8},{5,9},{6,10},{7,11},{8,12},{9,13},{1... | collective-permute-start | bytes 294920 | tf_op jit(solution)/shard_map/ppermute | solution.py:38
  38.7 4.5 %collective-permute-start.8 = (f32[5,32,128]{2,1,0:T(8,128)S(1)}, f32[5,32,128]{2,1,0:T(8,128)S(1)}, u32[]{:S(2)}, u32[]{:S(2)}) collective-permute-start(f32[5,32,128]{2,1,0:T(8,128)S(1)} %get-tuple-element.41.refs_3_), channel_id=1, source_target_pairs={{0,12},{1,13},{2,14},{3,15},{4,0},{5,1},{6,2},{7,3},{8,4},{9,5},{1... | collective-permute-start | bytes 245768 | tf_op jit(solution)/shard_map/ppermute | solution.py:38
  38.8 4.6 %collective-permute-start.9 = (f32[5,32,128]{2,1,0:T(8,128)S(1)}, f32[5,32,128]{2,1,0:T(8,128)S(1)}, u32[]{:S(2)}, u32[]{:S(2)}) collective-permute-start(f32[5,32,128]{2,1,0:T(8,128)S(1)} %get-tuple-element.43.refs_5_), channel_id=1, source_target_pairs={{0,4},{1,5},{2,6},{3,7},{4,8},{5,9},{6,10},{7,11},{8,12},{9,13},{1... | collective-permute-start | bytes 245768 | tf_op jit(solution)/shard_map/ppermute | solution.py:38
  39.3 11.0 %collective-permute-start.5 = (f32[10,32,128]{2,1,0:T(8,128)S(1)}, f32[10,32,128]{2,1,0:T(8,128)S(1)}, u32[]{:S(2)}, u32[]{:S(2)}) collective-permute-start(f32[10,32,128]{2,1,0:T(8,128)S(1)} %get-tuple-element.38.refs_0_), channel_id=1, source_target_pairs={{0,28},{1,29},{2,30},{3,31},{4,16},{5,17},{6,18},{7,19},{8,20},{9,... | collective-permute-start | bytes 491528 | tf_op jit(solution)/shard_map/ppermute | solution.py:38
  41.5 9.1 %collective-permute-start.6 = (f32[10,32,128]{2,1,0:T(8,128)S(1)}, f32[10,32,128]{2,1,0:T(8,128)S(1)}, u32[]{:S(2)}, u32[]{:S(2)}) collective-permute-start(f32[10,32,128]{2,1,0:T(8,128)S(1)} %get-tuple-element.39.refs_1_), channel_id=1, source_target_pairs={{0,16},{1,17},{2,18},{3,19},{4,20},{5,21},{6,22},{7,23},{8,24},{9,... | collective-permute-start | bytes 491528 | tf_op jit(solution)/shard_map/ppermute | solution.py:38
  42.0 9.8 %collective-permute-start.7 = (f32[10,32,128]{2,1,0:T(8,128)S(1)}, f32[10,32,128]{2,1,0:T(8,128)S(1)}, u32[]{:S(2)}, u32[]{:S(2)}) collective-permute-start(f32[10,32,128]{2,1,0:T(8,128)S(1)} %get-tuple-element.40.refs_2_), channel_id=1, source_target_pairs={{0,20},{1,21},{2,22},{3,23},{4,24},{5,25},{6,26},{7,27},{8,28},{9,... | collective-permute-start | bytes 491528 | tf_op jit(solution)/shard_map/ppermute | solution.py:38
  43.2 7.1 %collective-permute-start.10 = (f32[9,32,128]{2,1,0:T(8,128)S(1)}, f32[9,32,128]{2,1,0:T(8,128)S(1)}, u32[]{:S(2)}, u32[]{:S(2)}) collective-permute-start(f32[9,32,128]{2,1,0:T(8,128)S(1)} %get-tuple-element.48), channel_id=1, source_target_pairs={{0,1},{1,2},{2,3},{3,0},{4,5},{5,6},{6,7},{7,4},{8,9},{9,10},{10,1... | collective-permute-start | bytes 442376 | tf_op jit(solution)/shard_map/ppermute | solution.py:38
  43.3 7.0 %collective-permute-start.11 = (f32[9,32,128]{2,1,0:T(8,128)S(1)}, f32[9,32,128]{2,1,0:T(8,128)S(1)}, u32[]{:S(2)}, u32[]{:S(2)}) collective-permute-start(f32[9,32,128]{2,1,0:T(8,128)S(1)} %get-tuple-element.49), channel_id=1, source_target_pairs={{0,3},{1,0},{2,1},{3,2},{4,7},{5,4},{6,5},{7,6},{8,11},{9,8},{10,9... | collective-permute-start | bytes 442376 | tf_op jit(solution)/shard_map/ppermute | solution.py:38
  52.0 5.2 %collective-permute-start.12 = (f32[16,128]{1,0:T(8,128)S(1)}, f32[16,128]{1,0:T(8,128)S(1)}, u32[]{:S(2)}, u32[]{:S(2)}) collective-permute-start(f32[16,128]{1,0:T(8,128)S(1)} %get-tuple-element.50), channel_id=1, source_target_pairs={{0,3},{1,0},{2,1},{3,2},{4,7},{5,4},{6,5},{7,6},{8,11},{9,8},{10,9... | collective-permute-start | bytes 24584 | tf_op jit(solution)/shard_map/ppermute | solution.py:38
  55.8 5.4 %collective-permute-start.13 = (f32[16,128]{1,0:T(8,128)S(1)}, f32[16,128]{1,0:T(8,128)S(1)}, u32[]{:S(2)}, u32[]{:S(2)}) collective-permute-start(f32[16,128]{1,0:T(8,128)S(1)} %get-tuple-element.51), channel_id=1, source_target_pairs={{0,1},{1,2},{2,3},{3,0},{4,5},{5,6},{6,7},{7,4},{8,9},{9,10},{10,1... | collective-permute-start | bytes 24584 | tf_op jit(solution)/shard_map/ppermute | solution.py:38

commit v2 on v1

v2 whole, which is shorter than its diff:
```python
import functools

import jax
import jax.numpy as jnp
import numpy as np
from jax import lax
from jax.experimental import pallas as pl
from jax.experimental.pallas import tpu as pltpu
from jax.sharding import PartitionSpec as P

L2 = 32
WINDOW = 45
ITERS = 4
SPECIES = 4
DEPTH = 4
LANES = DEPTH * L2
ROWS = WINDOW * L2
CENTRE = WINDOW // 2
SUM_ROWS = 48
PIECES = 3
PIECE = WINDOW // PIECES
PIECE_ROWS = PIECE * L2
SPLIT_STEPS = 3
CHUNK = 15
MESH_AXES = ("gx", "gy", "gz")

bf16 = jnp.bfloat16
f32 = jnp.float32
highest = lax.Precision.HIGHEST
MIB = 1 << 20


def shifted(x, shift):
    sizes = [lax.axis_size(axis) for axis in MESH_AXES]
    pairs = []
    for source in np.ndindex(*sizes):
        target = [(i + d) % n for i, d, n in zip(source, shift, sizes)]
        pairs.append(
            (int(np.ravel_multi_index(source, sizes)), int(np.ravel_multi_index(target, sizes)))
        )
    return lax.ppermute(x, MESH_AXES, pairs)


def in_vmem(count):
    return [pl.BlockSpec(memory_space=pltpu.VMEM)] * count


def in_hbm(x):
    return pltpu.with_memory_space_constraint(x, pltpu.HBM)


def halves(x):
    high = x.astype(bf16)
    return high, (x - high.astype(f32)).astype(bf16)


def lane_index(shape):
    return lax.broadcasted_iota(jnp.int32, shape, len(shape) - 1)


def tile_kernel(flat_ref, tile_ref):
    row = lax.broadcasted_iota(jnp.int32, (DEPTH, LANES), 0)
    diagonal = lane_index((DEPTH, LANES)) // L2 == row
    for j in range(L2 // DEPTH):
        part = flat_ref[:, j * LANES : (j + 1) * LANES]
        rolled = [part] + [pltpu.roll(part, m * L2, 1) for m in range(1, DEPTH)]
        for k in range(DEPTH):
            picked = jnp.zeros((DEPTH, LANES), f32)
            for m in range(DEPTH):
                picked = jnp.where(diagonal & (row == (m + k) % DEPTH), rolled[m], picked)
            a = j * DEPTH + k
            tile_ref[a : a + 1, :] = jnp.sum(picked, axis=0, keepdims=True)


def flat_kernel(tile_ref, flat_ref):
    row = lax.broadcasted_iota(jnp.int32, (DEPTH, LANES), 0)
    diagonal = lane_index((DEPTH, LANES)) // L2 == row
    for j in range(L2 // DEPTH):
        spread = []
        for k in range(DEPTH):
            a = j * DEPTH + k
            line = jnp.broadcast_to(tile_ref[a : a + 1, :], (DEPTH, LANES))
            spread.append(jnp.where(diagonal, line, 0.0))
        value = jnp.zeros((DEPTH, LANES), f32)
        for m in range(DEPTH):
            picked = jnp.zeros((DEPTH, LANES), f32)
            for k in range(DEPTH):
                picked = jnp.where(row == (k - m) % DEPTH, spread[k], picked)
            value = value + (picked if m == 0 else pltpu.roll(picked, m * L2, 1))
        flat_ref[:, j * LANES : (j + 1) * LANES] = value


def own_tile(flat):
    return pl.pallas_call(
        tile_kernel,
        out_shape=jax.ShapeDtypeStruct((L2, LANES), f32),
        in_specs=in_vmem(1),
        out_specs=in_vmem(1)[0],
        compiler_params=pltpu.CompilerParams(vmem_limit_bytes=4 * MIB),
        name="own_tile",
    )(flat)


def split_kernel(piece, structure_hbm, own_ref, *refs):
    parts_ref, image_ref, buffer, sems = refs
    step_rows = PIECE_ROWS // SPLIT_STEPS

    def fetch(step):
        rows = pl.ds(piece * PIECE_ROWS + step * step_rows, step_rows)
        return pltpu.make_async_copy(structure_hbm.at[rows, :], buffer.at[step], sems.at[step])

    for step in range(SPLIT_STEPS):
        fetch(step).start()
    lane_tile = CENTRE * L2 // LANES * LANES
    before = CENTRE * L2 - lane_tile
    own_parts = jnp.concatenate(halves(own_ref[...]), axis=1)
    own_parts = jnp.concatenate(
        [
            jnp.zeros((before, 2 * LANES), bf16),
            own_parts,
            jnp.zeros((LANES - before - L2, 2 * LANES), bf16),
        ],
        axis=0,
    )
    half = L2 // 2
    for step in range(SPLIT_STEPS):
        fetch(step).wait()

        def half_cell(i, carry, step=step):
            source = pl.ds(pl.multiple_of(i * half, half), half)
            target = step * 2 * step_rows + i // 2 * 2 * L2 + i % 2 * half
            high, low = halves(buffer[step, source, :])
            parts_ref[pl.ds(pl.multiple_of(target, half), half), :] = high
            parts_ref[pl.ds(pl.multiple_of(target + L2, half), half), :] = low
            return carry

        lax.fori_loop(0, step_rows // half, half_cell, 0, unroll=2)
    product = jnp.dot(
        parts_ref[:, lane_tile : lane_tile + LANES], own_parts, preferred_element_type=f32
    )
    image_ref[...] = four_products(product)


def split_piece(piece, structure, own):
    return pl.pallas_call(
        functools.partial(split_kernel, piece),
        out_shape=(
            jax.ShapeDtypeStruct((2 * PIECE_ROWS, ROWS), bf16),
            jax.ShapeDtypeStruct((PIECE, L2, LANES), f32),
        ),
        in_specs=[pl.BlockSpec(memory_space=pltpu.HBM)] + in_vmem(1),
        out_specs=tuple(in_vmem(2)),
        scratch_shapes=[
            pltpu.VMEM((SPLIT_STEPS, PIECE_ROWS // SPLIT_STEPS, ROWS), f32),
            pltpu.SemaphoreType.DMA((SPLIT_STEPS,)),
        ],
        compiler_params=pltpu.CompilerParams(vmem_limit_bytes=8 * MIB),
        cost_estimate=pl.CostEstimate(
            flops=MIB, bytes_accessed=4 * PIECE_ROWS * ROWS, transcendentals=0
        ),
        name="split_piece",
    )(in_hbm(structure), own)


def setup_kernel(
    species_hbm,
    members_hbm,
    table_hbm,
    member_ref,
    delta_ref,
    species_ref,
    members_ref,
    table_ref,
    table_tile,
    sems,
):
    moves = [(species_hbm, species_ref), (members_hbm, members_ref), (table_hbm, table_ref)]
    copies = [
        pltpu.make_async_copy(source, target, sems.at[i])
        for i, (source, target) in enumerate(moves)
    ]
    for copy in copies:
        copy.start()
    for copy in copies:
        copy.wait()
    tile_kernel(table_ref, table_tile)
    table = table_tile[...]
    moved = [table] + [pltpu.roll(table, m * L2, 1) for m in range(1, SPECIES)]
    group = lane_index((L2, LANES)) // L2
    delta = jnp.zeros((L2, LANES), f32)
    for s in range(DEPTH):
        for kind in range(SPECIES):
            here = (group == s) & (species_ref[0, s] == kind)
            delta = jnp.where(here, moved[(s - kind) % SPECIES], delta)
    delta_ref[...] = delta

    cells = lax.broadcasted_iota(jnp.int32, (WINDOW, WINDOW), 0)
    group = lane_index((WINDOW, LANES)) // L2
    member = jnp.zeros((WINDOW, LANES), f32)
    for s in range(DEPTH):
        found = (members_ref[s : s + 1, :] == cells).astype(f32)
        found = jnp.max(found, axis=1, keepdims=True)
        member = jnp.where(group == s, found, member)
    member_ref[...] = member


def setup(species, members, table):
    return pl.pallas_call(
        setup_kernel,
        out_shape=(
            jax.ShapeDtypeStruct((WINDOW, LANES), f32),
            jax.ShapeDtypeStruct((L2, LANES), f32),
        ),
        in_specs=[pl.BlockSpec(memory_space=pltpu.HBM)] * 3,
        out_specs=tuple(in_vmem(2)),
        scratch_shapes=[
            pltpu.SMEM((1, DEPTH), jnp.int32),
            pltpu.VMEM((DEPTH, WINDOW), jnp.int32),
            pltpu.VMEM((SPECIES, L2 * L2), f32),
            pltpu.VMEM((L2, LANES), f32),
            pltpu.SemaphoreType.DMA((3,)),
        ],
        compiler_params=pltpu.CompilerParams(vmem_limit_bytes=2 * MIB),
        name="setup",
    )(in_hbm(species), in_hbm(members), in_hbm(table))


def four_products(product):
    parts = product.reshape(-1, 2, L2, 2 * LANES)
    high, low = parts[:, 0], parts[:, 1]
    return (high[..., :LANES] + high[..., LANES:]) + (low[..., :LANES] + low[..., LANES:])


def site_blocks(tile):
    lane = lane_index((L2, LANES))
    masks = [(lane // L2 == s).astype(f32).astype(bf16) for s in range(DEPTH)]
    return jnp.concatenate([tile * mask for mask in masks], axis=0)


def moved(window, cell, image):
    blocks = jnp.concatenate([site_blocks(part) for part in halves(image)], axis=1)
    product = jnp.dot(window[cell * 2 * L2 : (cell + 1) * 2 * L2, :], blocks, preferred_element_type=f32)
    return four_products(product)[0]


def keep(column, place, value):
    high, low = halves(value)
    rows = slice(place * L2, (place + 1) * L2)
    column[rows, :LANES] = high
    column[rows, LANES:] = low


def images(parts, cells, column):
    rows = []
    for cell in cells:
        base = cell % PIECE * 2 * L2
        if rows and rows[-1][0] == cell // PIECE and rows[-1][2] == base:
            rows[-1][2] = base + 2 * L2
        else:
            rows.append([cell // PIECE, base, base + 2 * L2])
    left = [parts[piece][low:high, :] for piece, low, high in rows]
    left = left[0] if len(left) == 1 else jnp.concatenate(left, axis=0)
    return four_products(jnp.dot(left, column[...], preferred_element_type=f32))


def window_tile(near_ref, cell):
    dx, dy, dz = cell // 15, cell // 5 % 3, cell % 5 - 2
    dx = dx % near_ref.shape[1]
    own = near_ref[dy, dx, 0]
    if dz == 0:
        return own
    lane = lane_index((L2, LANES))
    if dz > 0:
        joined = jnp.where(lane < dz * L2, near_ref[dy, dx, 2], own)
        return pltpu.roll(joined, LANES - dz * L2, 1)
    joined = jnp.where(lane >= LANES + dz * L2, near_ref[dy, dx, 1], own)
    return pltpu.roll(joined, -dz * L2, 1)


def sweep_over(parts, chunks, source, use_image, slots):
    for i, chunk in enumerate(chunks):
        slots[i % 2][: len(chunk)] = images(parts, chunk, source)
        if i > 0:
            use_image(i - 1, slots[(i - 1) % 2])
    use_image(len(chunks) - 1, slots[(len(chunks) - 1) % 2])


def last_sweep(parts, column, window, own_ref, delta_ref, stage, sent, tau_ref, slots, final):
    high, low = (site_blocks(part) for part in halves(delta_ref[...]))
    delta = jnp.concatenate(
        [
            jnp.concatenate([high, low], axis=1),
            jnp.concatenate([high, jnp.zeros_like(high)], axis=1),
        ],
        axis=0,
    )
    chunks = [[cell_of(ox, oy, oz) for ox, oy in group for oz in range(-2, 3)] for group in stage]

    def use_image(i, slot):
        for place, cell in enumerate(chunks[i]):
            value = moved(window, cell, slot[place])
            if cell == CENTRE:
                value = value + own_ref[...]
                tau_ref[...] = value
            keep(final, place, value)
        count = len(chunks[i])
        product = jnp.dot(final[: count * L2, :], delta, preferred_element_type=f32)
        value = product[:, :LANES] + product[:, LANES:]
        sent[i][...] = value.reshape(count, L2, LANES)

    sweep_over(parts, chunks, column, use_image, slots)


def first_kernel(stage, *refs):
    parts, firsts = refs[:PIECES], refs[PIECES : 2 * PIECES]
    near_ref, member_ref, own_ref, delta_ref = refs[2 * PIECES : 2 * PIECES + 4]
    outs = refs[2 * PIECES + 4 :]
    sent = outs[: len(stage)]
    column, window, other, slot_a, slot_b, final = outs[len(stage) :]
    slots = (slot_a, slot_b)
    for cell in range(WINDOW):
        high, low = halves(window_tile(near_ref, cell) * member_ref[cell : cell + 1, :])
        base = cell * 2 * L2
        window[base : base + L2, :] = high
        window[base + L2 : base + 2 * L2, :] = low

    def update(target, cell, image):
        value = moved(window, cell, image)
        if cell == CENTRE:
            value = value + own_ref[...]
        keep(target, cell, value)

    full = [list(range(base, base + CHUNK)) for base in range(0, WINDOW, CHUNK)]
    source, target = (column, other) if ITERS % 2 == 0 else (other, column)
    for cell in range(WINDOW):
        update(source, cell, firsts[cell // PIECE][cell % PIECE])
    for sweep in range(1, ITERS - 1):

        def use_image(i, slot, target=target):
            for place, cell in enumerate(full[i]):
                update(target, cell, slot[place])

        sweep_over(parts, full, source, use_image, slots)
        source, target = target, source
    last_sweep(parts, source, window, own_ref, delta_ref, stage, sent, None, slots, final)


def next_kernel(stage, *refs):
    parts = refs[:PIECES]
    column, window, own_ref, delta_ref = refs[PIECES : PIECES + 4]
    sent = refs[PIECES + 4 : PIECES + 4 + len(stage)]
    rest = refs[PIECES + 4 + len(stage) :]
    tau_ref = rest[0] if len(rest) == 4 else None
    slot_a, slot_b, final = rest[-3:]
    last_sweep(
        parts, column, window, own_ref, delta_ref, stage, sent, tau_ref, (slot_a, slot_b), final
    )


def stage_call(kernel, name, stage, extra_outs, extra_scratch, operands, flops):
    longest = max(CHUNK, 5 * max(len(group) for group in stage))
    out_shape = [jax.ShapeDtypeStruct((5 * len(group), L2, LANES), f32) for group in stage]
    out_shape += extra_outs
    return pl.pallas_call(
        functools.partial(kernel, stage),
        out_shape=tuple(out_shape),
        in_specs=in_vmem(len(operands)),
        out_specs=tuple(in_vmem(len(out_shape))),
        scratch_shapes=extra_scratch
        + [pltpu.VMEM((longest, L2, LANES), f32)] * 2
        + [pltpu.VMEM((longest * L2, 2 * LANES), bf16)],
        compiler_params=pltpu.CompilerParams(vmem_limit_bytes=16 * MIB),
        cost_estimate=pl.CostEstimate(flops=flops, bytes_accessed=MIB, transcendentals=0),
        name=name,
    )(*operands)


def first_stage(stage, parts, firsts, near, member, own, delta):
    return stage_call(
        first_kernel,
        "first_stage",
        stage,
        [
            jax.ShapeDtypeStruct((ROWS, 2 * LANES), bf16),
            jax.ShapeDtypeStruct((2 * ROWS, LANES), bf16),
        ],
        [pltpu.VMEM((ROWS, 2 * LANES), bf16)],
        (*parts, *firsts, near, member, own, delta),
        2 * 4 * (ITERS - 2) * ROWS * ROWS * LANES,
    )


def next_stage(stage, parts, column, window, own, delta):
    tau = [jax.ShapeDtypeStruct((L2, LANES), f32)]
    return stage_call(
        next_kernel,
        "next_stage",
        stage,
        tau if any((0, 0) in group for group in stage) else [],
        [],
        (*parts, column, window, own, delta),
        2 * ROWS * ROWS * LANES,
    )


def find_tile(groups, refs, ox, oy, oz):
    for group, ref in zip(groups, refs):
        if (ox, oy) in group:
            return ref[group.index((ox, oy)) * 5 + oz + 2]
    raise ValueError("no tile")


def plane_offsets():
    return [(ox, oy) for ox in (-1, 0, 1) for oy in (-1, 0, 1)]


def cell_of(dx, dy, dz):
    return ((dx + 1) * 3 + dy + 1) * 5 + dz + 2


def turn_kernel(groups, *refs):
    own = refs[: len(groups)]
    out, up_ref, down_ref = refs[len(groups) :]
    lane = lane_index((L2, LANES))

    def cell_tile(cell):
        cell = min(cell, WINDOW - 1)
        return find_tile(groups, own, cell // 15 - 1, cell // 5 % 3 - 1, cell % 5 - 2)

    for base in range(0, WINDOW, DEPTH):
        block = jnp.concatenate([cell_tile(base + k) for k in range(DEPTH)], axis=0)
        turned = block.T
        pieces = [turned[s * L2 : (s + 1) * L2] for s in range(DEPTH)]
        for k in range(min(DEPTH, WINDOW - base)):
            value = pieces[0] if k == 0 else pltpu.roll(pieces[0], (-k % DEPTH) * L2, 1)
            for s in range(1, DEPTH):
                move = (s - k) % DEPTH
                piece = pieces[s] if move == 0 else pltpu.roll(pieces[s], move * L2, 1)
                value = jnp.where(lane // L2 == s, piece, value)
            out[base + k] = value
    for place, (dx, dy) in enumerate(plane_offsets()):
        far = pltpu.roll(out[cell_of(dx, dy, 2)], 2 * L2, 1)
        up_ref[place] = jnp.where(lane < 2 * L2, far, out[cell_of(dx, dy, 1)])
        far = pltpu.roll(out[cell_of(dx, dy, -2)], 2 * L2, 1)
        down_ref[place] = jnp.where(lane >= 2 * L2, far, out[cell_of(dx, dy, -1)])


def turned_tiles(groups, own):
    edge = jax.ShapeDtypeStruct((9, L2, LANES), f32)
    return pl.pallas_call(
        functools.partial(turn_kernel, groups),
        out_shape=(jax.ShapeDtypeStruct((WINDOW, L2, LANES), f32), edge, edge),
        in_specs=in_vmem(len(own)),
        out_specs=tuple(in_vmem(3)),
        compiler_params=pltpu.CompilerParams(vmem_limit_bytes=8 * MIB),
        cost_estimate=pl.CostEstimate(flops=MIB, bytes_accessed=2 * MIB, transcendentals=0),
        name="turned_tiles",
    )(*own)


def edge_kernel(groups, *refs):
    got = refs[: len(groups)]
    from_below, from_above, to_below, to_above = refs[len(groups) :]
    lane = lane_index((L2, LANES))
    thin = lane_index((1, LANES))
    for ref in (to_below, to_above):
        ref[...] = jnp.zeros_like(ref)
    for place, (dx, dy) in enumerate(plane_offsets()):
        far = find_tile(groups, got, -dx, -dy, -2)
        close = pltpu.roll(find_tile(groups, got, -dx, -dy, -1), 3 * L2, 1)
        value = jnp.where(lane < 2 * L2, far, close) * from_below[place]
        row = jnp.sum(value, axis=0, keepdims=True)
        cell = cell_of(dx, dy, 1)
        to_below[cell : cell + 1, :] = jnp.where(thin >= 3 * L2, row, 0.0)
        cell = cell_of(dx, dy, 2)
        to_below[cell : cell + 1, :] = jnp.where(thin >= 2 * L2, pltpu.roll(row, 2 * L2, 1), 0.0)
        far = find_tile(groups, got, -dx, -dy, 2)
        close = pltpu.roll(find_tile(groups, got, -dx, -dy, 1), L2, 1)
        value = jnp.where(lane >= 2 * L2, far, close) * from_above[place]
        row = jnp.sum(value, axis=0, keepdims=True)
        cell = cell_of(dx, dy, -1)
        to_above[cell : cell + 1, :] = jnp.where(thin < L2, row, 0.0)
        cell = cell_of(dx, dy, -2)
        to_above[cell : cell + 1, :] = jnp.where(thin < 2 * L2, pltpu.roll(row, 2 * L2, 1), 0.0)


def edge_sums(groups, got, from_below, from_above):
    shape = jax.ShapeDtypeStruct((SUM_ROWS, LANES), f32)
    return pl.pallas_call(
        functools.partial(edge_kernel, groups),
        out_shape=(shape, shape),
        in_specs=in_vmem(len(got) + 2),
        out_specs=tuple(in_vmem(2)),
        compiler_params=pltpu.CompilerParams(vmem_limit_bytes=8 * MIB),
        name="edge_sums",
    )(*got, from_below, from_above)


def slab_kernel(groups, *refs):
    got = refs[: len(groups)]
    turned_ref, tau_ref, sums, flat_ref = refs[len(groups) :]
    flat_kernel(tau_ref, flat_ref)
    sums[WINDOW:, :] = jnp.zeros((SUM_ROWS - WINDOW, LANES), f32)
    lane = lane_index((1, LANES))
    for dx, dy in plane_offsets():
        for dz in range(-2, 3):
            cell = cell_of(dx, dy, dz)
            tile = find_tile(groups, got, -dx, -dy, -dz)
            if dz != 0:
                tile = pltpu.roll(tile, -dz % DEPTH * L2, 1)
            row = jnp.sum(tile * turned_ref[cell], axis=0, keepdims=True)
            if dz > 0:
                row = jnp.where(lane < (DEPTH - dz) * L2, row, 0.0)
            elif dz < 0:
                row = jnp.where(lane >= -dz * L2, row, 0.0)
            sums[cell : cell + 1, :] = row


def slab_sums(groups, got, turned, tau):
    return pl.pallas_call(
        functools.partial(slab_kernel, groups),
        out_shape=(
            jax.ShapeDtypeStruct((SUM_ROWS, LANES), f32),
            jax.ShapeDtypeStruct((DEPTH, L2 * L2), f32),
        ),
        in_specs=in_vmem(len(got) + 2),
        out_specs=tuple(in_vmem(2)),
        compiler_params=pltpu.CompilerParams(vmem_limit_bytes=8 * MIB),
        cost_estimate=pl.CostEstimate(flops=MIB, bytes_accessed=2 * MIB, transcendentals=0),
        name="slab_sums",
    )(*got, turned, tau)


def total_kernel(slab_ref, above_ref, below_ref, out_ref):
    sums = slab_ref[...] + (above_ref[...] + below_ref[...])
    site = lax.broadcasted_iota(jnp.int32, (8, LANES), 0)
    pick = (lane_index((8, LANES)) // L2 == site).astype(f32).astype(bf16)
    high = sums.astype(bf16)
    rest = sums - high.astype(f32)
    middle = rest.astype(bf16)
    low = (rest - middle.astype(f32)).astype(bf16)
    total = lax.dot_general(
        pick,
        jnp.concatenate([high, middle, low], axis=0),
        (((1,), (1,)), ((), ())),
        preferred_element_type=f32,
    )
    total = (total[:, :SUM_ROWS] + total[:, SUM_ROWS : 2 * SUM_ROWS]) + total[:, 2 * SUM_ROWS :]
    out_ref[...] = total[:DEPTH, :WINDOW]


def total_sums(slab, above, below):
    return pl.pallas_call(
        total_kernel,
        out_shape=jax.ShapeDtypeStruct((DEPTH, WINDOW), f32),
        in_specs=in_vmem(3),
        out_specs=in_vmem(1)[0],
        compiler_params=pltpu.CompilerParams(vmem_limit_bytes=4 * MIB),
        name="total_sums",
    )(slab, above, below)


def plane_groups():
    counts = (lax.axis_size("gx"), lax.axis_size("gy"))
    groups = {}
    for ox, oy in plane_offsets():
        groups.setdefault((ox % counts[0], oy % counts[1]), []).append((ox, oy))
    return groups


def body(t_matrix, structure, species, members, delta_table):
    own = own_tile(t_matrix.reshape(DEPTH, L2 * L2))
    structure = structure[0]

    below, above = shifted(own, (0, 0, 1)), shifted(own, (0, 0, -1))
    first = split_piece(0, structure, own)
    slabs = jnp.stack([own, below, above])
    slabs, structure, *first = lax.optimization_barrier((slabs, structure, *first))
    if lax.axis_size("gx") == 2:
        sides = [shifted(slabs, (1, 0, 0)), slabs]
    else:
        sides = [shifted(slabs, (1, 0, 0)), slabs, shifted(slabs, (-1, 0, 0))]
    second = split_piece(1, structure, own)
    plane = jnp.stack(sides)
    plane, structure, *second = lax.optimization_barrier((plane, structure, *second))
    planes = [shifted(plane, (0, 1, 0)), plane, shifted(plane, (0, -1, 0))]
    third = split_piece(2, structure, own)
    member, delta = setup(
        species.reshape(1, DEPTH), members.reshape(DEPTH, WINDOW), delta_table
    )
    near = jnp.stack(planes)
    parts, firsts = zip(first, second, third)

    table = plane_groups()
    shifts = list(table)
    stages = [
        [shift for shift in shifts if shift[0] != 0 and shift[1] == 0],
        [shift for shift in shifts if shift[0] != 0 and shift[1] != 0],
        [shift for shift in shifts if shift[0] == 0],
    ]
    *tiles, column, window = first_stage(
        [table[shift] for shift in stages[0]], parts, firsts, near, member, own, delta
    )
    blocks = dict(zip(stages[0], tiles))
    for stage in stages[1:]:
        *tiles, tau = next_stage(
            [table[shift] for shift in stage], parts, column, window, own, delta
        ) + ((None,) if (0, 0) not in stage else ())
        blocks.update(zip(stage, tiles))
    groups = [table[shift] for shift in shifts]
    sent = [blocks[shift] for shift in shifts]
    got = [
        block if shift == (0, 0) else shifted(block, shift + (0,))
        for shift, block in zip(shifts, sent)
    ]
    turned, up, down = turned_tiles(groups, sent)
    from_below = shifted(up, (0, 0, 1))
    from_above = shifted(down, (0, 0, -1))
    to_below, to_above = edge_sums(groups, got, from_below, from_above)
    above = shifted(to_below, (0, 0, -1))
    below = shifted(to_above, (0, 0, 1))
    slab, site_tau = slab_sums(groups, got, turned, tau)
    pairs = total_sums(slab, above, below)
    return (
        site_tau.reshape(1, 1, 1, DEPTH, L2 * L2),
        pairs.reshape(1, 1, DEPTH, WINDOW),
    )


def solution(mesh):
    placed = (
        P(None, "gx", "gy", "gz", None),
        P(),
        P("gx", "gy", "gz"),
        P("gx", "gy", "gz", None),
        P(),
    )
    return jax.shard_map(
        body,
        mesh=mesh,
        in_specs=placed,
        out_specs=(P(None, "gx", "gy", "gz", None), P("gx", "gy", "gz", None)),
        check_vma=False,
    )
```

time: 62.4 us -> 57.2 us (0.917)
  Pallas kernels: 25.4 us -> 22.7 us
  waiting for transfers between devices: 16.7 us -> 14.5 us
    pallas_call x2 -> x7, Pallas kernels: 22.6 us -> 19.9 us  [the longest x3 12.1 us: stage_call(): pl.pallas_call(functools.partial(kernel, stage), out_shape=tuple(out_shap...]
    ppermute x14, waiting for transfers between devices: 16.7 us -> 14.5 us  [shifted(): return lax.ppermute(x, MESH_AXES, pairs)]
  transfers between devices with their start and end apart: 14 -> 14, of which waited for: 9 -> 7; matrix products, arithmetic and copies ran while one was open for 0% -> 0% of each run, Pallas kernels for 16% -> 19%
where the time goes in v2:
time: 57.2 us; the launch traced here: 56.8 us
  Pallas kernels  22.7 us (40%)
  starting transfers between devices  18.2 us (32%)
  waiting for transfers between devices  14.5 us (25%)
  between operations  0.78 us (1%)
  local copies, waits for them, and re-layouts  0.71 us (1%)
    ppermute x14, starting transfers between devices, shifted(): return lax.ppermute(x, MESH_AXES, pairs)  18.2 us
    ppermute x14, waiting for transfers between devices, shifted(): return lax.ppermute(x, MESH_AXES, pairs)  14.5 us
    pallas_call x3, Pallas kernels, stage_call(): pl.pallas_call(functools.partial(kernel, stage), out_shape=tuple(out_shap...  12.1 us
    pallas_call x3, Pallas kernels, split_piece(): pl.pallas_call(functools.partial(split_kernel, piece), out_shape=(jax.Sha...  6.77 us
  transfers between devices with their start and end apart: 14, of which 7 were waited for; matrix products, arithmetic and copies ran while one was open for 0% of the time, Pallas kernels for 19%

profile of v2, /device:TPU:0, one launch (start us, length us, event | category | flops | bytes accessed | tf_op | source)
XLA Modules:
  0.0 56.8 jit_solution(6535386510265327787)
XLA Ops:
  0.6 0.0 copy-start
  0.6 0.7 %copy-done = f32[1,1,1,4,1024]{4,3,2,1,0:T(4,128)S(1)} copy-done((f32[1,1,1,4,1024]{4,3,2,1,0:T(4,128)S(1)}, f32[1,1,1,4,1024]{4,3,2,1,0:T(4,128)}, u32[]{:S(2)}) %copy-start) | copy-done | bytes 16408
  1.3 0.1 own_tile.1.own_ref.refs_8_.refs_5_
  1.5 5.1 %collective-permute-start.1 = (f32[32,128]{1,0:T(8,128)S(1)}, f32[32,128]{1,0:T(8,128)S(1)}, u32[]{:S(2)}, u32[]{:S(2)}) collective-permute-start(f32[32,128]{1,0:T(8,128)S(1)} %own_tile.1.own_ref.refs_8_.refs_5_), channel_id=1, source_target_pairs={{0,3},{1,0},{2,1},{3,2},{4,7},{5,4},{6,5},{7,6},{8,11},{9,8},{10,9... | collective-permute-start | bytes 49160 | tf_op jit(solution)/shard_map/ppermute | solution.py:41
  6.6 0.0 collective-permute-start
  6.6 2.3 %split_piece.3 = (bf16[960,1440]{1,0:T(8,128)(2,1)S(1)}, f32[15,32,128]{2,1,0:T(8,128)S(1)}) custom-call(f32[1440,1440]{1,0:T(8,128)} %bitcast.16, f32[32,128]{1,0:T(8,128)S(1)} %own_tile.1.own_ref.refs_8_.refs_5_), custom_call_target="tpu_custom_call" | custom-call | flops 1048576 | bytes 2764800 | tf_op jit(solution)/shard_map/split_piece/pallas_call | solution.py:145
  8.9 0.0 collective-permute-done.1
  8.9 3.3 %collective-permute-done = f32[32,128]{1,0:T(8,128)S(1)} collective-permute-done((f32[32,128]{1,0:T(8,128)S(1)}, f32[32,128]{1,0:T(8,128)S(1)}, u32[]{:S(2)}, u32[]{:S(2)}) %collective-permute-start) | collective-permute-done | bytes 16416 | tf_op jit(solution)/shard_map/ppermute | solution.py:41
  12.1 1.5 %collective-permute-start.2 = (f32[3,32,128]{2,1,0:T(8,128)S(1)}, f32[3,32,128]{2,1,0:T(8,128)S(1)}, u32[]{:S(2)}, u32[]{:S(2)}) collective-permute-start(f32[3,32,128]{2,1,0:T(8,128)S(1)} %pad_maximum_fusion.2), channel_id=1, source_target_pairs={{0,16},{1,17},{2,18},{3,19},{4,20},{5,21},{6,22},{7,23},{8,24},{9,... | collective-permute-start | bytes 147464 | tf_op jit(solution)/shard_map/ppermute | solution.py:41
  13.6 2.3 %split_piece.4 = (bf16[960,1440]{1,0:T(8,128)(2,1)S(1)}, f32[15,32,128]{2,1,0:T(8,128)S(1)}) custom-call(f32[1440,1440]{1,0:T(8,128)} %bitcast.17, f32[32,128]{1,0:T(8,128)S(1)} %own_tile.1.own_ref.refs_8_.refs_5_), custom_call_target="tpu_custom_call" | custom-call | flops 1048576 | bytes 2764800 | tf_op jit(solution)/shard_map/split_piece/pallas_call | solution.py:145
  15.9 0.3 collective-permute-done.2
  16.2 0.1 collective-permute-start.4
  16.3 0.5 collective-permute-start.3
  16.8 1.0 %setup.1 = (f32[45,128]{1,0:T(8,128)S(1)}, f32[32,128]{1,0:T(8,128)S(1)}) custom-call(s32[1,4]{1,0:T(1,128)} %bitcast.28, s32[4,45]{1,0:T(4,128)} %bitcast.26, f32[4,1024]{1,0:T(4,128)} %table_hbm.1), custom_call_target="tpu_custom_call" | custom-call | tf_op jit(solution)/shard_map/setup/pallas_call | solution.py:208
  17.8 2.3 %split_piece.5 = (bf16[960,1440]{1,0:T(8,128)(2,1)S(1)}, f32[15,32,128]{2,1,0:T(8,128)S(1)}) custom-call(f32[1440,1440]{1,0:T(8,128)} %bitcast.18, f32[32,128]{1,0:T(8,128)S(1)} %own_tile.1.own_ref.refs_8_.refs_5_), custom_call_target="tpu_custom_call" | custom-call | flops 1048576 | bytes 2764800 | tf_op jit(solution)/shard_map/split_piece/pallas_call | solution.py:145
  20.1 0.0 collective-permute-done.4
  20.1 1.4 %collective-permute-done.3 = f32[2,3,32,128]{3,2,1,0:T(8,128)S(1)} collective-permute-done((f32[2,3,32,128]{3,2,1,0:T(8,128)S(1)}, f32[2,3,32,128]{3,2,1,0:T(8,128)S(1)}, u32[]{:S(2)}, u32[]{:S(2)}) %collective-permute-start.3) | collective-permute-done | bytes 98336 | tf_op jit(solution)/shard_map/ppermute | solution.py:41
  21.5 8.9 %first_stage.1 = (f32[10,32,128]{2,1,0:T(8,128)S(1)}, bf16[1440,256]{1,0:T(8,128)(2,1)S(1)}, bf16[2880,128]{1,0:T(8,128)(2,1)S(1)}) custom-call(bf16[960,1440]{1,0:T(8,128)(2,1)S(1)} %get-tuple-element.36.refs_0_, bf16[960,1440]{1,0:T(8,128)(2,1)S(1)} %get-tuple-element.41.refs_1_, bf16[960,1440]{1,0:T(8,128)(2,1)S(1)} %get-tuple-element.43.refs_2_, ...), custom_call_target="tpu_custom_call" | custom-call | flops 4246732800 | bytes 1048576 | tf_op jit(solution)/shard_map/first_stage/pallas_call | solution.py:364
  30.3 1.6 %next_stage.3 = (f32[5,32,128]{2,1,0:T(8,128)S(1)}, f32[5,32,128]{2,1,0:T(8,128)S(1)}, f32[5,32,128]{2,1,0:T(8,128)S(1)}, f32[32,128]{1,0:T(8,128)S(1)}) custom-call(bf16[960,1440]{1,0:T(8,128)(2,1)S(1)} %get-tuple-element.36.refs_0_, bf16[960,1440]{1,0:T(8,128)(2,1)S(1)} %get-tuple-element.41.refs_1_, bf16[960,1440]{1,0:T(8,128)(2,1)S(1)} %get-tuple-element.43.refs_2_, ...), custom_call_target="tpu_custom_call" | custom-call | flops 530841600 | bytes 1048576 | tf_op jit(solution)/shard_map/next_stage/pallas_call | solution.py:364
  31.9 0.1 collective-permute-start.8
  32.0 0.5 collective-permute-start.9
  32.5 1.5 %collective-permute-start.6 = (f32[10,32,128]{2,1,0:T(8,128)S(1)}, f32[10,32,128]{2,1,0:T(8,128)S(1)}, u32[]{:S(2)}, u32[]{:S(2)}) collective-permute-start(f32[10,32,128]{2,1,0:T(8,128)S(1)} %get-tuple-element.53.refs_1_), channel_id=1, source_target_pairs={{0,16},{1,17},{2,18},{3,19},{4,20},{5,21},{6,22},{7,23},{8,24},{9,... | collective-permute-start | bytes 491528 | tf_op jit(solution)/shard_map/ppermute | solution.py:41
  34.0 1.6 %next_stage.2 = (f32[10,32,128]{2,1,0:T(8,128)S(1)}, f32[10,32,128]{2,1,0:T(8,128)S(1)}) custom-call(bf16[960,1440]{1,0:T(8,128)(2,1)S(1)} %get-tuple-element.36.refs_0_, bf16[960,1440]{1,0:T(8,128)(2,1)S(1)} %get-tuple-element.41.refs_1_, bf16[960,1440]{1,0:T(8,128)(2,1)S(1)} %get-tuple-element.43.refs_2_, bf16[1440,256]{1,0:T(8,128)(2,1)S(1)} %get-tuple-element.50.refs_3_, ...), custom_call_target="tpu_custom_call" | custom-call | flops 530841600 | bytes 1048576 | tf_op jit(solution)/shard_map/next_stage/pallas_call | solution.py:364
  35.7 1.0 %collective-permute-start.5 = (f32[10,32,128]{2,1,0:T(8,128)S(1)}, f32[10,32,128]{2,1,0:T(8,128)S(1)}, u32[]{:S(2)}, u32[]{:S(2)}) collective-permute-start(f32[10,32,128]{2,1,0:T(8,128)S(1)} %get-tuple-element.52.refs_0_), channel_id=1, source_target_pairs={{0,28},{1,29},{2,30},{3,31},{4,16},{5,17},{6,18},{7,19},{8,20},{9,... | collective-permute-start | bytes 491528 | tf_op jit(solution)/shard_map/ppermute | solution.py:41
  36.7 0.8 %collective-permute-start.7 = (f32[10,32,128]{2,1,0:T(8,128)S(1)}, f32[10,32,128]{2,1,0:T(8,128)S(1)}, u32[]{:S(2)}, u32[]{:S(2)}) collective-permute-start(f32[10,32,128]{2,1,0:T(8,128)S(1)} %get-tuple-element.54.refs_2_), channel_id=1, source_target_pairs={{0,20},{1,21},{2,22},{3,23},{4,24},{5,25},{6,26},{7,27},{8,28},{9,... | collective-permute-start | bytes 491528 | tf_op jit(solution)/shard_map/ppermute | solution.py:41
  37.5 0.9 %turned_tiles.1 = (f32[45,32,128]{2,1,0:T(8,128)S(1)}, f32[9,32,128]{2,1,0:T(8,128)S(1)}, f32[9,32,128]{2,1,0:T(8,128)S(1)}) custom-call(f32[10,32,128]{2,1,0:T(8,128)S(1)} %get-tuple-element.52.refs_0_, f32[10,32,128]{2,1,0:T(8,128)S(1)} %get-tuple-element.53.refs_1_, f32[10,32,128]{2,1,0:T(8,128)S(1)} %get-tuple-element.54.refs_2_, ...), custom_call_target="tpu_custom_call" | custom-call | flops 1048576 | bytes 2097152 | tf_op jit(solution)/shard_map/turned_tiles/pallas_call | solution.py:450
  38.4 0.0 collective-permute-done.8.refs_3_
  38.4 0.1 collective-permute-start.10
  38.5 0.0 collective-permute-done.9.refs_5_
  38.5 3.8 %collective-permute-start.11 = (f32[9,32,128]{2,1,0:T(8,128)S(1)}, f32[9,32,128]{2,1,0:T(8,128)S(1)}, u32[]{:S(2)}, u32[]{:S(2)}) collective-permute-start(f32[9,32,128]{2,1,0:T(8,128)S(1)} %get-tuple-element.63), channel_id=1, source_target_pairs={{0,3},{1,0},{2,1},{3,2},{4,7},{5,4},{6,5},{7,6},{8,11},{9,8},{10,9... | collective-permute-start | bytes 442376 | tf_op jit(solution)/shard_map/ppermute | solution.py:41
  42.3 3.8 %collective-permute-done.10.refs_6_ = f32[9,32,128]{2,1,0:T(8,128)S(1)} collective-permute-done((f32[9,32,128]{2,1,0:T(8,128)S(1)}, f32[9,32,128]{2,1,0:T(8,128)S(1)}, u32[]{:S(2)}, u32[]{:S(2)}) %collective-permute-start.10) | collective-permute-done | bytes 147488 | tf_op jit(solution)/shard_map/ppermute | solution.py:41
  46.1 0.7 %collective-permute-done.11.refs_7_ = f32[9,32,128]{2,1,0:T(8,128)S(1)} collective-permute-done((f32[9,32,128]{2,1,0:T(8,128)S(1)}, f32[9,32,128]{2,1,0:T(8,128)S(1)}, u32[]{:S(2)}, u32[]{:S(2)}) %collective-permute-start.11) | collective-permute-done | bytes 147488 | tf_op jit(solution)/shard_map/ppermute | solution.py:41
  46.9 0.0 collective-permute-done.6.refs_1_
  46.9 0.0 collective-permute-done.5.refs_0_
  46.9 0.0 collective-permute-done.7.refs_2_
  46.9 0.2 edge_sums.1
  47.1 3.3 %collective-permute-start.12 = (f32[48,128]{1,0:T(8,128)S(1)}, f32[48,128]{1,0:T(8,128)S(1)}, u32[]{:S(2)}, u32[]{:S(2)}) collective-permute-start(f32[48,128]{1,0:T(8,128)S(1)} %get-tuple-element.64), channel_id=1, source_target_pairs={{0,3},{1,0},{2,1},{3,2},{4,7},{5,4},{6,5},{7,6},{8,11},{9,8},{10,9... | collective-permute-start | bytes 73736 | tf_op jit(solution)/shard_map/ppermute | solution.py:41
  50.4 0.0 collective-permute-start.13
  50.4 0.7 %slab_sums.1 = (f32[48,128]{1,0:T(8,128)S(1)}, f32[4,1024]{1,0:T(4,128)}) custom-call(f32[10,32,128]{2,1,0:T(8,128)S(1)} %collective-permute-done.5.refs_0_, f32[10,32,128]{2,1,0:T(8,128)S(1)} %collective-permute-done.6.refs_1_, f32[10,32,128]{2,1,0:T(8,128)S(1)} %collective-permute-done.7.refs_2_, f32[5,32,128]{2,1,0:T(8,128)S(1)} %collective-permute-done.8.refs_3_, ...), custom_call_target="tpu_custom_call" | custom-call | flops 1048576 | bytes 2097152 | tf_op jit(solution)/shard_map/slab_sums/pallas_call | solution.py:520
  51.1 0.8 %collective-permute-done.12.above_ref = f32[48,128]{1,0:T(8,128)S(1)} collective-permute-done((f32[48,128]{1,0:T(8,128)S(1)}, f32[48,128]{1,0:T(8,128)S(1)}, u32[]{:S(2)}, u32[]{:S(2)}) %collective-permute-start.12) | collective-permute-done | bytes 24608 | tf_op jit(solution)/shard_map/ppermute | solution.py:41
  51.9 4.1 %collective-permute-done.13.below_ref = f32[48,128]{1,0:T(8,128)S(1)} collective-permute-done((f32[48,128]{1,0:T(8,128)S(1)}, f32[48,128]{1,0:T(8,128)S(1)}, u32[]{:S(2)}, u32[]{:S(2)}) %collective-permute-start.13) | collective-permute-done | bytes 24608 | tf_op jit(solution)/shard_map/ppermute | solution.py:41
  56.0 0.8 %total_sums.1 = f32[4,45]{1,0:T(4,128)} custom-call(f32[48,128]{1,0:T(8,128)S(1)} %get-tuple-element.61.slab_ref, f32[48,128]{1,0:T(8,128)S(1)} %collective-permute-done.12.above_ref, f32[48,128]{1,0:T(8,128)S(1)} %collective-permute-done.13.below_ref), custom_call_target="tpu_custom_call" | custom-call | tf_op jit(solution)/shard_map/total_sums/pallas_call | solution.py:553
  (3 shorter events, 0.0 us)
Async XLA Ops:
  0.6 0.7 %copy-start = (f32[1,1,1,4,1024]{4,3,2,1,0:T(4,128)S(1)}, f32[1,1,1,4,1024]{4,3,2,1,0:T(4,128)}, u32[]{:S(2)}) copy-start(f32[1,1,1,4,1024]{4,3,2,1,0:T(4,128)} %param.5) | copy-start | bytes 49156
  1.5 7.4 %collective-permute-start.1 = (f32[32,128]{1,0:T(8,128)S(1)}, f32[32,128]{1,0:T(8,128)S(1)}, u32[]{:S(2)}, u32[]{:S(2)}) collective-permute-start(f32[32,128]{1,0:T(8,128)S(1)} %own_tile.1.own_ref.refs_8_.refs_5_), channel_id=1, source_target_pairs={{0,3},{1,0},{2,1},{3,2},{4,7},{5,4},{6,5},{7,6},{8,11},{9,8},{10,9... | collective-permute-start | bytes 49160 | tf_op jit(solution)/shard_map/ppermute | solution.py:41
  6.6 5.5 %collective-permute-start = (f32[32,128]{1,0:T(8,128)S(1)}, f32[32,128]{1,0:T(8,128)S(1)}, u32[]{:S(2)}, u32[]{:S(2)}) collective-permute-start(f32[32,128]{1,0:T(8,128)S(1)} %own_tile.1.own_ref.refs_8_.refs_5_), channel_id=1, source_target_pairs={{0,1},{1,2},{2,3},{3,0},{4,5},{5,6},{6,7},{7,4},{8,9},{9,10},{10,1... | collective-permute-start | bytes 49160 | tf_op jit(solution)/shard_map/ppermute | solution.py:41
  12.1 4.1 %collective-permute-start.2 = (f32[3,32,128]{2,1,0:T(8,128)S(1)}, f32[3,32,128]{2,1,0:T(8,128)S(1)}, u32[]{:S(2)}, u32[]{:S(2)}) collective-permute-start(f32[3,32,128]{2,1,0:T(8,128)S(1)} %pad_maximum_fusion.2), channel_id=1, source_target_pairs={{0,16},{1,17},{2,18},{3,19},{4,20},{5,21},{6,22},{7,23},{8,24},{9,... | collective-permute-start | bytes 147464 | tf_op jit(solution)/shard_map/ppermute | solution.py:41
  16.2 3.8 %collective-permute-start.4 = (f32[2,3,32,128]{3,2,1,0:T(8,128)S(1)}, f32[2,3,32,128]{3,2,1,0:T(8,128)S(1)}, u32[]{:S(2)}, u32[]{:S(2)}) collective-permute-start(f32[2,3,32,128]{3,2,1,0:T(8,128)S(1)} %pad_maximum_fusion.1), channel_id=1, source_target_pairs={{0,12},{1,13},{2,14},{3,15},{4,0},{5,1},{6,2},{7,3},{8,4},{9,5},{1... | collective-permute-start | bytes 294920 | tf_op jit(solution)/shard_map/ppermute | solution.py:41
  16.3 5.1 %collective-permute-start.3 = (f32[2,3,32,128]{3,2,1,0:T(8,128)S(1)}, f32[2,3,32,128]{3,2,1,0:T(8,128)S(1)}, u32[]{:S(2)}, u32[]{:S(2)}) collective-permute-start(f32[2,3,32,128]{3,2,1,0:T(8,128)S(1)} %pad_maximum_fusion.1), channel_id=1, source_target_pairs={{0,4},{1,5},{2,6},{3,7},{4,8},{5,9},{6,10},{7,11},{8,12},{9,13},{1... | collective-permute-start | bytes 294920 | tf_op jit(solution)/shard_map/ppermute | solution.py:41
  31.9 6.5 %collective-permute-start.8 = (f32[5,32,128]{2,1,0:T(8,128)S(1)}, f32[5,32,128]{2,1,0:T(8,128)S(1)}, u32[]{:S(2)}, u32[]{:S(2)}) collective-permute-start(f32[5,32,128]{2,1,0:T(8,128)S(1)} %get-tuple-element.55.refs_3_), channel_id=1, source_target_pairs={{0,12},{1,13},{2,14},{3,15},{4,0},{5,1},{6,2},{7,3},{8,4},{9,5},{1... | collective-permute-start | bytes 245768 | tf_op jit(solution)/shard_map/ppermute | solution.py:41
  32.0 6.5 %collective-permute-start.9 = (f32[5,32,128]{2,1,0:T(8,128)S(1)}, f32[5,32,128]{2,1,0:T(8,128)S(1)}, u32[]{:S(2)}, u32[]{:S(2)}) collective-permute-start(f32[5,32,128]{2,1,0:T(8,128)S(1)} %get-tuple-element.57.refs_5_), channel_id=1, source_target_pairs={{0,4},{1,5},{2,6},{3,7},{4,8},{5,9},{6,10},{7,11},{8,12},{9,13},{1... | collective-permute-start | bytes 245768 | tf_op jit(solution)/shard_map/ppermute | solution.py:41
  32.5 14.4 %collective-permute-start.6 = (f32[10,32,128]{2,1,0:T(8,128)S(1)}, f32[10,32,128]{2,1,0:T(8,128)S(1)}, u32[]{:S(2)}, u32[]{:S(2)}) collective-permute-start(f32[10,32,128]{2,1,0:T(8,128)S(1)} %get-tuple-element.53.refs_1_), channel_id=1, source_target_pairs={{0,16},{1,17},{2,18},{3,19},{4,20},{5,21},{6,22},{7,23},{8,24},{9,... | collective-permute-start | bytes 491528 | tf_op jit(solution)/shard_map/ppermute | solution.py:41
  35.7 11.2 %collective-permute-start.5 = (f32[10,32,128]{2,1,0:T(8,128)S(1)}, f32[10,32,128]{2,1,0:T(8,128)S(1)}, u32[]{:S(2)}, u32[]{:S(2)}) collective-permute-start(f32[10,32,128]{2,1,0:T(8,128)S(1)} %get-tuple-element.52.refs_0_), channel_id=1, source_target_pairs={{0,28},{1,29},{2,30},{3,31},{4,16},{5,17},{6,18},{7,19},{8,20},{9,... | collective-permute-start | bytes 491528 | tf_op jit(solution)/shard_map/ppermute | solution.py:41
  36.7 10.2 %collective-permute-start.7 = (f32[10,32,128]{2,1,0:T(8,128)S(1)}, f32[10,32,128]{2,1,0:T(8,128)S(1)}, u32[]{:S(2)}, u32[]{:S(2)}) collective-permute-start(f32[10,32,128]{2,1,0:T(8,128)S(1)} %get-tuple-element.54.refs_2_), channel_id=1, source_target_pairs={{0,20},{1,21},{2,22},{3,23},{4,24},{5,25},{6,26},{7,27},{8,28},{9,... | collective-permute-start | bytes 491528 | tf_op jit(solution)/shard_map/ppermute | solution.py:41
  38.4 7.7 %collective-permute-start.10 = (f32[9,32,128]{2,1,0:T(8,128)S(1)}, f32[9,32,128]{2,1,0:T(8,128)S(1)}, u32[]{:S(2)}, u32[]{:S(2)}) collective-permute-start(f32[9,32,128]{2,1,0:T(8,128)S(1)} %get-tuple-element.62), channel_id=1, source_target_pairs={{0,1},{1,2},{2,3},{3,0},{4,5},{5,6},{6,7},{7,4},{8,9},{9,10},{10,1... | collective-permute-start | bytes 442376 | tf_op jit(solution)/shard_map/ppermute | solution.py:41
  38.5 8.4 %collective-permute-start.11 = (f32[9,32,128]{2,1,0:T(8,128)S(1)}, f32[9,32,128]{2,1,0:T(8,128)S(1)}, u32[]{:S(2)}, u32[]{:S(2)}) collective-permute-start(f32[9,32,128]{2,1,0:T(8,128)S(1)} %get-tuple-element.63), channel_id=1, source_target_pairs={{0,3},{1,0},{2,1},{3,2},{4,7},{5,4},{6,5},{7,6},{8,11},{9,8},{10,9... | collective-permute-start | bytes 442376 | tf_op jit(solution)/shard_map/ppermute | solution.py:41
  47.1 4.8 %collective-permute-start.12 = (f32[48,128]{1,0:T(8,128)S(1)}, f32[48,128]{1,0:T(8,128)S(1)}, u32[]{:S(2)}, u32[]{:S(2)}) collective-permute-start(f32[48,128]{1,0:T(8,128)S(1)} %get-tuple-element.64), channel_id=1, source_target_pairs={{0,3},{1,0},{2,1},{3,2},{4,7},{5,4},{6,5},{7,6},{8,11},{9,8},{10,9... | collective-permute-start | bytes 73736 | tf_op jit(solution)/shard_map/ppermute | solution.py:41
  50.4 5.6 %collective-permute-start.13 = (f32[48,128]{1,0:T(8,128)S(1)}, f32[48,128]{1,0:T(8,128)S(1)}, u32[]{:S(2)}, u32[]{:S(2)}) collective-permute-start(f32[48,128]{1,0:T(8,128)S(1)} %get-tuple-element.65), channel_id=1, source_target_pairs={{0,1},{1,2},{2,3},{3,0},{4,5},{5,6},{6,7},{7,4},{8,9},{9,10},{10,1... | collective-permute-start | bytes 73736 | tf_op jit(solution)/shard_map/ppermute | solution.py:41

commit v3 on v2

--- a/solution.py
+++ b/solution.py
@@ -7,6 +7,7 @@
 from jax.experimental import pallas as pl
 from jax.experimental.pallas import tpu as pltpu
 from jax.sharding import PartitionSpec as P
+
 
 L2 = 32
 WINDOW = 45
@@ -24,9 +25,9 @@
 CHUNK = 15
 MESH_AXES = ("gx", "gy", "gz")
 
+
 bf16 = jnp.bfloat16
 f32 = jnp.float32
-highest = lax.Precision.HIGHEST
 MIB = 1 << 20
 
 
@@ -334,7 +335,7 @@
     source, target = (column, other) if ITERS % 2 == 0 else (other, column)
     for cell in range(WINDOW):
         update(source, cell, firsts[cell // PIECE][cell % PIECE])
-    for sweep in range(1, ITERS - 1):
+    for _ in range(1, ITERS - 1):
 
         def use_image(i, slot, target=target):
             for place, cell in enumerate(full[i]):
@@ -357,7 +358,7 @@
     )
 
 
-def stage_call(kernel, name, stage, extra_outs, extra_scratch, operands, flops):
+def stage_call(kernel, stage, extra_outs, extra_scratch, operands, flops):
     longest = max(CHUNK, 5 * max(len(group) for group in stage))
     out_shape = [jax.ShapeDtypeStruct((5 * len(group), L2, LANES), f32) for group in stage]
     out_shape += extra_outs
@@ -371,14 +372,12 @@
         + [pltpu.VMEM((longest * L2, 2 * LANES), bf16)],
         compiler_params=pltpu.CompilerParams(vmem_limit_bytes=16 * MIB),
         cost_estimate=pl.CostEstimate(flops=flops, bytes_accessed=MIB, transcendentals=0),
-        name=name,
     )(*operands)
 
 
 def first_stage(stage, parts, firsts, near, member, own, delta):
     return stage_call(
         first_kernel,
-        "first_stage",
         stage,
         [
             jax.ShapeDtypeStruct((ROWS, 2 * LANES), bf16),
@@ -394,7 +393,6 @@
     tau = [jax.ShapeDtypeStruct((L2, LANES), f32)]
     return stage_call(
         next_kernel,
-        "next_stage",
         stage,
         tau if any((0, 0) in group for group in stage) else [],
         [],
@@ -602,17 +600,19 @@
         [table[shift] for shift in stages[0]], parts, firsts, near, member, own, delta
     )
     blocks = dict(zip(stages[0], tiles))
-    for stage in stages[1:]:
-        *tiles, tau = next_stage(
-            [table[shift] for shift in stage], parts, column, window, own, delta
-        ) + ((None,) if (0, 0) not in stage else ())
-        blocks.update(zip(stage, tiles))
+    got = {}
+    for number, stage in enumerate(stages):
+        if number > 0:
+            tiles = next_stage([table[shift] for shift in stage], parts, column, window, own, delta)
+            if (0, 0) in stage:
+                tau = tiles[-1]
+            blocks.update(zip(stage, tiles))
+        for shift in stage:
+            block = blocks[shift]
+            got[shift] = block if shift == (0, 0) else shifted(block, shift + (0,))
     groups = [table[shift] for shift in shifts]
     sent = [blocks[shift] for shift in shifts]
-    got = [
-        block if shift == (0, 0) else shifted(block, shift + (0,))
-        for shift, block in zip(shifts, sent)
-    ]
+    got = [got[shift] for shift in shifts]
     turned, up, down = turned_tiles(groups, sent)
     from_below = shifted(up, (0, 0, 1))
     from_above = shifted(down, (0, 0, -1))

time: 57.2 us -> 57.2 us (level)
  no operation moved by 1% of the time
where the time goes in v3:
time: 57.2 us; the launch traced here: 56.8 us
  Pallas kernels  22.7 us (40%)
  starting transfers between devices  18.2 us (32%)
  waiting for transfers between devices  14.5 us (25%)
  between operations  0.78 us (1%)
  local copies, waits for them, and re-layouts  0.71 us (1%)
    ppermute x14, starting transfers between devices, shifted(): return lax.ppermute(x, MESH_AXES, pairs)  18.2 us
    ppermute x14, waiting for transfers between devices, shifted(): return lax.ppermute(x, MESH_AXES, pairs)  14.5 us
    pallas_call x3, Pallas kernels, stage_call(): pl.pallas_call(functools.partial(kernel, stage), out_shape=tuple(out_shap...  12.1 us
    pallas_call x3, Pallas kernels, split_piece(): pl.pallas_call(functools.partial(split_kernel, piece), out_shape=(jax.Sha...  6.77 us
  transfers between devices with their start and end apart: 14, of which 7 were waited for; matrix products, arithmetic and copies ran while one was open for 0% of the time, Pallas kernels for 19%

profile of v3, /device:TPU:0, one launch (start us, length us, event | category | flops | bytes accessed | tf_op | source)
XLA Modules:
  0.0 56.8 jit_solution(6535386510265327787)
XLA Ops:
  0.6 0.0 copy-start
  0.6 0.7 %copy-done = f32[1,1,1,4,1024]{4,3,2,1,0:T(4,128)S(1)} copy-done((f32[1,1,1,4,1024]{4,3,2,1,0:T(4,128)S(1)}, f32[1,1,1,4,1024]{4,3,2,1,0:T(4,128)}, u32[]{:S(2)}) %copy-start) | copy-done | bytes 16408
  1.3 0.1 own_tile.1.own_ref.refs_8_.refs_5_
  1.5 5.1 %collective-permute-start.1 = (f32[32,128]{1,0:T(8,128)S(1)}, f32[32,128]{1,0:T(8,128)S(1)}, u32[]{:S(2)}, u32[]{:S(2)}) collective-permute-start(f32[32,128]{1,0:T(8,128)S(1)} %own_tile.1.own_ref.refs_8_.refs_5_), channel_id=1, source_target_pairs={{0,3},{1,0},{2,1},{3,2},{4,7},{5,4},{6,5},{7,6},{8,11},{9,8},{10,9... | collective-permute-start | bytes 49160 | tf_op jit(solution)/shard_map/ppermute | solution.py:42
  6.6 0.0 collective-permute-start
  6.6 2.3 %split_piece.3 = (bf16[960,1440]{1,0:T(8,128)(2,1)S(1)}, f32[15,32,128]{2,1,0:T(8,128)S(1)}) custom-call(f32[1440,1440]{1,0:T(8,128)} %bitcast.16, f32[32,128]{1,0:T(8,128)S(1)} %own_tile.1.own_ref.refs_8_.refs_5_), custom_call_target="tpu_custom_call" | custom-call | flops 1048576 | bytes 2764800 | tf_op jit(solution)/shard_map/split_piece/pallas_call | solution.py:146
  8.9 0.0 collective-permute-done.1
  8.9 3.3 %collective-permute-done = f32[32,128]{1,0:T(8,128)S(1)} collective-permute-done((f32[32,128]{1,0:T(8,128)S(1)}, f32[32,128]{1,0:T(8,128)S(1)}, u32[]{:S(2)}, u32[]{:S(2)}) %collective-permute-start) | collective-permute-done | bytes 16416 | tf_op jit(solution)/shard_map/ppermute | solution.py:42
  12.1 1.5 %collective-permute-start.2 = (f32[3,32,128]{2,1,0:T(8,128)S(1)}, f32[3,32,128]{2,1,0:T(8,128)S(1)}, u32[]{:S(2)}, u32[]{:S(2)}) collective-permute-start(f32[3,32,128]{2,1,0:T(8,128)S(1)} %pad_maximum_fusion.2), channel_id=1, source_target_pairs={{0,16},{1,17},{2,18},{3,19},{4,20},{5,21},{6,22},{7,23},{8,24},{9,... | collective-permute-start | bytes 147464 | tf_op jit(solution)/shard_map/ppermute | solution.py:42
  13.6 2.3 %split_piece.4 = (bf16[960,1440]{1,0:T(8,128)(2,1)S(1)}, f32[15,32,128]{2,1,0:T(8,128)S(1)}) custom-call(f32[1440,1440]{1,0:T(8,128)} %bitcast.17, f32[32,128]{1,0:T(8,128)S(1)} %own_tile.1.own_ref.refs_8_.refs_5_), custom_call_target="tpu_custom_call" | custom-call | flops 1048576 | bytes 2764800 | tf_op jit(solution)/shard_map/split_piece/pallas_call | solution.py:146
  15.9 0.3 collective-permute-done.2
  16.2 0.1 collective-permute-start.4
  16.3 0.5 collective-permute-start.3
  16.8 1.0 %setup.1 = (f32[45,128]{1,0:T(8,128)S(1)}, f32[32,128]{1,0:T(8,128)S(1)}) custom-call(s32[1,4]{1,0:T(1,128)} %bitcast.28, s32[4,45]{1,0:T(4,128)} %bitcast.26, f32[4,1024]{1,0:T(4,128)} %table_hbm.1), custom_call_target="tpu_custom_call" | custom-call | tf_op jit(solution)/shard_map/setup/pallas_call | solution.py:209
  17.8 2.3 %split_piece.5 = (bf16[960,1440]{1,0:T(8,128)(2,1)S(1)}, f32[15,32,128]{2,1,0:T(8,128)S(1)}) custom-call(f32[1440,1440]{1,0:T(8,128)} %bitcast.18, f32[32,128]{1,0:T(8,128)S(1)} %own_tile.1.own_ref.refs_8_.refs_5_), custom_call_target="tpu_custom_call" | custom-call | flops 1048576 | bytes 2764800 | tf_op jit(solution)/shard_map/split_piece/pallas_call | solution.py:146
  20.1 0.0 collective-permute-done.4
  20.1 1.4 %collective-permute-done.3 = f32[2,3,32,128]{3,2,1,0:T(8,128)S(1)} collective-permute-done((f32[2,3,32,128]{3,2,1,0:T(8,128)S(1)}, f32[2,3,32,128]{3,2,1,0:T(8,128)S(1)}, u32[]{:S(2)}, u32[]{:S(2)}) %collective-permute-start.3) | collective-permute-done | bytes 98336 | tf_op jit(solution)/shard_map/ppermute | solution.py:42
  21.5 8.9 %shard_map.68 = (f32[10,32,128]{2,1,0:T(8,128)S(1)}, bf16[1440,256]{1,0:T(8,128)(2,1)S(1)}, bf16[2880,128]{1,0:T(8,128)(2,1)S(1)}) custom-call(bf16[960,1440]{1,0:T(8,128)(2,1)S(1)} %get-tuple-element.36.refs_0_, bf16[960,1440]{1,0:T(8,128)(2,1)S(1)} %get-tuple-element.41.refs_1_, bf16[960,1440]{1,0:T(8,128)(2,1)S(1)} %get-tuple-element.43.refs_2_, ...), custom_call_target="tpu_custom_call" | custom-call | flops 4246732800 | bytes 1048576 | tf_op jit(solution)/shard_map/pallas_call | solution.py:365
  30.3 1.6 %shard_map.70 = (f32[5,32,128]{2,1,0:T(8,128)S(1)}, f32[5,32,128]{2,1,0:T(8,128)S(1)}, f32[5,32,128]{2,1,0:T(8,128)S(1)}, f32[32,128]{1,0:T(8,128)S(1)}) custom-call(bf16[960,1440]{1,0:T(8,128)(2,1)S(1)} %get-tuple-element.36.refs_0_, bf16[960,1440]{1,0:T(8,128)(2,1)S(1)} %get-tuple-element.41.refs_1_, bf16[960,1440]{1,0:T(8,128)(2,1)S(1)} %get-tuple-element.43.refs_2_, ...), custom_call_target="tpu_custom_call" | custom-call | flops 530841600 | bytes 1048576 | tf_op jit(solution)/shard_map/pallas_call | solution.py:365
  31.9 0.1 collective-permute-start.8
  32.0 0.5 collective-permute-start.9
  32.5 1.5 %collective-permute-start.6 = (f32[10,32,128]{2,1,0:T(8,128)S(1)}, f32[10,32,128]{2,1,0:T(8,128)S(1)}, u32[]{:S(2)}, u32[]{:S(2)}) collective-permute-start(f32[10,32,128]{2,1,0:T(8,128)S(1)} %get-tuple-element.53.refs_1_), channel_id=1, source_target_pairs={{0,16},{1,17},{2,18},{3,19},{4,20},{5,21},{6,22},{7,23},{8,24},{9,... | collective-permute-start | bytes 491528 | tf_op jit(solution)/shard_map/ppermute | solution.py:42
  34.0 1.6 %shard_map.69 = (f32[10,32,128]{2,1,0:T(8,128)S(1)}, f32[10,32,128]{2,1,0:T(8,128)S(1)}) custom-call(bf16[960,1440]{1,0:T(8,128)(2,1)S(1)} %get-tuple-element.36.refs_0_, bf16[960,1440]{1,0:T(8,128)(2,1)S(1)} %get-tuple-element.41.refs_1_, bf16[960,1440]{1,0:T(8,128)(2,1)S(1)} %get-tuple-element.43.refs_2_, bf16[1440,256]{1,0:T(8,128)(2,1)S(1)} %get-tuple-element.50.refs_3_, ...), custom_call_target="tpu_custom_call" | custom-call | flops 530841600 | bytes 1048576 | tf_op jit(solution)/shard_map/pallas_call | solution.py:365
  35.7 1.0 %collective-permute-start.5 = (f32[10,32,128]{2,1,0:T(8,128)S(1)}, f32[10,32,128]{2,1,0:T(8,128)S(1)}, u32[]{:S(2)}, u32[]{:S(2)}) collective-permute-start(f32[10,32,128]{2,1,0:T(8,128)S(1)} %get-tuple-element.52.refs_0_), channel_id=1, source_target_pairs={{0,28},{1,29},{2,30},{3,31},{4,16},{5,17},{6,18},{7,19},{8,20},{9,... | collective-permute-start | bytes 491528 | tf_op jit(solution)/shard_map/ppermute | solution.py:42
  36.7 0.8 %collective-permute-start.7 = (f32[10,32,128]{2,1,0:T(8,128)S(1)}, f32[10,32,128]{2,1,0:T(8,128)S(1)}, u32[]{:S(2)}, u32[]{:S(2)}) collective-permute-start(f32[10,32,128]{2,1,0:T(8,128)S(1)} %get-tuple-element.54.refs_2_), channel_id=1, source_target_pairs={{0,20},{1,21},{2,22},{3,23},{4,24},{5,25},{6,26},{7,27},{8,28},{9,... | collective-permute-start | bytes 491528 | tf_op jit(solution)/shard_map/ppermute | solution.py:42
  37.5 0.9 %turned_tiles.1 = (f32[45,32,128]{2,1,0:T(8,128)S(1)}, f32[9,32,128]{2,1,0:T(8,128)S(1)}, f32[9,32,128]{2,1,0:T(8,128)S(1)}) custom-call(f32[10,32,128]{2,1,0:T(8,128)S(1)} %get-tuple-element.52.refs_0_, f32[10,32,128]{2,1,0:T(8,128)S(1)} %get-tuple-element.53.refs_1_, f32[10,32,128]{2,1,0:T(8,128)S(1)} %get-tuple-element.54.refs_2_, ...), custom_call_target="tpu_custom_call" | custom-call | flops 1048576 | bytes 2097152 | tf_op jit(solution)/shard_map/turned_tiles/pallas_call | solution.py:448
  38.4 0.0 collective-permute-done.8.refs_3_
  38.4 0.1 collective-permute-start.10
  38.5 0.0 collective-permute-done.9.refs_5_
  38.5 3.8 %collective-permute-start.11 = (f32[9,32,128]{2,1,0:T(8,128)S(1)}, f32[9,32,128]{2,1,0:T(8,128)S(1)}, u32[]{:S(2)}, u32[]{:S(2)}) collective-permute-start(f32[9,32,128]{2,1,0:T(8,128)S(1)} %get-tuple-element.63), channel_id=1, source_target_pairs={{0,3},{1,0},{2,1},{3,2},{4,7},{5,4},{6,5},{7,6},{8,11},{9,8},{10,9... | collective-permute-start | bytes 442376 | tf_op jit(solution)/shard_map/ppermute | solution.py:42
  42.3 3.8 %collective-permute-done.10.refs_6_ = f32[9,32,128]{2,1,0:T(8,128)S(1)} collective-permute-done((f32[9,32,128]{2,1,0:T(8,128)S(1)}, f32[9,32,128]{2,1,0:T(8,128)S(1)}, u32[]{:S(2)}, u32[]{:S(2)}) %collective-permute-start.10) | collective-permute-done | bytes 147488 | tf_op jit(solution)/shard_map/ppermute | solution.py:42
  46.1 0.7 %collective-permute-done.11.refs_7_ = f32[9,32,128]{2,1,0:T(8,128)S(1)} collective-permute-done((f32[9,32,128]{2,1,0:T(8,128)S(1)}, f32[9,32,128]{2,1,0:T(8,128)S(1)}, u32[]{:S(2)}, u32[]{:S(2)}) %collective-permute-start.11) | collective-permute-done | bytes 147488 | tf_op jit(solution)/shard_map/ppermute | solution.py:42
  46.9 0.0 collective-permute-done.6.refs_1_
  46.9 0.0 collective-permute-done.5.refs_0_
  46.9 0.0 collective-permute-done.7.refs_2_
  46.9 0.2 edge_sums.1
  47.1 3.3 %collective-permute-start.12 = (f32[48,128]{1,0:T(8,128)S(1)}, f32[48,128]{1,0:T(8,128)S(1)}, u32[]{:S(2)}, u32[]{:S(2)}) collective-permute-start(f32[48,128]{1,0:T(8,128)S(1)} %get-tuple-element.64), channel_id=1, source_target_pairs={{0,3},{1,0},{2,1},{3,2},{4,7},{5,4},{6,5},{7,6},{8,11},{9,8},{10,9... | collective-permute-start | bytes 73736 | tf_op jit(solution)/shard_map/ppermute | solution.py:42
  50.4 0.0 collective-permute-start.13
  50.4 0.7 %slab_sums.1 = (f32[48,128]{1,0:T(8,128)S(1)}, f32[4,1024]{1,0:T(4,128)}) custom-call(f32[10,32,128]{2,1,0:T(8,128)S(1)} %collective-permute-done.5.refs_0_, f32[10,32,128]{2,1,0:T(8,128)S(1)} %collective-permute-done.6.refs_1_, f32[10,32,128]{2,1,0:T(8,128)S(1)} %collective-permute-done.7.refs_2_, f32[5,32,128]{2,1,0:T(8,128)S(1)} %collective-permute-done.8.refs_3_, ...), custom_call_target="tpu_custom_call" | custom-call | flops 1048576 | bytes 2097152 | tf_op jit(solution)/shard_map/slab_sums/pallas_call | solution.py:518
  51.1 0.8 %collective-permute-done.12.above_ref = f32[48,128]{1,0:T(8,128)S(1)} collective-permute-done((f32[48,128]{1,0:T(8,128)S(1)}, f32[48,128]{1,0:T(8,128)S(1)}, u32[]{:S(2)}, u32[]{:S(2)}) %collective-permute-start.12) | collective-permute-done | bytes 24608 | tf_op jit(solution)/shard_map/ppermute | solution.py:42
  51.9 4.1 %collective-permute-done.13.below_ref = f32[48,128]{1,0:T(8,128)S(1)} collective-permute-done((f32[48,128]{1,0:T(8,128)S(1)}, f32[48,128]{1,0:T(8,128)S(1)}, u32[]{:S(2)}, u32[]{:S(2)}) %collective-permute-start.13) | collective-permute-done | bytes 24608 | tf_op jit(solution)/shard_map/ppermute | solution.py:42
  56.0 0.8 %total_sums.1 = f32[4,45]{1,0:T(4,128)} custom-call(f32[48,128]{1,0:T(8,128)S(1)} %get-tuple-element.61.slab_ref, f32[48,128]{1,0:T(8,128)S(1)} %collective-permute-done.12.above_ref, f32[48,128]{1,0:T(8,128)S(1)} %collective-permute-done.13.below_ref), custom_call_target="tpu_custom_call" | custom-call | tf_op jit(solution)/shard_map/total_sums/pallas_call | solution.py:551
  (3 shorter events, 0.0 us)
Async XLA Ops:
  0.6 0.7 %copy-start = (f32[1,1,1,4,1024]{4,3,2,1,0:T(4,128)S(1)}, f32[1,1,1,4,1024]{4,3,2,1,0:T(4,128)}, u32[]{:S(2)}) copy-start(f32[1,1,1,4,1024]{4,3,2,1,0:T(4,128)} %param.5) | copy-start | bytes 49156
  1.5 7.4 %collective-permute-start.1 = (f32[32,128]{1,0:T(8,128)S(1)}, f32[32,128]{1,0:T(8,128)S(1)}, u32[]{:S(2)}, u32[]{:S(2)}) collective-permute-start(f32[32,128]{1,0:T(8,128)S(1)} %own_tile.1.own_ref.refs_8_.refs_5_), channel_id=1, source_target_pairs={{0,3},{1,0},{2,1},{3,2},{4,7},{5,4},{6,5},{7,6},{8,11},{9,8},{10,9... | collective-permute-start | bytes 49160 | tf_op jit(solution)/shard_map/ppermute | solution.py:42
  6.6 5.5 %collective-permute-start = (f32[32,128]{1,0:T(8,128)S(1)}, f32[32,128]{1,0:T(8,128)S(1)}, u32[]{:S(2)}, u32[]{:S(2)}) collective-permute-start(f32[32,128]{1,0:T(8,128)S(1)} %own_tile.1.own_ref.refs_8_.refs_5_), channel_id=1, source_target_pairs={{0,1},{1,2},{2,3},{3,0},{4,5},{5,6},{6,7},{7,4},{8,9},{9,10},{10,1... | collective-permute-start | bytes 49160 | tf_op jit(solution)/shard_map/ppermute | solution.py:42
  12.1 4.1 %collective-permute-start.2 = (f32[3,32,128]{2,1,0:T(8,128)S(1)}, f32[3,32,128]{2,1,0:T(8,128)S(1)}, u32[]{:S(2)}, u32[]{:S(2)}) collective-permute-start(f32[3,32,128]{2,1,0:T(8,128)S(1)} %pad_maximum_fusion.2), channel_id=1, source_target_pairs={{0,16},{1,17},{2,18},{3,19},{4,20},{5,21},{6,22},{7,23},{8,24},{9,... | collective-permute-start | bytes 147464 | tf_op jit(solution)/shard_map/ppermute | solution.py:42
  16.2 3.8 %collective-permute-start.4 = (f32[2,3,32,128]{3,2,1,0:T(8,128)S(1)}, f32[2,3,32,128]{3,2,1,0:T(8,128)S(1)}, u32[]{:S(2)}, u32[]{:S(2)}) collective-permute-start(f32[2,3,32,128]{3,2,1,0:T(8,128)S(1)} %pad_maximum_fusion.1), channel_id=1, source_target_pairs={{0,12},{1,13},{2,14},{3,15},{4,0},{5,1},{6,2},{7,3},{8,4},{9,5},{1... | collective-permute-start | bytes 294920 | tf_op jit(solution)/shard_map/ppermute | solution.py:42
  16.3 5.1 %collective-permute-start.3 = (f32[2,3,32,128]{3,2,1,0:T(8,128)S(1)}, f32[2,3,32,128]{3,2,1,0:T(8,128)S(1)}, u32[]{:S(2)}, u32[]{:S(2)}) collective-permute-start(f32[2,3,32,128]{3,2,1,0:T(8,128)S(1)} %pad_maximum_fusion.1), channel_id=1, source_target_pairs={{0,4},{1,5},{2,6},{3,7},{4,8},{5,9},{6,10},{7,11},{8,12},{9,13},{1... | collective-permute-start | bytes 294920 | tf_op jit(solution)/shard_map/ppermute | solution.py:42
  31.9 6.5 %collective-permute-start.8 = (f32[5,32,128]{2,1,0:T(8,128)S(1)}, f32[5,32,128]{2,1,0:T(8,128)S(1)}, u32[]{:S(2)}, u32[]{:S(2)}) collective-permute-start(f32[5,32,128]{2,1,0:T(8,128)S(1)} %get-tuple-element.55.refs_3_), channel_id=1, source_target_pairs={{0,12},{1,13},{2,14},{3,15},{4,0},{5,1},{6,2},{7,3},{8,4},{9,5},{1... | collective-permute-start | bytes 245768 | tf_op jit(solution)/shard_map/ppermute | solution.py:42
  32.0 6.5 %collective-permute-start.9 = (f32[5,32,128]{2,1,0:T(8,128)S(1)}, f32[5,32,128]{2,1,0:T(8,128)S(1)}, u32[]{:S(2)}, u32[]{:S(2)}) collective-permute-start(f32[5,32,128]{2,1,0:T(8,128)S(1)} %get-tuple-element.57.refs_5_), channel_id=1, source_target_pairs={{0,4},{1,5},{2,6},{3,7},{4,8},{5,9},{6,10},{7,11},{8,12},{9,13},{1... | collective-permute-start | bytes 245768 | tf_op jit(solution)/shard_map/ppermute | solution.py:42
  32.5 14.4 %collective-permute-start.6 = (f32[10,32,128]{2,1,0:T(8,128)S(1)}, f32[10,32,128]{2,1,0:T(8,128)S(1)}, u32[]{:S(2)}, u32[]{:S(2)}) collective-permute-start(f32[10,32,128]{2,1,0:T(8,128)S(1)} %get-tuple-element.53.refs_1_), channel_id=1, source_target_pairs={{0,16},{1,17},{2,18},{3,19},{4,20},{5,21},{6,22},{7,23},{8,24},{9,... | collective-permute-start | bytes 491528 | tf_op jit(solution)/shard_map/ppermute | solution.py:42
  35.7 11.2 %collective-permute-start.5 = (f32[10,32,128]{2,1,0:T(8,128)S(1)}, f32[10,32,128]{2,1,0:T(8,128)S(1)}, u32[]{:S(2)}, u32[]{:S(2)}) collective-permute-start(f32[10,32,128]{2,1,0:T(8,128)S(1)} %get-tuple-element.52.refs_0_), channel_id=1, source_target_pairs={{0,28},{1,29},{2,30},{3,31},{4,16},{5,17},{6,18},{7,19},{8,20},{9,... | collective-permute-start | bytes 491528 | tf_op jit(solution)/shard_map/ppermute | solution.py:42
  36.7 10.2 %collective-permute-start.7 = (f32[10,32,128]{2,1,0:T(8,128)S(1)}, f32[10,32,128]{2,1,0:T(8,128)S(1)}, u32[]{:S(2)}, u32[]{:S(2)}) collective-permute-start(f32[10,32,128]{2,1,0:T(8,128)S(1)} %get-tuple-element.54.refs_2_), channel_id=1, source_target_pairs={{0,20},{1,21},{2,22},{3,23},{4,24},{5,25},{6,26},{7,27},{8,28},{9,... | collective-permute-start | bytes 491528 | tf_op jit(solution)/shard_map/ppermute | solution.py:42
  38.4 7.7 %collective-permute-start.10 = (f32[9,32,128]{2,1,0:T(8,128)S(1)}, f32[9,32,128]{2,1,0:T(8,128)S(1)}, u32[]{:S(2)}, u32[]{:S(2)}) collective-permute-start(f32[9,32,128]{2,1,0:T(8,128)S(1)} %get-tuple-element.62), channel_id=1, source_target_pairs={{0,1},{1,2},{2,3},{3,0},{4,5},{5,6},{6,7},{7,4},{8,9},{9,10},{10,1... | collective-permute-start | bytes 442376 | tf_op jit(solution)/shard_map/ppermute | solution.py:42
  38.5 8.4 %collective-permute-start.11 = (f32[9,32,128]{2,1,0:T(8,128)S(1)}, f32[9,32,128]{2,1,0:T(8,128)S(1)}, u32[]{:S(2)}, u32[]{:S(2)}) collective-permute-start(f32[9,32,128]{2,1,0:T(8,128)S(1)} %get-tuple-element.63), channel_id=1, source_target_pairs={{0,3},{1,0},{2,1},{3,2},{4,7},{5,4},{6,5},{7,6},{8,11},{9,8},{10,9... | collective-permute-start | bytes 442376 | tf_op jit(solution)/shard_map/ppermute | solution.py:42
  47.1 4.8 %collective-permute-start.12 = (f32[48,128]{1,0:T(8,128)S(1)}, f32[48,128]{1,0:T(8,128)S(1)}, u32[]{:S(2)}, u32[]{:S(2)}) collective-permute-start(f32[48,128]{1,0:T(8,128)S(1)} %get-tuple-element.64), channel_id=1, source_target_pairs={{0,3},{1,0},{2,1},{3,2},{4,7},{5,4},{6,5},{7,6},{8,11},{9,8},{10,9... | collective-permute-start | bytes 73736 | tf_op jit(solution)/shard_map/ppermute | solution.py:42
  50.4 5.6 %collective-permute-start.13 = (f32[48,128]{1,0:T(8,128)S(1)}, f32[48,128]{1,0:T(8,128)S(1)}, u32[]{:S(2)}, u32[]{:S(2)}) collective-permute-start(f32[48,128]{1,0:T(8,128)S(1)} %get-tuple-element.65), channel_id=1, source_target_pairs={{0,1},{1,2},{2,3},{3,0},{4,5},{5,6},{6,7},{7,4},{8,9},{9,10},{10,1... | collective-permute-start | bytes 73736 | tf_op jit(solution)/shard_map/ppermute | solution.py:42

commit v4 on v3

v4 whole, which is shorter than its diff:
```python
import functools

import jax
import jax.numpy as jnp
import numpy as np
from jax import lax
from jax.experimental import pallas as pl
from jax.experimental.pallas import tpu as pltpu
from jax.sharding import PartitionSpec as P


L2 = 32
WINDOW = 45
ITERS = 4
SPECIES = 4
DEPTH = 4
LANES = DEPTH * L2
ROWS = WINDOW * L2
CENTRE = WINDOW // 2
SUM_ROWS = 48
PACK_ROWS = L2 + 8
PIECES = 3
PIECE = WINDOW // PIECES
PIECE_ROWS = PIECE * L2
SPLIT_STEPS = 3
CHUNK = 15
MESH_AXES = ("gx", "gy", "gz")


bf16 = jnp.bfloat16
f32 = jnp.float32
MIB = 1 << 20


def shifted(x, shift):
    sizes = [lax.axis_size(axis) for axis in MESH_AXES]
    pairs = []
    for source in np.ndindex(*sizes):
        target = [(i + d) % n for i, d, n in zip(source, shift, sizes)]
        pairs.append(
            (int(np.ravel_multi_index(source, sizes)), int(np.ravel_multi_index(target, sizes)))
        )
    return lax.ppermute(x, MESH_AXES, pairs)


def in_vmem(count):
    return [pl.BlockSpec(memory_space=pltpu.VMEM)] * count


def in_hbm(x):
    return pltpu.with_memory_space_constraint(x, pltpu.HBM)


def halves(x):
    high = x.astype(bf16)
    return high, (x - high.astype(f32)).astype(bf16)


def lane_index(shape):
    return lax.broadcasted_iota(jnp.int32, shape, len(shape) - 1)


def tile_kernel(flat_ref, tile_ref):
    row = lax.broadcasted_iota(jnp.int32, (DEPTH, LANES), 0)
    diagonal = lane_index((DEPTH, LANES)) // L2 == row
    for j in range(L2 // DEPTH):
        part = flat_ref[:, j * LANES : (j + 1) * LANES]
        rolled = [part] + [pltpu.roll(part, m * L2, 1) for m in range(1, DEPTH)]
        for k in range(DEPTH):
            picked = jnp.zeros((DEPTH, LANES), f32)
            for m in range(DEPTH):
                picked = jnp.where(diagonal & (row == (m + k) % DEPTH), rolled[m], picked)
            a = j * DEPTH + k
            tile_ref[a : a + 1, :] = jnp.sum(picked, axis=0, keepdims=True)


def flat_kernel(tile_ref, flat_ref):
    row = lax.broadcasted_iota(jnp.int32, (DEPTH, LANES), 0)
    diagonal = lane_index((DEPTH, LANES)) // L2 == row
    for j in range(L2 // DEPTH):
        spread = []
        for k in range(DEPTH):
            a = j * DEPTH + k
            line = jnp.broadcast_to(tile_ref[a : a + 1, :], (DEPTH, LANES))
            spread.append(jnp.where(diagonal, line, 0.0))
        value = jnp.zeros((DEPTH, LANES), f32)
        for m in range(DEPTH):
            picked = jnp.zeros((DEPTH, LANES), f32)
            for k in range(DEPTH):
                picked = jnp.where(row == (k - m) % DEPTH, spread[k], picked)
            value = value + (picked if m == 0 else pltpu.roll(picked, m * L2, 1))
        flat_ref[:, j * LANES : (j + 1) * LANES] = value


def pack_kernel(flat_hbm, members_hbm, species_hbm, pack_ref, flat_ref, members_ref, species_ref, sems):
    moves = [(flat_hbm, flat_ref), (members_hbm, members_ref), (species_hbm, species_ref)]
    copies = [
        pltpu.make_async_copy(source, target, sems.at[i])
        for i, (source, target) in enumerate(moves)
    ]
    for copy in copies:
        copy.start()
    for copy in copies:
        copy.wait()
    tile_kernel(flat_ref, pack_ref)
    pack_ref[L2:, :] = jnp.full((PACK_ROWS - L2, LANES), -1.0, f32)
    pack_ref[L2 : L2 + DEPTH, :WINDOW] = members_ref[...].astype(f32)
    pack_ref[L2 + DEPTH : L2 + DEPTH + 1, :DEPTH] = species_ref[...].astype(f32)


def packed_own(flat, members, species):
    return pl.pallas_call(
        pack_kernel,
        out_shape=jax.ShapeDtypeStruct((PACK_ROWS, LANES), f32),
        in_specs=[pl.BlockSpec(memory_space=pltpu.HBM)] * 3,
        out_specs=in_vmem(1)[0],
        scratch_shapes=[
            pltpu.VMEM((DEPTH, L2 * L2), f32),
            pltpu.VMEM((DEPTH, WINDOW), jnp.int32),
            pltpu.VMEM((1, DEPTH), jnp.int32),
            pltpu.SemaphoreType.DMA((3,)),
        ],
        compiler_params=pltpu.CompilerParams(vmem_limit_bytes=4 * MIB),
        name="packed_own",
    )(in_hbm(flat), in_hbm(members), in_hbm(species))


def split_kernel(piece, structure_hbm, parts_ref, buffer, sems):
    step_rows = PIECE_ROWS // SPLIT_STEPS

    def fetch(step):
        rows = pl.ds(piece * PIECE_ROWS + step * step_rows, step_rows)
        return pltpu.make_async_copy(structure_hbm.at[rows, :], buffer.at[step], sems.at[step])

    for step in range(SPLIT_STEPS):
        fetch(step).start()
    half = L2 // 2
    for step in range(SPLIT_STEPS):
        fetch(step).wait()

        def half_cell(i, carry, step=step):
            source = pl.ds(pl.multiple_of(i * half, half), half)
            target = step * 2 * step_rows + i // 2 * 2 * L2 + i % 2 * half
            high, low = halves(buffer[step, source, :])
            parts_ref[pl.ds(pl.multiple_of(target, half), half), :] = high
            parts_ref[pl.ds(pl.multiple_of(target + L2, half), half), :] = low
            return carry

        lax.fori_loop(0, step_rows // half, half_cell, 0, unroll=2)


def split_piece(piece, structure):
    return pl.pallas_call(
        functools.partial(split_kernel, piece),
        out_shape=jax.ShapeDtypeStruct((2 * PIECE_ROWS, ROWS), bf16),
        in_specs=[pl.BlockSpec(memory_space=pltpu.HBM)],
        out_specs=in_vmem(1)[0],
        scratch_shapes=[
            pltpu.VMEM((SPLIT_STEPS, PIECE_ROWS // SPLIT_STEPS, ROWS), f32),
            pltpu.SemaphoreType.DMA((SPLIT_STEPS,)),
        ],
        compiler_params=pltpu.CompilerParams(vmem_limit_bytes=8 * MIB),
        cost_estimate=pl.CostEstimate(
            flops=MIB, bytes_accessed=4 * PIECE_ROWS * ROWS, transcendentals=0
        ),
        name="split_piece",
    )(in_hbm(structure))


def both_tiles(own, below, above):
    lane = lane_index(own.shape)
    return [own, jnp.where(lane < 2 * L2, above, below)]


def setup_kernel(own_ref, below_ref, above_ref, table_hbm, member_ref, delta_ref, tile_ref, *rest):
    table_ref, table_tile, sem = rest
    copy = pltpu.make_async_copy(table_hbm, table_ref, sem.at[0])
    copy.start()
    cells = lax.broadcasted_iota(jnp.int32, (WINDOW, LANES), 0).astype(f32)
    group = lane_index((WINDOW, LANES)) // L2
    sources = [[own_ref] * DEPTH, [above_ref, above_ref, below_ref, below_ref]]
    for half, refs in enumerate(sources):
        member = jnp.zeros((WINDOW, LANES), f32)
        for g, ref in enumerate(refs):
            found = (ref[L2 + g : L2 + g + 1, :] == cells).astype(f32)
            found = jnp.max(found, axis=1, keepdims=True)
            member = jnp.where(group == g, found, member)
        member_ref[:, half * LANES : (half + 1) * LANES] = member
    tiles = both_tiles(own_ref[:L2, :], below_ref[:L2, :], above_ref[:L2, :])
    for half, tile in enumerate(tiles):
        tile_ref[:, half * LANES : (half + 1) * LANES] = tile

    copy.wait()
    tile_kernel(table_ref, table_tile)
    table = table_tile[...]
    turns = [table] + [pltpu.roll(table, m * L2, 1) for m in range(1, SPECIES)]
    group = lane_index((L2, LANES)) // L2
    thin = lane_index((1, LANES))
    row = slice(L2 + DEPTH, L2 + DEPTH + 1)
    for half, refs in enumerate(sources):
        delta = jnp.zeros((L2, LANES), f32)
        for g, ref in enumerate(refs):
            kinds = jnp.max(jnp.where(thin == g, ref[row, :], -1.0), axis=1, keepdims=True)
            for kind in range(SPECIES):
                here = (group == g) & (kinds == kind)
                delta = jnp.where(here, turns[(g - kind) % SPECIES], delta)
        delta_ref[:, half * LANES : (half + 1) * LANES] = delta


def setup(own, below, above, table):
    return pl.pallas_call(
        setup_kernel,
        out_shape=(
            jax.ShapeDtypeStruct((WINDOW, 2 * LANES), f32),
            jax.ShapeDtypeStruct((L2, 2 * LANES), f32),
            jax.ShapeDtypeStruct((L2, 2 * LANES), f32),
        ),
        in_specs=in_vmem(3) + [pl.BlockSpec(memory_space=pltpu.HBM)],
        out_specs=tuple(in_vmem(3)),
        scratch_shapes=[
            pltpu.VMEM((SPECIES, L2 * L2), f32),
            pltpu.VMEM((L2, LANES), f32),
            pltpu.SemaphoreType.DMA((1,)),
        ],
        compiler_params=pltpu.CompilerParams(vmem_limit_bytes=4 * MIB),
        name="setup",
    )(own, below, above, in_hbm(table))


def four_products(product):
    parts = product.reshape(-1, 2, L2, 2 * LANES)
    high, low = parts[:, 0], parts[:, 1]
    return (high[..., :LANES] + high[..., LANES:]) + (low[..., :LANES] + low[..., LANES:])


def first_image_kernel(*refs):
    parts, (tile_ref, image_ref) = refs[:PIECES], refs[PIECES:]
    lane_tile = CENTRE * L2 // LANES * LANES
    before = CENTRE * L2 - lane_tile
    for half in range(2):
        lanes = slice(half * LANES, (half + 1) * LANES)
        right = jnp.concatenate(halves(tile_ref[:, lanes]), axis=1)
        right = jnp.concatenate(
            [
                jnp.zeros((before, 2 * LANES), bf16),
                right,
                jnp.zeros((LANES - before - L2, 2 * LANES), bf16),
            ],
            axis=0,
        )
        for piece, ref in enumerate(parts):
            left = ref[:, lane_tile : lane_tile + LANES]
            product = jnp.dot(left, right, preferred_element_type=f32)
            image_ref[piece * PIECE : (piece + 1) * PIECE, :, lanes] = four_products(product)


def first_images(parts, tile):
    return pl.pallas_call(
        first_image_kernel,
        out_shape=jax.ShapeDtypeStruct((WINDOW, L2, 2 * LANES), f32),
        in_specs=in_vmem(PIECES + 1),
        out_specs=in_vmem(1)[0],
        compiler_params=pltpu.CompilerParams(vmem_limit_bytes=8 * MIB),
        name="first_images",
    )(*parts, tile)


def site_blocks(tile):
    lane = lane_index((L2, LANES))
    masks = [(lane // L2 == s).astype(f32).astype(bf16) for s in range(DEPTH)]
    return jnp.concatenate([tile * mask for mask in masks], axis=0)


def moved(window, cell, half, image):
    blocks = jnp.concatenate([site_blocks(part) for part in halves(image)], axis=1)
    left = window[cell * 2 * L2 : (cell + 1) * 2 * L2, half * LANES : (half + 1) * LANES]
    return four_products(jnp.dot(left, blocks, preferred_element_type=f32))[0]


HIGH_AT = (1, 2)
LOW_AT = (0, 3)


def keep(column, place, half, value):
    rows = slice(place * L2, (place + 1) * L2)
    for at, part in zip((HIGH_AT[half], LOW_AT[half]), halves(value)):
        column[rows, at * LANES : (at + 1) * LANES] = part


def set_images(parts, cells, column, slot):
    high, low = [], []
    for cell in cells:
        ref, base = parts[cell // PIECE], cell % PIECE * 2 * L2
        high.append(ref[base : base + L2, :])
        low.append(ref[base + L2 : base + 2 * L2, :])
    high, low = jnp.concatenate(high, axis=0), jnp.concatenate(low, axis=0)
    own = jnp.dot(high, column[:, : 2 * LANES], preferred_element_type=f32)
    other = jnp.dot(high, column[:, 2 * LANES :], preferred_element_type=f32)
    both = jnp.dot(low, column[:, LANES : 3 * LANES], preferred_element_type=f32)
    shape = (len(cells), L2, LANES)
    image = own[:, :LANES] + own[:, LANES:] + both[:, :LANES]
    slot[: len(cells), :, :LANES] = image.reshape(shape)
    image = other[:, :LANES] + other[:, LANES:] + both[:, LANES:]
    slot[: len(cells), :, LANES:] = image.reshape(shape)


def window_tiles(near_ref, cell):
    dx, dy, dz = cell // 15, cell // 5 % 3, cell % 5 - 2
    dx = dx % near_ref.shape[1]
    own, below, above = (near_ref[dy, dx, i] for i in range(3))
    group = lane_index((L2, LANES)) // L2
    first, second = own, jnp.where(group < 2, above, below)
    if dz > 0:
        first = jnp.where(group < dz, above, own)
        second = jnp.where(group < dz, own, jnp.where(group < 2 + dz, above, below))
    elif dz < 0:
        first = jnp.where(group >= DEPTH + dz, below, own)
        second = jnp.where(group >= DEPTH + dz, own, jnp.where(group < 2 + dz, above, below))
    move = -dz % DEPTH * L2
    return [tile if move == 0 else pltpu.roll(tile, move, 1) for tile in (first, second)]


def sweep_over(parts, chunks, source, use_image, slots):
    for i, chunk in enumerate(chunks):
        set_images(parts, chunk, source, slots[i % 2])
        if i > 0:
            use_image(i - 1, slots[(i - 1) % 2])
    use_image(len(chunks) - 1, slots[(len(chunks) - 1) % 2])


def delta_blocks(tile):
    high, low = (site_blocks(part) for part in halves(tile))
    return jnp.concatenate(
        [
            jnp.concatenate([high, low], axis=1),
            jnp.concatenate([high, jnp.zeros_like(high)], axis=1),
        ],
        axis=0,
    )


def last_sweep(parts, column, window, tile_ref, delta_ref, stage, sent, local, tau_ref, slots, final):
    deltas = [delta_blocks(delta_ref[:, half * LANES : (half + 1) * LANES]) for half in range(2)]
    chunks = [[cell_of(ox, oy, oz) for ox, oy in group for oz in range(-2, 3)] for group in stage]
    group_of = lane_index((L2, LANES)) // L2

    def use_image(i, slot):
        count = len(chunks[i])
        values = []
        for half in range(2):
            lanes = slice(half * LANES, (half + 1) * LANES)
            for place, cell in enumerate(chunks[i]):
                value = moved(window, cell, half, slot[place, :, lanes])
                if cell == CENTRE:
                    value = value + tile_ref[:, lanes]
                    if half == 0:
                        tau_ref[...] = value
                rows = slice(place * L2, (place + 1) * L2)
                high, low = halves(value)
                final[half, rows, :LANES] = high
                final[half, rows, LANES:] = low
            product = jnp.dot(
                final[half, : count * L2, :], deltas[half], preferred_element_type=f32
            )
            product = product[:, :LANES] + product[:, LANES:]
            values.append(product.reshape(count, L2, LANES))
        local[i][...] = values[0]
        for place, cell in enumerate(chunks[i]):
            oz = cell % 5 - 2
            value = values[0][place]
            if oz > 0:
                value = jnp.where(group_of >= DEPTH - oz, values[1][place], value)
            elif oz < 0:
                value = jnp.where(group_of < -oz, values[1][place], value)
            if oz != 0:
                value = pltpu.roll(value, oz % DEPTH * L2, 1)
            sent[i][place] = value

    sweep_over(parts, chunks, column, use_image, slots)


def first_kernel(stage, *refs):
    parts, refs = refs[:PIECES], refs[PIECES:]
    image_ref, near_ref, member_ref, tile_ref, delta_ref = refs[:5]
    sent, local = refs[5 : 5 + len(stage)], refs[5 + len(stage) : 5 + 2 * len(stage)]
    column, window, other, slot_a, slot_b, final = refs[5 + 2 * len(stage) :]
    slots = (slot_a, slot_b)
    halves_lanes = [slice(half * LANES, (half + 1) * LANES) for half in range(2)]
    for cell in range(WINDOW):
        base = cell * 2 * L2
        for lanes, tile in zip(halves_lanes, window_tiles(near_ref, cell)):
            high, low = halves(tile * member_ref[cell : cell + 1, lanes])
            window[base : base + L2, lanes] = high
            window[base + L2 : base + 2 * L2, lanes] = low

    def update(target, cell, image):
        for half, lanes in enumerate(halves_lanes):
            value = moved(window, cell, half, image[:, lanes])
            if cell == CENTRE:
                value = value + tile_ref[:, lanes]
            keep(target, cell, half, value)

    full = [list(range(base, base + CHUNK)) for base in range(0, WINDOW, CHUNK)]
    source, target = (column, other) if ITERS % 2 == 0 else (other, column)
    for cell in range(WINDOW):
        update(source, cell, image_ref[cell])
    for _ in range(1, ITERS - 1):

        def use_image(i, slot, target=target):
            for place, cell in enumerate(full[i]):
                update(target, cell, slot[place])

        sweep_over(parts, full, source, use_image, slots)
        source, target = target, source
    last_sweep(
        parts, source, window, tile_ref, delta_ref, stage, sent, local, None, slots, final
    )


def next_kernel(stage, *refs):
    parts, refs = refs[:PIECES], refs[PIECES:]
    column, window, tile_ref, delta_ref = refs[:4]
    sent, local = refs[4 : 4 + len(stage)], refs[4 + len(stage) : 4 + 2 * len(stage)]
    rest = refs[4 + 2 * len(stage) :]
    tau_ref = rest[0] if len(rest) == 4 else None
    slot_a, slot_b, final = rest[-3:]
    last_sweep(
        parts,
        column,
        window,
        tile_ref,
        delta_ref,
        stage,
        sent,
        local,
        tau_ref,
        (slot_a, slot_b),
        final,
    )


def stage_call(kernel, stage, extra_outs, extra_scratch, operands, flops):
    longest = max(CHUNK, 5 * max(len(group) for group in stage))
    out_shape = [jax.ShapeDtypeStruct((5 * len(group), L2, LANES), f32) for group in stage] * 2
    out_shape += extra_outs
    return pl.pallas_call(
        functools.partial(kernel, stage),
        out_shape=tuple(out_shape),
        in_specs=in_vmem(len(operands)),
        out_specs=tuple(in_vmem(len(out_shape))),
        scratch_shapes=extra_scratch
        + [pltpu.VMEM((longest, L2, 2 * LANES), f32)] * 2
        + [pltpu.VMEM((2, longest * L2, 2 * LANES), bf16)],
        compiler_params=pltpu.CompilerParams(vmem_limit_bytes=24 * MIB),
        cost_estimate=pl.CostEstimate(flops=flops, bytes_accessed=MIB, transcendentals=0),
    )(*operands)


def first_stage(stage, parts, images, near, member, tile, delta):
    return stage_call(
        first_kernel,
        stage,
        [
            jax.ShapeDtypeStruct((ROWS, 4 * LANES), bf16),
            jax.ShapeDtypeStruct((2 * ROWS, 2 * LANES), bf16),
        ],
        [pltpu.VMEM((ROWS, 4 * LANES), bf16)],
        (*parts, images, near, member, tile, delta),
        2 * 6 * (ITERS - 2) * ROWS * ROWS * LANES,
    )


def next_stage(stage, parts, column, window, tile, delta):
    tau = [jax.ShapeDtypeStruct((L2, LANES), f32)]
    return stage_call(
        next_kernel,
        stage,
        tau if any((0, 0) in group for group in stage) else [],
        [],
        (*parts, column, window, tile, delta),
        2 * ROWS * ROWS * LANES,
    )


def find_tile(groups, refs, ox, oy, oz):
    for group, ref in zip(groups, refs):
        if (ox, oy) in group:
            return ref[group.index((ox, oy)) * 5 + oz + 2]
    raise ValueError("no tile")


def plane_offsets():
    return [(ox, oy) for ox in (-1, 0, 1) for oy in (-1, 0, 1)]


def cell_of(dx, dy, dz):
    return ((dx + 1) * 3 + dy + 1) * 5 + dz + 2


def turn_kernel(groups, *refs):
    own, out = refs[:-1], refs[-1]
    lane = lane_index((L2, LANES))

    def cell_tile(cell):
        cell = min(cell, WINDOW - 1)
        return find_tile(groups, own, cell // 15 - 1, cell // 5 % 3 - 1, cell % 5 - 2)

    for base in range(0, WINDOW, DEPTH):
        block = jnp.concatenate([cell_tile(base + k) for k in range(DEPTH)], axis=0)
        turned = block.T
        pieces = [turned[s * L2 : (s + 1) * L2] for s in range(DEPTH)]
        for k in range(min(DEPTH, WINDOW - base)):
            value = pieces[0] if k == 0 else pltpu.roll(pieces[0], (-k % DEPTH) * L2, 1)
            for s in range(1, DEPTH):
                move = (s - k) % DEPTH
                piece = pieces[s] if move == 0 else pltpu.roll(pieces[s], move * L2, 1)
                value = jnp.where(lane // L2 == s, piece, value)
            out[base + k] = value


def turned_tiles(groups, own):
    return pl.pallas_call(
        functools.partial(turn_kernel, groups),
        out_shape=jax.ShapeDtypeStruct((WINDOW, L2, LANES), f32),
        in_specs=in_vmem(len(own)),
        out_specs=in_vmem(1)[0],
        compiler_params=pltpu.CompilerParams(vmem_limit_bytes=8 * MIB),
        cost_estimate=pl.CostEstimate(flops=MIB, bytes_accessed=2 * MIB, transcendentals=0),
        name="turned_tiles",
    )(*own)


def add_rows(groups, got, turned_ref, sums):
    for group, ref in zip(groups, got):
        for place, (ox, oy) in enumerate(group):
            for oz in range(-2, 3):
                cell = cell_of(-ox, -oy, -oz)
                value = ref[place * 5 + oz + 2] * turned_ref[cell]
                sums[cell : cell + 1, :] = jnp.sum(value, axis=0, keepdims=True)


def near_kernel(groups, *refs):
    got = refs[: len(groups)]
    turned_ref, tau_ref, sums, flat_ref = refs[len(groups) :]
    flat_kernel(tau_ref, flat_ref)
    sums[...] = jnp.zeros_like(sums)
    add_rows(groups, got, turned_ref, sums)


def near_sums(groups, got, turned, tau):
    return pl.pallas_call(
        functools.partial(near_kernel, groups),
        out_shape=(
            jax.ShapeDtypeStruct((SUM_ROWS, LANES), f32),
            jax.ShapeDtypeStruct((DEPTH, L2 * L2), f32),
        ),
        in_specs=in_vmem(len(got) + 2),
        out_specs=tuple(in_vmem(2)),
        compiler_params=pltpu.CompilerParams(vmem_limit_bytes=8 * MIB),
        name="near_sums",
    )(*got, turned, tau)


def total_kernel(groups, *refs):
    got = refs[: len(groups)]
    turned_ref, near_ref, out_ref, rows = refs[len(groups) :]
    rows[...] = near_ref[...]
    add_rows(groups, got, turned_ref, rows)
    sums = rows[...]
    site = lax.broadcasted_iota(jnp.int32, (8, LANES), 0)
    pick = (lane_index((8, LANES)) // L2 == site).astype(f32).astype(bf16)
    high = sums.astype(bf16)
    rest = sums - high.astype(f32)
    middle = rest.astype(bf16)
    low = (rest - middle.astype(f32)).astype(bf16)
    total = lax.dot_general(
        pick,
        jnp.concatenate([high, middle, low], axis=0),
        (((1,), (1,)), ((), ())),
        preferred_element_type=f32,
    )
    total = (total[:, :SUM_ROWS] + total[:, SUM_ROWS : 2 * SUM_ROWS]) + total[:, 2 * SUM_ROWS :]
    out_ref[...] = total[:DEPTH, :WINDOW]


def total_sums(groups, got, turned, near):
    return pl.pallas_call(
        functools.partial(total_kernel, groups),
        out_shape=jax.ShapeDtypeStruct((DEPTH, WINDOW), f32),
        in_specs=in_vmem(len(got) + 2),
        out_specs=in_vmem(1)[0],
        scratch_shapes=[pltpu.VMEM((SUM_ROWS, LANES), f32)],
        compiler_params=pltpu.CompilerParams(vmem_limit_bytes=8 * MIB),
        name="total_sums",
    )(*got, turned, near)


def plane_offsets():
    return [(ox, oy) for ox in (-1, 0, 1) for oy in (-1, 0, 1)]


def cell_of(dx, dy, dz):
    return ((dx + 1) * 3 + dy + 1) * 5 + dz + 2


def plane_groups():
    counts = (lax.axis_size("gx"), lax.axis_size("gy"))
    groups = {}
    for ox, oy in plane_offsets():
        groups.setdefault((ox % counts[0], oy % counts[1]), []).append((ox, oy))
    return groups


def body(t_matrix, structure, species, members, delta_table):
    own = packed_own(
        t_matrix.reshape(DEPTH, L2 * L2),
        members.reshape(DEPTH, WINDOW),
        species.reshape(1, DEPTH),
    )
    structure = structure[0]

    below, above = shifted(own, (0, 0, 1)), shifted(own, (0, 0, -1))
    first = split_piece(0, structure)
    slabs = jnp.stack([own[:L2], below[:L2], above[:L2]])
    slabs, structure, first = lax.optimization_barrier((slabs, structure, first))
    if lax.axis_size("gx") == 2:
        sides = [shifted(slabs, (1, 0, 0)), slabs]
    else:
        sides = [shifted(slabs, (1, 0, 0)), slabs, shifted(slabs, (-1, 0, 0))]
    second = split_piece(1, structure)
    plane = jnp.stack(sides)
    plane, structure, second = lax.optimization_barrier((plane, structure, second))
    planes = [shifted(plane, (0, 1, 0)), plane, shifted(plane, (0, -1, 0))]
    third = split_piece(2, structure)
    member, delta, tile = setup(own, below, above, delta_table)
    parts = (first, second, third)
    images = first_images(parts, tile)
    near = jnp.stack(planes)

    table = plane_groups()
    stages = [
        [shift for shift in table if shift[0] != 0 and shift[1] == 0],
        [shift for shift in table if shift[0] != 0 and shift[1] != 0],
        [shift for shift in table if shift[0] == 0],
    ]
    got, local = {}, {}
    for number, stage in enumerate(stages):
        groups = [table[shift] for shift in stage]
        if number == 0:
            *tiles, column, window = first_stage(groups, parts, images, near, member, tile, delta)
        else:
            tiles = next_stage(groups, parts, column, window, tile, delta)
        if (0, 0) in stage:
            tau = tiles[-1]
        local.update(zip(stage, tiles[len(stage) :]))
        for shift, block in zip(stage, tiles):
            got[shift] = block if shift == (0, 0) else shifted(block, shift + (0,))
    shifts = list(table)
    turned = turned_tiles([table[shift] for shift in shifts], [local[shift] for shift in shifts])
    close = stages[2]
    near_rows, site_tau = near_sums(
        [table[shift] for shift in close], [got[shift] for shift in close], turned, tau
    )
    far = stages[0] + stages[1]
    pairs = total_sums(
        [table[shift] for shift in far], [got[shift] for shift in far], turned, near_rows
    )
    return (
        site_tau.reshape(1, 1, 1, DEPTH, L2 * L2),
        pairs.reshape(1, 1, DEPTH, WINDOW),
    )


def solution(mesh):
    placed = (
        P(None, "gx", "gy", "gz", None),
        P(),
        P("gx", "gy", "gz"),
        P("gx", "gy", "gz", None),
        P(),
    )
    return jax.shard_map(
        body,
        mesh=mesh,
        in_specs=placed,
        out_specs=(P(None, "gx", "gy", "gz", None), P("gx", "gy", "gz", None)),
        check_vma=False,
    )
```

time: 57.2 us -> 50.6 us (0.88)
  starting transfers between devices: 18.2 us -> 11.7 us
  Pallas kernels: 22.7 us -> 28.5 us
  waiting for transfers between devices: 14.5 us -> 9.23 us
  local copies, waits for them, and re-layouts: 0.71 us -> 0.01 us
    ppermute x14 -> x10, starting transfers between devices: 18.2 us -> 11.7 us  [shifted(): return lax.ppermute(x, MESH_AXES, pairs)]
    pallas_call x3, Pallas kernels: 12.1 us -> 17.3 us  [stage_call(): pl.pallas_call(functools.partial(kernel, stage), out_shape=tuple(out_shap...]
    ppermute x14 -> x10, waiting for transfers between devices: 14.5 us -> 9.23 us  [shifted(): return lax.ppermute(x, MESH_AXES, pairs)]
    unnamed x2 -> x0, local copies, waits for them, and re-layouts: 0.71 us -> none
    pallas_call x9, Pallas kernels: 10.6 us -> 11.2 us  [the longest x3 5.98 us: split_piece(): pl.pallas_call(functools.partial(split_kernel, piece), out_shape=jax.Shap...]
  transfers between devices with their start and end apart: 14 -> 10, of which waited for: 7 -> 5; matrix products, arithmetic and copies ran while one was open for 0% -> 0% of each run, Pallas kernels for 19% -> 29%
where the time goes in v4:
time: 50.6 us; the launch traced here: 50.3 us
  Pallas kernels  28.5 us (56%)
  starting transfers between devices  11.7 us (23%)
  waiting for transfers between devices  9.23 us (18%)
  between operations  0.74 us (1%)
    pallas_call x3, Pallas kernels, stage_call(): pl.pallas_call(functools.partial(kernel, stage), out_shape=tuple(out_shap...  17.3 us
    ppermute x10, starting transfers between devices, shifted(): return lax.ppermute(x, MESH_AXES, pairs)  11.7 us
    ppermute x10, waiting for transfers between devices, shifted(): return lax.ppermute(x, MESH_AXES, pairs)  9.23 us
    pallas_call x3, Pallas kernels, split_piece(): pl.pallas_call(functools.partial(split_kernel, piece), out_shape=jax.Shap...  5.98 us
  transfers between devices with their start and end apart: 10, of which 5 were waited for; matrix products, arithmetic and copies ran while one was open for 0% of the time, Pallas kernels for 29%

profile of v4, /device:TPU:0, one launch (start us, length us, event | category | flops | bytes accessed | tf_op | source)
XLA Modules:
  0.0 50.3 jit_solution(17373923355945582840)
XLA Ops:
  0.6 0.9 %packed_own.1.own_ref = f32[40,128]{1,0:T(8,128)S(1)} custom-call(f32[4,1024]{1,0:T(4,128)} %bitcast.25, s32[4,45]{1,0:T(4,128)} %bitcast.27, s32[1,4]{1,0:T(1,128)} %bitcast.28), custom_call_target="tpu_custom_call" | custom-call | tf_op jit(solution)/shard_map/packed_own/pallas_call | solution.py:112
  1.5 5.1 %collective-permute-start.1 = (f32[40,128]{1,0:T(8,128)S(1)}, f32[40,128]{1,0:T(8,128)S(1)}, u32[]{:S(2)}, u32[]{:S(2)}) collective-permute-start(f32[40,128]{1,0:T(8,128)S(1)} %packed_own.1.own_ref), channel_id=1, source_target_pairs={{0,3},{1,0},{2,1},{3,2},{4,7},{5,4},{6,5},{7,6},{8,11},{9,8},{10,9... | collective-permute-start | bytes 61448 | tf_op jit(solution)/shard_map/ppermute | solution.py:43
  6.6 0.0 collective-permute-start
  6.6 2.0 %split_piece.3.refs_0_ = bf16[960,1440]{1,0:T(8,128)(2,1)S(1)} custom-call(f32[1440,1440]{1,0:T(8,128)} %bitcast.17), custom_call_target="tpu_custom_call" | custom-call | flops 1048576 | bytes 2764800 | tf_op jit(solution)/shard_map/split_piece/pallas_call | solution.py:153
  8.6 0.0 collective-permute-done.1.above_ref
  8.7 3.6 %collective-permute-done.below_ref = f32[40,128]{1,0:T(8,128)S(1)} collective-permute-done((f32[40,128]{1,0:T(8,128)S(1)}, f32[40,128]{1,0:T(8,128)S(1)}, u32[]{:S(2)}, u32[]{:S(2)}) %collective-permute-start) | collective-permute-done | bytes 20512 | tf_op jit(solution)/shard_map/ppermute | solution.py:43
  12.2 1.5 %collective-permute-start.2 = (f32[3,32,128]{2,1,0:T(8,128)S(1)}, f32[3,32,128]{2,1,0:T(8,128)S(1)}, u32[]{:S(2)}, u32[]{:S(2)}) collective-permute-start(f32[3,32,128]{2,1,0:T(8,128)S(1)} %pad_maximum_fusion.2), channel_id=1, source_target_pairs={{0,16},{1,17},{2,18},{3,19},{4,20},{5,21},{6,22},{7,23},{8,24},{9,... | collective-permute-start | bytes 147464 | tf_op jit(solution)/shard_map/ppermute | solution.py:43
  13.8 2.0 %split_piece.4.refs_1_ = bf16[960,1440]{1,0:T(8,128)(2,1)S(1)} custom-call(f32[1440,1440]{1,0:T(8,128)} %bitcast.18), custom_call_target="tpu_custom_call" | custom-call | flops 1048576 | bytes 2764800 | tf_op jit(solution)/shard_map/split_piece/pallas_call | solution.py:153
  15.8 0.6 %collective-permute-done.2 = f32[3,32,128]{2,1,0:T(8,128)S(1)} collective-permute-done((f32[3,32,128]{2,1,0:T(8,128)S(1)}, f32[3,32,128]{2,1,0:T(8,128)S(1)}, u32[]{:S(2)}, u32[]{:S(2)}) %collective-permute-start.2) | collective-permute-done | bytes 49184 | tf_op jit(solution)/shard_map/ppermute | solution.py:43
  16.4 0.1 collective-permute-start.4
  16.5 0.5 collective-permute-start.3
  17.0 0.9 %setup.1 = (f32[45,256]{1,0:T(8,128)S(1)}, f32[32,256]{1,0:T(8,128)S(1)}, f32[32,256]{1,0:T(8,128)S(1)}) custom-call(f32[40,128]{1,0:T(8,128)S(1)} %packed_own.1.own_ref, f32[40,128]{1,0:T(8,128)S(1)} %collective-permute-done.below_ref, f32[40,128]{1,0:T(8,128)S(1)} %collective-permute-done.1.above_ref, f32[4,1024]{1,0:T(4,128)} %table_hbm.1), custom_call_target="tpu_custom_call" | custom-call | tf_op jit(solution)/shard_map/setup/pallas_call | solution.py:211
  17.9 2.0 %split_piece.5.refs_2_ = bf16[960,1440]{1,0:T(8,128)(2,1)S(1)} custom-call(f32[1440,1440]{1,0:T(8,128)} %bitcast.19), custom_call_target="tpu_custom_call" | custom-call | flops 1048576 | bytes 2764800 | tf_op jit(solution)/shard_map/split_piece/pallas_call | solution.py:153
  19.9 0.9 %first_images.1.refs_3_ = f32[45,32,256]{2,1,0:T(8,128)S(1)} custom-call(bf16[960,1440]{1,0:T(8,128)(2,1)S(1)} %split_piece.3.refs_0_, bf16[960,1440]{1,0:T(8,128)(2,1)S(1)} %split_piece.4.refs_1_, bf16[960,1440]{1,0:T(8,128)(2,1)S(1)} %split_piece.5.refs_2_, f32[32,256]{1,0:T(8,128)S(1)} %get-tuple-element.33.refs_3_.refs_6_.refs_5_), custom_call_target="tpu_custom_call" | custom-call | tf_op jit(solution)/shard_map/first_images/pallas_call | solution.py:258
  20.8 0.0 collective-permute-done.4
  20.8 0.8 %collective-permute-done.3 = f32[2,3,32,128]{3,2,1,0:T(8,128)S(1)} collective-permute-done((f32[2,3,32,128]{3,2,1,0:T(8,128)S(1)}, f32[2,3,32,128]{3,2,1,0:T(8,128)S(1)}, u32[]{:S(2)}, u32[]{:S(2)}) %collective-permute-start.3) | collective-permute-done | bytes 98336 | tf_op jit(solution)/shard_map/ppermute | solution.py:43
  21.6 12.2 %shard_map.68 = (f32[10,32,128]{2,1,0:T(8,128)S(1)}, f32[10,32,128]{2,1,0:T(8,128)S(1)}, bf16[1440,512]{1,0:T(8,128)(2,1)S(1)}, bf16[2880,256]{1,0:T(8,128)(2,1)S(1)}) custom-call(bf16[960,1440]{1,0:T(8,128)(2,1)S(1)} %split_piece.3.refs_0_, bf16[960,1440]{1,0:T(8,128)(2,1)S(1)} %split_piece.4.refs_1_, bf16[960,1440]{1,0:T(8,128)(2,1)S(1)} %split_piece.5.refs_2_, ...), custom_call_target="tpu_custom_call" | custom-call | flops 6370099200 | bytes 1048576 | tf_op jit(solution)/shard_map/pallas_call | solution.py:446
  33.9 1.5 %collective-permute-start.7 = (f32[10,32,128]{2,1,0:T(8,128)S(1)}, f32[10,32,128]{2,1,0:T(8,128)S(1)}, u32[]{:S(2)}, u32[]{:S(2)}) collective-permute-start(f32[10,32,128]{2,1,0:T(8,128)S(1)} %get-tuple-element.50), channel_id=1, source_target_pairs={{0,16},{1,17},{2,18},{3,19},{4,20},{5,21},{6,22},{7,23},{8,24},{9,... | collective-permute-start | bytes 491528 | tf_op jit(solution)/shard_map/ppermute | solution.py:43
  35.4 2.8 %shard_map.70 = (f32[10,32,128]{2,1,0:T(8,128)S(1)}, f32[10,32,128]{2,1,0:T(8,128)S(1)}, f32[10,32,128]{2,1,0:T(8,128)S(1)}, f32[10,32,128]{2,1,0:T(8,128)S(1)}) custom-call(bf16[960,1440]{1,0:T(8,128)(2,1)S(1)} %split_piece.3.refs_0_, bf16[960,1440]{1,0:T(8,128)(2,1)S(1)} %split_piece.4.refs_1_, bf16[960,1440]{1,0:T(8,128)(2,1)S(1)} %split_piece.5.refs_2_, ...), custom_call_target="tpu_custom_call" | custom-call | flops 530841600 | bytes 1048576 | tf_op jit(solution)/shard_map/pallas_call | solution.py:446
  38.2 0.3 collective-permute-start.8
  38.4 1.5 %collective-permute-start.9 = (f32[10,32,128]{2,1,0:T(8,128)S(1)}, f32[10,32,128]{2,1,0:T(8,128)S(1)}, u32[]{:S(2)}, u32[]{:S(2)}) collective-permute-start(f32[10,32,128]{2,1,0:T(8,128)S(1)} %get-tuple-element.52), channel_id=1, source_target_pairs={{0,20},{1,21},{2,22},{3,23},{4,24},{5,25},{6,26},{7,27},{8,28},{9,... | collective-permute-start | bytes 491528 | tf_op jit(solution)/shard_map/ppermute | solution.py:43
  40.0 2.3 %shard_map.69 = (f32[5,32,128]{2,1,0:T(8,128)S(1)}, f32[5,32,128]{2,1,0:T(8,128)S(1)}, f32[5,32,128]{2,1,0:T(8,128)S(1)}, f32[5,32,128]{2,1,0:T(8,128)S(1)}, f32...) custom-call(bf16[960,1440]{1,0:T(8,128)(2,1)S(1)} %split_piece.3.refs_0_, ...), custom_call_target="tpu_custom_call" | custom-call | flops 530841600 | bytes 1048576 | tf_op jit(solution)/shard_map/pallas_call | solution.py:446
  42.3 1.2 %collective-permute-start.5 = (f32[5,32,128]{2,1,0:T(8,128)S(1)}, f32[5,32,128]{2,1,0:T(8,128)S(1)}, u32[]{:S(2)}, u32[]{:S(2)}) collective-permute-start(f32[5,32,128]{2,1,0:T(8,128)S(1)} %get-tuple-element.39), channel_id=1, source_target_pairs={{0,12},{1,13},{2,14},{3,15},{4,0},{5,1},{6,2},{7,3},{8,4},{9,5},{1... | collective-permute-start | bytes 245768 | tf_op jit(solution)/shard_map/ppermute | solution.py:43
  43.5 0.0 collective-permute-start.6
  43.5 0.9 %turned_tiles.1.refs_3_ = f32[45,32,128]{2,1,0:T(8,128)S(1)} custom-call(f32[10,32,128]{2,1,0:T(8,128)S(1)} %get-tuple-element.42.refs_0_, f32[10,32,128]{2,1,0:T(8,128)S(1)} %get-tuple-element.43.refs_1_, f32[10,32,128]{2,1,0:T(8,128)S(1)} %get-tuple-element.44.refs_2_, f32[5,32,128]{2,1,0:T(8,128)S(1)} %get-tuple-element.45.refs_3_, ...), custom_call_target="tpu_custom_call" | custom-call | flops 1048576 | bytes 2097152 | tf_op jit(solution)/shard_map/turned_tiles/pallas_call | solution.py:522
  44.4 2.3 %collective-permute-done.5.refs_0_ = f32[5,32,128]{2,1,0:T(8,128)S(1)} collective-permute-done((f32[5,32,128]{2,1,0:T(8,128)S(1)}, f32[5,32,128]{2,1,0:T(8,128)S(1)}, u32[]{:S(2)}, u32[]{:S(2)}) %collective-permute-start.5) | collective-permute-done | bytes 81952 | tf_op jit(solution)/shard_map/ppermute | solution.py:43
  46.6 2.0 %collective-permute-done.6.refs_2_ = f32[5,32,128]{2,1,0:T(8,128)S(1)} collective-permute-done((f32[5,32,128]{2,1,0:T(8,128)S(1)}, f32[5,32,128]{2,1,0:T(8,128)S(1)}, u32[]{:S(2)}, u32[]{:S(2)}) %collective-permute-start.6) | collective-permute-done | bytes 81952 | tf_op jit(solution)/shard_map/ppermute | solution.py:43
  48.7 0.7 %near_sums.1 = (f32[48,128]{1,0:T(8,128)S(1)}, f32[4,1024]{1,0:T(4,128)}) custom-call(f32[5,32,128]{2,1,0:T(8,128)S(1)} %collective-permute-done.5.refs_0_, f32[5,32,128]{2,1,0:T(8,128)S(1)} %get-tuple-element.40.refs_1_, f32[5,32,128]{2,1,0:T(8,128)S(1)} %collective-permute-done.6.refs_2_, f32[45,32,128]{2,1,0:T(8,128)S(1)} %turned_tiles.1.refs_3_, ...), custom_call_target="tpu_custom_call" | custom-call | tf_op jit(solution)/shard_map/near_sums/pallas_call | solution.py:551
  49.4 0.0 collective-permute-done.7.refs_0_
  49.4 0.0 collective-permute-done.8.refs_1_
  49.4 0.0 collective-permute-done.9.refs_2_
  49.4 0.9 %total_sums.1 = f32[4,45]{1,0:T(4,128)} custom-call(f32[10,32,128]{2,1,0:T(8,128)S(1)} %collective-permute-done.7.refs_0_, f32[10,32,128]{2,1,0:T(8,128)S(1)} %collective-permute-done.8.refs_1_, f32[10,32,128]{2,1,0:T(8,128)S(1)} %collective-permute-done.9.refs_2_, f32[45,32,128]{2,1,0:T(8,128)S(1)} %turned_tiles.1.refs_3_, ...), custom_call_target="tpu_custom_call" | custom-call | tf_op jit(solution)/shard_map/total_sums/pallas_call | solution.py:587
  (6 shorter events, 0.0 us)
Async XLA Ops:
  1.5 7.1 %collective-permute-start.1 = (f32[40,128]{1,0:T(8,128)S(1)}, f32[40,128]{1,0:T(8,128)S(1)}, u32[]{:S(2)}, u32[]{:S(2)}) collective-permute-start(f32[40,128]{1,0:T(8,128)S(1)} %packed_own.1.own_ref), channel_id=1, source_target_pairs={{0,3},{1,0},{2,1},{3,2},{4,7},{5,4},{6,5},{7,6},{8,11},{9,8},{10,9... | collective-permute-start | bytes 61448 | tf_op jit(solution)/shard_map/ppermute | solution.py:43
  6.6 5.6 %collective-permute-start = (f32[40,128]{1,0:T(8,128)S(1)}, f32[40,128]{1,0:T(8,128)S(1)}, u32[]{:S(2)}, u32[]{:S(2)}) collective-permute-start(f32[40,128]{1,0:T(8,128)S(1)} %packed_own.1.own_ref), channel_id=1, source_target_pairs={{0,1},{1,2},{2,3},{3,0},{4,5},{5,6},{6,7},{7,4},{8,9},{9,10},{10,1... | collective-permute-start | bytes 61448 | tf_op jit(solution)/shard_map/ppermute | solution.py:43
  12.2 4.1 %collective-permute-start.2 = (f32[3,32,128]{2,1,0:T(8,128)S(1)}, f32[3,32,128]{2,1,0:T(8,128)S(1)}, u32[]{:S(2)}, u32[]{:S(2)}) collective-permute-start(f32[3,32,128]{2,1,0:T(8,128)S(1)} %pad_maximum_fusion.2), channel_id=1, source_target_pairs={{0,16},{1,17},{2,18},{3,19},{4,20},{5,21},{6,22},{7,23},{8,24},{9,... | collective-permute-start | bytes 147464 | tf_op jit(solution)/shard_map/ppermute | solution.py:43
  16.4 4.4 %collective-permute-start.4 = (f32[2,3,32,128]{3,2,1,0:T(8,128)S(1)}, f32[2,3,32,128]{3,2,1,0:T(8,128)S(1)}, u32[]{:S(2)}, u32[]{:S(2)}) collective-permute-start(f32[2,3,32,128]{3,2,1,0:T(8,128)S(1)} %pad_maximum_fusion.1), channel_id=1, source_target_pairs={{0,12},{1,13},{2,14},{3,15},{4,0},{5,1},{6,2},{7,3},{8,4},{9,5},{1... | collective-permute-start | bytes 294920 | tf_op jit(solution)/shard_map/ppermute | solution.py:43
  16.5 5.1 %collective-permute-start.3 = (f32[2,3,32,128]{3,2,1,0:T(8,128)S(1)}, f32[2,3,32,128]{3,2,1,0:T(8,128)S(1)}, u32[]{:S(2)}, u32[]{:S(2)}) collective-permute-start(f32[2,3,32,128]{3,2,1,0:T(8,128)S(1)} %pad_maximum_fusion.1), channel_id=1, source_target_pairs={{0,4},{1,5},{2,6},{3,7},{4,8},{5,9},{6,10},{7,11},{8,12},{9,13},{1... | collective-permute-start | bytes 294920 | tf_op jit(solution)/shard_map/ppermute | solution.py:43
  33.9 15.5 %collective-permute-start.7 = (f32[10,32,128]{2,1,0:T(8,128)S(1)}, f32[10,32,128]{2,1,0:T(8,128)S(1)}, u32[]{:S(2)}, u32[]{:S(2)}) collective-permute-start(f32[10,32,128]{2,1,0:T(8,128)S(1)} %get-tuple-element.50), channel_id=1, source_target_pairs={{0,16},{1,17},{2,18},{3,19},{4,20},{5,21},{6,22},{7,23},{8,24},{9,... | collective-permute-start | bytes 491528 | tf_op jit(solution)/shard_map/ppermute | solution.py:43
  38.2 11.2 %collective-permute-start.8 = (f32[10,32,128]{2,1,0:T(8,128)S(1)}, f32[10,32,128]{2,1,0:T(8,128)S(1)}, u32[]{:S(2)}, u32[]{:S(2)}) collective-permute-start(f32[10,32,128]{2,1,0:T(8,128)S(1)} %get-tuple-element.51), channel_id=1, source_target_pairs={{0,28},{1,29},{2,30},{3,31},{4,16},{5,17},{6,18},{7,19},{8,20},{9,... | collective-permute-start | bytes 491528 | tf_op jit(solution)/shard_map/ppermute | solution.py:43
  38.4 10.9 %collective-permute-start.9 = (f32[10,32,128]{2,1,0:T(8,128)S(1)}, f32[10,32,128]{2,1,0:T(8,128)S(1)}, u32[]{:S(2)}, u32[]{:S(2)}) collective-permute-start(f32[10,32,128]{2,1,0:T(8,128)S(1)} %get-tuple-element.52), channel_id=1, source_target_pairs={{0,20},{1,21},{2,22},{3,23},{4,24},{5,25},{6,26},{7,27},{8,28},{9,... | collective-permute-start | bytes 491528 | tf_op jit(solution)/shard_map/ppermute | solution.py:43
  42.3 4.3 %collective-permute-start.5 = (f32[5,32,128]{2,1,0:T(8,128)S(1)}, f32[5,32,128]{2,1,0:T(8,128)S(1)}, u32[]{:S(2)}, u32[]{:S(2)}) collective-permute-start(f32[5,32,128]{2,1,0:T(8,128)S(1)} %get-tuple-element.39), channel_id=1, source_target_pairs={{0,12},{1,13},{2,14},{3,15},{4,0},{5,1},{6,2},{7,3},{8,4},{9,5},{1... | collective-permute-start | bytes 245768 | tf_op jit(solution)/shard_map/ppermute | solution.py:43
  43.5 5.2 %collective-permute-start.6 = (f32[5,32,128]{2,1,0:T(8,128)S(1)}, f32[5,32,128]{2,1,0:T(8,128)S(1)}, u32[]{:S(2)}, u32[]{:S(2)}) collective-permute-start(f32[5,32,128]{2,1,0:T(8,128)S(1)} %get-tuple-element.41), channel_id=1, source_target_pairs={{0,4},{1,5},{2,6},{3,7},{4,8},{5,9},{6,10},{7,11},{8,12},{9,13},{1... | collective-permute-start | bytes 245768 | tf_op jit(solution)/shard_map/ppermute | solution.py:43

commit v5 on v4

--- a/solution.py
+++ b/solution.py
@@ -304,10 +304,9 @@
     slot[: len(cells), :, LANES:] = image.reshape(shape)
 
 
-def window_tiles(near_ref, cell):
+def window_tiles(near, cell):
     dx, dy, dz = cell // 15, cell // 5 % 3, cell % 5 - 2
-    dx = dx % near_ref.shape[1]
-    own, below, above = (near_ref[dy, dx, i] for i in range(3))
+    own, below, above = (near(dx, dy, i) for i in range(3))
     group = lane_index((L2, LANES)) // L2
     first, second = own, jnp.where(group < 2, above, below)
     if dz > 0:
@@ -318,6 +317,52 @@
         second = jnp.where(group >= DEPTH + dz, own, jnp.where(group < 2 + dz, above, below))
     move = -dz % DEPTH * L2
     return [tile if move == 0 else pltpu.roll(tile, move, 1) for tile in (first, second)]
+
+
+def set_window(window, near, member_ref, cell):
+    base = cell * 2 * L2
+    for half, tile in enumerate(window_tiles(near, cell)):
+        lanes = slice(half * LANES, (half + 1) * LANES)
+        high, low = halves(tile * member_ref[cell : cell + 1, lanes])
+        window[base : base + L2, lanes] = high
+        window[base + L2 : base + 2 * L2, lanes] = low
+
+
+def set_column(column, window, tile_ref, cell, image):
+    for half in range(2):
+        lanes = slice(half * LANES, (half + 1) * LANES)
+        value = moved(window, cell, half, image[:, lanes])
+        if cell == CENTRE:
+            value = value + tile_ref[:, lanes]
+        keep(column, cell, half, value)
+
+
+def early_cells():
+    return [cell for cell in range(WINDOW) if cell // 5 % 3 == 1]
+
+
+def early_kernel(plane_ref, member_ref, tile_ref, image_ref, column, window):
+    def near(dx, dy, slab):
+        return plane_ref[dx % plane_ref.shape[0], slab]
+
+    for cell in early_cells():
+        set_window(window, near, member_ref, cell)
+    for cell in early_cells():
+        set_column(column, window, tile_ref, cell, image_ref[cell])
+
+
+def early_columns(plane, member, tile, images):
+    return pl.pallas_call(
+        early_kernel,
+        out_shape=(
+            jax.ShapeDtypeStruct((ROWS, 4 * LANES), bf16),
+            jax.ShapeDtypeStruct((2 * ROWS, 2 * LANES), bf16),
+        ),
+        in_specs=in_vmem(4),
+        out_specs=tuple(in_vmem(2)),
+        compiler_params=pltpu.CompilerParams(vmem_limit_bytes=8 * MIB),
+        name="early_columns",
+    )(plane, member, tile, images)
 
 
 def sweep_over(parts, chunks, source, use_image, slots):
@@ -381,39 +426,34 @@
 
 def first_kernel(stage, *refs):
     parts, refs = refs[:PIECES], refs[PIECES:]
-    image_ref, near_ref, member_ref, tile_ref, delta_ref = refs[:5]
-    sent, local = refs[5 : 5 + len(stage)], refs[5 + len(stage) : 5 + 2 * len(stage)]
-    column, window, other, slot_a, slot_b, final = refs[5 + 2 * len(stage) :]
+    _, _, image_ref, south_ref, north_ref, member_ref, tile_ref, delta_ref = refs[:8]
+    sent, local = refs[8 : 8 + len(stage)], refs[8 + len(stage) : 8 + 2 * len(stage)]
+    column, window, other, slot_a, slot_b, final = refs[8 + 2 * len(stage) :]
     slots = (slot_a, slot_b)
-    halves_lanes = [slice(half * LANES, (half + 1) * LANES) for half in range(2)]
-    for cell in range(WINDOW):
-        base = cell * 2 * L2
-        for lanes, tile in zip(halves_lanes, window_tiles(near_ref, cell)):
-            high, low = halves(tile * member_ref[cell : cell + 1, lanes])
-            window[base : base + L2, lanes] = high
-            window[base + L2 : base + 2 * L2, lanes] = low
-
-    def update(target, cell, image):
-        for half, lanes in enumerate(halves_lanes):
-            value = moved(window, cell, half, image[:, lanes])
-            if cell == CENTRE:
-                value = value + tile_ref[:, lanes]
-            keep(target, cell, half, value)
-
+
+    def near(dx, dy, slab):
+        ref = south_ref if dy == 0 else north_ref
+        return ref[dx % ref.shape[0], slab]
+
+    late = [cell for cell in range(WINDOW) if cell not in early_cells()]
+    for cell in late:
+        set_window(window, near, member_ref, cell)
+    for cell in late:
+        set_column(column, window, tile_ref, cell, image_ref[cell])
+    source, target = column, other
     full = [list(range(base, base + CHUNK)) for base in range(0, WINDOW, CHUNK)]
-    source, target = (column, other) if ITERS % 2 == 0 else (other, column)
-    for cell in range(WINDOW):
-        update(source, cell, image_ref[cell])
     for _ in range(1, ITERS - 1):
 
         def use_image(i, slot, target=target):
             for place, cell in enumerate(full[i]):
-                update(target, cell, slot[place])
+                set_column(target, window, tile_ref, cell, slot[place])
 
         sweep_over(parts, full, source, use_image, slots)
         source, target = target, source
+    if source is not column:
+        column[...] = source[...]
     last_sweep(
-        parts, source, window, tile_ref, delta_ref, stage, sent, local, None, slots, final
+        parts, column, window, tile_ref, delta_ref, stage, sent, local, None, slots, final
     )
 
 
@@ -439,7 +479,7 @@
     )
 
 
-def stage_call(kernel, stage, extra_outs, extra_scratch, operands, flops):
+def stage_call(kernel, stage, extra_outs, extra_scratch, operands, flops, aliases=()):
     longest = max(CHUNK, 5 * max(len(group) for group in stage))
     out_shape = [jax.ShapeDtypeStruct((5 * len(group), L2, LANES), f32) for group in stage] * 2
     out_shape += extra_outs
@@ -451,12 +491,15 @@
         scratch_shapes=extra_scratch
         + [pltpu.VMEM((longest, L2, 2 * LANES), f32)] * 2
         + [pltpu.VMEM((2, longest * L2, 2 * LANES), bf16)],
+        input_output_aliases={
+            operand: 2 * len(stage) + i for i, operand in enumerate(aliases)
+        },
         compiler_params=pltpu.CompilerParams(vmem_limit_bytes=24 * MIB),
         cost_estimate=pl.CostEstimate(flops=flops, bytes_accessed=MIB, transcendentals=0),
     )(*operands)
 
 
-def first_stage(stage, parts, images, near, member, tile, delta):
+def first_stage(stage, parts, column, window, images, south, north, member, tile, delta):
     return stage_call(
         first_kernel,
         stage,
@@ -465,8 +508,9 @@
             jax.ShapeDtypeStruct((2 * ROWS, 2 * LANES), bf16),
         ],
         [pltpu.VMEM((ROWS, 4 * LANES), bf16)],
-        (*parts, images, near, member, tile, delta),
+        (*parts, column, window, images, south, north, member, tile, delta),
         2 * 6 * (ITERS - 2) * ROWS * ROWS * LANES,
+        (PIECES, PIECES + 1),
     )
 
 
@@ -620,34 +664,36 @@
     structure = structure[0]
 
     below, above = shifted(own, (0, 0, 1)), shifted(own, (0, 0, -1))
-    first = split_piece(0, structure)
+    first, second = split_piece(0, structure), split_piece(1, structure)
     slabs = jnp.stack([own[:L2], below[:L2], above[:L2]])
-    slabs, structure, first = lax.optimization_barrier((slabs, structure, first))
+    slabs, structure, first, second = lax.optimization_barrier((slabs, structure, first, second))
     if lax.axis_size("gx") == 2:
         sides = [shifted(slabs, (1, 0, 0)), slabs]
     else:
         sides = [shifted(slabs, (1, 0, 0)), slabs, shifted(slabs, (-1, 0, 0))]
-    second = split_piece(1, structure)
+    prepared = setup(own, below, above, delta_table)
     plane = jnp.stack(sides)
-    plane, structure, second = lax.optimization_barrier((plane, structure, second))
-    planes = [shifted(plane, (0, 1, 0)), plane, shifted(plane, (0, -1, 0))]
-    third = split_piece(2, structure)
-    member, delta, tile = setup(own, below, above, delta_table)
-    parts = (first, second, third)
+    plane, structure, *prepared = lax.optimization_barrier((plane, structure, *prepared))
+    member, delta, tile = prepared
+    south, north = shifted(plane, (0, 1, 0)), shifted(plane, (0, -1, 0))
+    parts = (first, second, split_piece(2, structure))
     images = first_images(parts, tile)
-    near = jnp.stack(planes)
+    column, window = early_columns(plane, member, tile, images)
 
     table = plane_groups()
     stages = [
+        [shift for shift in table if shift[0] != 0 and shift[1] != 0],
         [shift for shift in table if shift[0] != 0 and shift[1] == 0],
-        [shift for shift in table if shift[0] != 0 and shift[1] != 0],
-        [shift for shift in table if shift[0] == 0],
+        [shift for shift in table if shift[0] == 0 and shift[1] != 0],
+        [(0, 0)],
     ]
     got, local = {}, {}
     for number, stage in enumerate(stages):
         groups = [table[shift] for shift in stage]
         if number == 0:
-            *tiles, column, window = first_stage(groups, parts, images, near, member, tile, delta)
+            *tiles, column, window = first_stage(
+                groups, parts, column, window, images, south, north, member, tile, delta
+            )
         else:
             tiles = next_stage(groups, parts, column, window, tile, delta)
         if (0, 0) in stage:
@@ -657,11 +703,8 @@
             got[shift] = block if shift == (0, 0) else shifted(block, shift + (0,))
     shifts = list(table)
     turned = turned_tiles([table[shift] for shift in shifts], [local[shift] for shift in shifts])
-    close = stages[2]
-    near_rows, site_tau = near_sums(
-        [table[shift] for shift in close], [got[shift] for shift in close], turned, tau
-    )
-    far = stages[0] + stages[1]
+    near_rows, site_tau = near_sums([table[0, 0]], [got[0, 0]], turned, tau)
+    far = [shift for shift in shifts if shift != (0, 0)]
     pairs = total_sums(
         [table[shift] for shift in far], [got[shift] for shift in far], turned, near_rows
     )

time: 50.6 us -> 48.8 us (0.964)
  waiting for transfers between devices: 9.23 us -> 7.45 us
    ppermute x10, waiting for transfers between devices: 9.23 us -> 7.45 us  [shifted(): return lax.ppermute(x, MESH_AXES, pairs)]
    pallas_call x0 -> x1, Pallas kernels: none -> 0.53 us  [early_columns(): pl.pallas_call(early_kernel, out_shape=(jax.ShapeDtypeStruct((ROWS, 4 * L...]
    pallas_call x3 -> x4, Pallas kernels: 17.3 us -> 17.1 us  [stage_call(): pl.pallas_call(functools.partial(kernel, stage), out_shape=tuple(out_shap...]
  transfers between devices with their start and end apart: 10 -> 10, of which waited for: 5 -> 5; matrix products, arithmetic and copies ran while one was open for 0% -> 0% of each run, Pallas kernels for 29% -> 30%
where the time goes in v5:
time: 48.8 us; the launch traced here: 48.4 us
  Pallas kernels  28.9 us (59%)
  starting transfers between devices  11.3 us (23%)
  waiting for transfers between devices  7.45 us (15%)
  between operations  0.74 us (2%)
    pallas_call x4, Pallas kernels, stage_call(): pl.pallas_call(functools.partial(kernel, stage), out_shape=tuple(out_shap...  17.1 us
    ppermute x10, starting transfers between devices, shifted(): return lax.ppermute(x, MESH_AXES, pairs)  11.3 us
    ppermute x10, waiting for transfers between devices, shifted(): return lax.ppermute(x, MESH_AXES, pairs)  7.45 us
    pallas_call x3, Pallas kernels, split_piece(): pl.pallas_call(functools.partial(split_kernel, piece), out_shape=jax.Shap...  5.98 us
  transfers between devices with their start and end apart: 10, of which 5 were waited for; matrix products, arithmetic and copies ran while one was open for 0% of the time, Pallas kernels for 30%

profile of v5, /device:TPU:0, one launch (start us, length us, event | category | flops | bytes accessed | tf_op | source)
XLA Modules:
  0.0 48.4 jit_solution(6215945220123747803)
XLA Ops:
  0.6 0.9 %packed_own.1.own_ref = f32[40,128]{1,0:T(8,128)S(1)} custom-call(f32[4,1024]{1,0:T(4,128)} %bitcast.19, s32[4,45]{1,0:T(4,128)} %bitcast.21, s32[1,4]{1,0:T(1,128)} %bitcast.22), custom_call_target="tpu_custom_call" | custom-call | tf_op jit(solution)/shard_map/packed_own/pallas_call | solution.py:112
  1.5 5.1 %collective-permute-start.1 = (f32[40,128]{1,0:T(8,128)S(1)}, f32[40,128]{1,0:T(8,128)S(1)}, u32[]{:S(2)}, u32[]{:S(2)}) collective-permute-start(f32[40,128]{1,0:T(8,128)S(1)} %packed_own.1.own_ref), channel_id=1, source_target_pairs={{0,3},{1,0},{2,1},{3,2},{4,7},{5,4},{6,5},{7,6},{8,11},{9,8},{10,9... | collective-permute-start | bytes 61448 | tf_op jit(solution)/shard_map/ppermute | solution.py:43
  6.6 0.0 collective-permute-start
  6.6 2.0 %split_piece.4.refs_1_ = bf16[960,1440]{1,0:T(8,128)(2,1)S(1)} custom-call(f32[1440,1440]{1,0:T(8,128)} %bitcast.14), custom_call_target="tpu_custom_call" | custom-call | flops 1048576 | bytes 2764800 | tf_op jit(solution)/shard_map/split_piece/pallas_call | solution.py:153
  8.6 2.0 %split_piece.3.refs_0_ = bf16[960,1440]{1,0:T(8,128)(2,1)S(1)} custom-call(f32[1440,1440]{1,0:T(8,128)} %bitcast.15), custom_call_target="tpu_custom_call" | custom-call | flops 1048576 | bytes 2764800 | tf_op jit(solution)/shard_map/split_piece/pallas_call | solution.py:153
  10.6 0.0 collective-permute-done.1.above_ref
  10.7 1.6 %collective-permute-done.below_ref = f32[40,128]{1,0:T(8,128)S(1)} collective-permute-done((f32[40,128]{1,0:T(8,128)S(1)}, f32[40,128]{1,0:T(8,128)S(1)}, u32[]{:S(2)}, u32[]{:S(2)}) %collective-permute-start) | collective-permute-done | bytes 20512 | tf_op jit(solution)/shard_map/ppermute | solution.py:43
  12.2 1.5 %collective-permute-start.2 = (f32[3,32,128]{2,1,0:T(8,128)S(1)}, f32[3,32,128]{2,1,0:T(8,128)S(1)}, u32[]{:S(2)}, u32[]{:S(2)}) collective-permute-start(f32[3,32,128]{2,1,0:T(8,128)S(1)} %pad_maximum_fusion.1), channel_id=1, source_target_pairs={{0,16},{1,17},{2,18},{3,19},{4,20},{5,21},{6,22},{7,23},{8,24},{9,... | collective-permute-start | bytes 147464 | tf_op jit(solution)/shard_map/ppermute | solution.py:43
  13.8 0.9 %setup.1 = (f32[45,256]{1,0:T(8,128)S(1)}, f32[32,256]{1,0:T(8,128)S(1)}, f32[32,256]{1,0:T(8,128)S(1)}) custom-call(f32[40,128]{1,0:T(8,128)S(1)} %packed_own.1.own_ref, f32[40,128]{1,0:T(8,128)S(1)} %collective-permute-done.below_ref, f32[40,128]{1,0:T(8,128)S(1)} %collective-permute-done.1.above_ref, f32[4,1024]{1,0:T(4,128)} %table_hbm.1), custom_call_target="tpu_custom_call" | custom-call | tf_op jit(solution)/shard_map/setup/pallas_call | solution.py:211
  14.7 1.6 %collective-permute-done.2 = f32[3,32,128]{2,1,0:T(8,128)S(1)} collective-permute-done((f32[3,32,128]{2,1,0:T(8,128)S(1)}, f32[3,32,128]{2,1,0:T(8,128)S(1)}, u32[]{:S(2)}, u32[]{:S(2)}) %collective-permute-start.2) | collective-permute-done | bytes 49184 | tf_op jit(solution)/shard_map/ppermute | solution.py:43
  16.4 0.1 collective-permute-start.4
  16.5 0.5 %collective-permute-start.3 = (f32[2,3,32,128]{3,2,1,0:T(8,128)S(1)}, f32[2,3,32,128]{3,2,1,0:T(8,128)S(1)}, u32[]{:S(2)}, u32[]{:S(2)}) collective-permute-start(f32[2,3,32,128]{3,2,1,0:T(8,128)S(1)} %pad_maximum_fusion.plane_ref), channel_id=1, source_target_pairs={{0,4},{1,5},{2,6},{3,7},{4,8},{5,9},{6,10},{7,11},{8,12},{9,13},{1... | collective-permute-start | bytes 294920 | tf_op jit(solution)/shard_map/ppermute | solution.py:43
  17.0 2.0 %split_piece.5.refs_2_ = bf16[960,1440]{1,0:T(8,128)(2,1)S(1)} custom-call(f32[1440,1440]{1,0:T(8,128)} %bitcast.16), custom_call_target="tpu_custom_call" | custom-call | flops 1048576 | bytes 2764800 | tf_op jit(solution)/shard_map/split_piece/pallas_call | solution.py:153
  18.9 0.9 %first_images.1.image_ref.refs_5_ = f32[45,32,256]{2,1,0:T(8,128)S(1)} custom-call(bf16[960,1440]{1,0:T(8,128)(2,1)S(1)} %split_piece.3.refs_0_, bf16[960,1440]{1,0:T(8,128)(2,1)S(1)} %split_piece.4.refs_1_, bf16[960,1440]{1,0:T(8,128)(2,1)S(1)} %split_piece.5.refs_2_, f32[32,256]{1,0:T(8,128)S(1)} %get-tuple-element.43.refs_3_.tile_ref.refs_9_.refs_5_), custom_call_target="tpu_custom_call" | custom-call | tf_op jit(solution)/shard_map/first_images/pallas_call | solution.py:258
  19.9 0.5 %early_columns.1 = (bf16[1440,512]{1,0:T(8,128)(2,1)S(1)}, bf16[2880,256]{1,0:T(8,128)(2,1)S(1)}) custom-call(f32[2,3,32,128]{3,2,1,0:T(8,128)S(1)} %pad_maximum_fusion.plane_ref, f32[45,256]{1,0:T(8,128)S(1)} %get-tuple-element.42.member_ref.refs_8_, f32[32,256]{1,0:T(8,128)S(1)} %get-tuple-element.43.refs_3_.tile_ref.refs_9_.refs_5_, ...), custom_call_target="tpu_custom_call" | custom-call | tf_op jit(solution)/shard_map/early_columns/pallas_call | solution.py:355
  20.4 0.0 collective-permute-done.4.refs_7_
  20.4 1.2 %collective-permute-done.3.refs_6_ = f32[2,3,32,128]{3,2,1,0:T(8,128)S(1)} collective-permute-done((f32[2,3,32,128]{3,2,1,0:T(8,128)S(1)}, f32[2,3,32,128]{3,2,1,0:T(8,128)S(1)}, u32[]{:S(2)}, u32[]{:S(2)}) %collective-permute-start.3) | collective-permute-done | bytes 98336 | tf_op jit(solution)/shard_map/ppermute | solution.py:43
  21.6 12.3 %shard_map.68 = (f32[10,32,128]{2,1,0:T(8,128)S(1)}, f32[10,32,128]{2,1,0:T(8,128)S(1)}, f32[10,32,128]{2,1,0:T(8,128)S(1)}, f32[10,32,128]{2,1,0:T(8,128)S(1)},...) custom-call(bf16[960,1440]{1,0:T(8,128)(2,1)S(1)} %split_piece.3.refs_, ...), custom_call_target="tpu_custom_call", output_to_operand_aliasing={{4}: (3, {}), {5}: (4, {})} | custom-call | flops 6370099200 | bytes 1048576 | tf_op jit(solution)/shard_map/pallas_call | solution.py:486
  33.9 1.1 %collective-permute-start.5 = (f32[10,32,128]{2,1,0:T(8,128)S(1)}, f32[10,32,128]{2,1,0:T(8,128)S(1)}, u32[]{:S(2)}, u32[]{:S(2)}) collective-permute-start(f32[10,32,128]{2,1,0:T(8,128)S(1)} %get-tuple-element.58), channel_id=1, source_target_pairs={{0,28},{1,29},{2,30},{3,31},{4,16},{5,17},{6,18},{7,19},{8,20},{9,... | collective-permute-start | bytes 491528 | tf_op jit(solution)/shard_map/ppermute | solution.py:43
  35.0 0.7 %collective-permute-start.7 = (f32[10,32,128]{2,1,0:T(8,128)S(1)}, f32[10,32,128]{2,1,0:T(8,128)S(1)}, u32[]{:S(2)}, u32[]{:S(2)}) collective-permute-start(f32[10,32,128]{2,1,0:T(8,128)S(1)} %get-tuple-element.60), channel_id=1, source_target_pairs={{0,20},{1,21},{2,22},{3,23},{4,24},{5,25},{6,26},{7,27},{8,28},{9,... | collective-permute-start | bytes 491528 | tf_op jit(solution)/shard_map/ppermute | solution.py:43
  35.7 1.9 %shard_map.70 = (f32[10,32,128]{2,1,0:T(8,128)S(1)}, f32[10,32,128]{2,1,0:T(8,128)S(1)}) custom-call(bf16[960,1440]{1,0:T(8,128)(2,1)S(1)} %split_piece.3.refs_0_, bf16[960,1440]{1,0:T(8,128)(2,1)S(1)} %split_piece.4.refs_1_, bf16[960,1440]{1,0:T(8,128)(2,1)S(1)} %split_piece.5.refs_2_, bf16[1440,512]{1,0:T(8,128)(2,1)S(1)} %get-tuple-element.47.refs_3_, ...), custom_call_target="tpu_custom_call" | custom-call | flops 530841600 | bytes 1048576 | tf_op jit(solution)/shard_map/pallas_call | solution.py:486
  37.6 1.5 %collective-permute-start.6 = (f32[10,32,128]{2,1,0:T(8,128)S(1)}, f32[10,32,128]{2,1,0:T(8,128)S(1)}, u32[]{:S(2)}, u32[]{:S(2)}) collective-permute-start(f32[10,32,128]{2,1,0:T(8,128)S(1)} %get-tuple-element.59), channel_id=1, source_target_pairs={{0,16},{1,17},{2,18},{3,19},{4,20},{5,21},{6,22},{7,23},{8,24},{9,... | collective-permute-start | bytes 491528 | tf_op jit(solution)/shard_map/ppermute | solution.py:43
  39.2 1.6 %shard_map.71 = (f32[5,32,128]{2,1,0:T(8,128)S(1)}, f32[5,32,128]{2,1,0:T(8,128)S(1)}, f32[5,32,128]{2,1,0:T(8,128)S(1)}, f32[5,32,128]{2,1,0:T(8,128)S(1)}) custom-call(bf16[960,1440]{1,0:T(8,128)(2,1)S(1)} %split_piece.3.refs_0_, bf16[960,1440]{1,0:T(8,128)(2,1)S(1)} %split_piece.4.refs_1_, bf16[960,1440]{1,0:T(8,128)(2,1)S(1)} %split_piece.5.refs_2_, ...), custom_call_target="tpu_custom_call" | custom-call | flops 530841600 | bytes 1048576 | tf_op jit(solution)/shard_map/pallas_call | solution.py:486
  40.8 0.8 %collective-permute-start.8 = (f32[5,32,128]{2,1,0:T(8,128)S(1)}, f32[5,32,128]{2,1,0:T(8,128)S(1)}, u32[]{:S(2)}, u32[]{:S(2)}) collective-permute-start(f32[5,32,128]{2,1,0:T(8,128)S(1)} %get-tuple-element.61), channel_id=1, source_target_pairs={{0,12},{1,13},{2,14},{3,15},{4,0},{5,1},{6,2},{7,3},{8,4},{9,5},{1... | collective-permute-start | bytes 245768 | tf_op jit(solution)/shard_map/ppermute | solution.py:43
  41.5 0.1 collective-permute-start.9
  41.6 1.3 %shard_map.69 = (f32[5,32,128]{2,1,0:T(8,128)S(1)}, f32[5,32,128]{2,1,0:T(8,128)S(1)}, f32[32,128]{1,0:T(8,128)S(1)}) custom-call(bf16[960,1440]{1,0:T(8,128)(2,1)S(1)} %split_piece.3.refs_0_, bf16[960,1440]{1,0:T(8,128)(2,1)S(1)} %split_piece.4.refs_1_, bf16[960,1440]{1,0:T(8,128)(2,1)S(1)} %split_piece.5.refs_2_, ...), custom_call_target="tpu_custom_call" | custom-call | flops 530841600 | bytes 1048576 | tf_op jit(solution)/shard_map/pallas_call | solution.py:486
  42.8 0.9 %turned_tiles.1.refs_1_.refs_5_ = f32[45,32,128]{2,1,0:T(8,128)S(1)} custom-call(f32[10,32,128]{2,1,0:T(8,128)S(1)} %get-tuple-element.50.refs_0_, f32[10,32,128]{2,1,0:T(8,128)S(1)} %get-tuple-element.51.refs_1_, f32[10,32,128]{2,1,0:T(8,128)S(1)} %get-tuple-element.52.refs_2_, f32[5,32,128]{2,1,0:T(8,128)S(1)} %get-tuple-element.53.refs_3_, ...), custom_call_target="tpu_custom_call" | custom-call | flops 1048576 | bytes 2097152 | tf_op jit(solution)/shard_map/turned_tiles/pallas_call | solution.py:566
  43.7 0.7 %near_sums.1 = (f32[48,128]{1,0:T(8,128)S(1)}, f32[4,1024]{1,0:T(4,128)}) custom-call(f32[5,32,128]{2,1,0:T(8,128)S(1)} %get-tuple-element.49.refs_0_, f32[45,32,128]{2,1,0:T(8,128)S(1)} %turned_tiles.1.refs_1_.refs_5_, f32[32,128]{1,0:T(8,128)S(1)} %get-tuple-element.56.refs_2_), custom_call_target="tpu_custom_call" | custom-call | tf_op jit(solution)/shard_map/near_sums/pallas_call | solution.py:595
  44.4 0.0 collective-permute-done.8.refs_3_
  44.4 1.6 %collective-permute-done.9.refs_4_ = f32[5,32,128]{2,1,0:T(8,128)S(1)} collective-permute-done((f32[5,32,128]{2,1,0:T(8,128)S(1)}, f32[5,32,128]{2,1,0:T(8,128)S(1)}, u32[]{:S(2)}, u32[]{:S(2)}) %collective-permute-start.9) | collective-permute-done | bytes 81952 | tf_op jit(solution)/shard_map/ppermute | solution.py:43
  46.1 0.0 collective-permute-done.5.refs_0_
  46.1 0.0 collective-permute-done.7.refs_2_
  46.1 1.4 %collective-permute-done.6.refs_1_ = f32[10,32,128]{2,1,0:T(8,128)S(1)} collective-permute-done((f32[10,32,128]{2,1,0:T(8,128)S(1)}, f32[10,32,128]{2,1,0:T(8,128)S(1)}, u32[]{:S(2)}, u32[]{:S(2)}) %collective-permute-start.6) | collective-permute-done | bytes 163872 | tf_op jit(solution)/shard_map/ppermute | solution.py:43
  47.5 0.9 %total_sums.1 = f32[4,45]{1,0:T(4,128)} custom-call(f32[10,32,128]{2,1,0:T(8,128)S(1)} %collective-permute-done.5.refs_0_, f32[10,32,128]{2,1,0:T(8,128)S(1)} %collective-permute-done.6.refs_1_, f32[10,32,128]{2,1,0:T(8,128)S(1)} %collective-permute-done.7.refs_2_, f32[5,32,128]{2,1,0:T(8,128)S(1)} %collective-permute-done.8.refs_3_, ...), custom_call_target="tpu_custom_call" | custom-call | tf_op jit(solution)/shard_map/total_sums/pallas_call | solution.py:631
  (5 shorter events, 0.0 us)
Async XLA Ops:
  1.5 9.1 %collective-permute-start.1 = (f32[40,128]{1,0:T(8,128)S(1)}, f32[40,128]{1,0:T(8,128)S(1)}, u32[]{:S(2)}, u32[]{:S(2)}) collective-permute-start(f32[40,128]{1,0:T(8,128)S(1)} %packed_own.1.own_ref), channel_id=1, source_target_pairs={{0,3},{1,0},{2,1},{3,2},{4,7},{5,4},{6,5},{7,6},{8,11},{9,8},{10,9... | collective-permute-start | bytes 61448 | tf_op jit(solution)/shard_map/ppermute | solution.py:43
  6.6 5.6 %collective-permute-start = (f32[40,128]{1,0:T(8,128)S(1)}, f32[40,128]{1,0:T(8,128)S(1)}, u32[]{:S(2)}, u32[]{:S(2)}) collective-permute-start(f32[40,128]{1,0:T(8,128)S(1)} %packed_own.1.own_ref), channel_id=1, source_target_pairs={{0,1},{1,2},{2,3},{3,0},{4,5},{5,6},{6,7},{7,4},{8,9},{9,10},{10,1... | collective-permute-start | bytes 61448 | tf_op jit(solution)/shard_map/ppermute | solution.py:43
  12.2 4.1 %collective-permute-start.2 = (f32[3,32,128]{2,1,0:T(8,128)S(1)}, f32[3,32,128]{2,1,0:T(8,128)S(1)}, u32[]{:S(2)}, u32[]{:S(2)}) collective-permute-start(f32[3,32,128]{2,1,0:T(8,128)S(1)} %pad_maximum_fusion.1), channel_id=1, source_target_pairs={{0,16},{1,17},{2,18},{3,19},{4,20},{5,21},{6,22},{7,23},{8,24},{9,... | collective-permute-start | bytes 147464 | tf_op jit(solution)/shard_map/ppermute | solution.py:43
  16.4 4.0 %collective-permute-start.4 = (f32[2,3,32,128]{3,2,1,0:T(8,128)S(1)}, f32[2,3,32,128]{3,2,1,0:T(8,128)S(1)}, u32[]{:S(2)}, u32[]{:S(2)}) collective-permute-start(f32[2,3,32,128]{3,2,1,0:T(8,128)S(1)} %pad_maximum_fusion.plane_ref), channel_id=1, source_target_pairs={{0,12},{1,13},{2,14},{3,15},{4,0},{5,1},{6,2},{7,3},{8,4},{9,5},{1... | collective-permute-start | bytes 294920 | tf_op jit(solution)/shard_map/ppermute | solution.py:43
  16.5 5.1 %collective-permute-start.3 = (f32[2,3,32,128]{3,2,1,0:T(8,128)S(1)}, f32[2,3,32,128]{3,2,1,0:T(8,128)S(1)}, u32[]{:S(2)}, u32[]{:S(2)}) collective-permute-start(f32[2,3,32,128]{3,2,1,0:T(8,128)S(1)} %pad_maximum_fusion.plane_ref), channel_id=1, source_target_pairs={{0,4},{1,5},{2,6},{3,7},{4,8},{5,9},{6,10},{7,11},{8,12},{9,13},{1... | collective-permute-start | bytes 294920 | tf_op jit(solution)/shard_map/ppermute | solution.py:43
  33.9 12.2 %collective-permute-start.5 = (f32[10,32,128]{2,1,0:T(8,128)S(1)}, f32[10,32,128]{2,1,0:T(8,128)S(1)}, u32[]{:S(2)}, u32[]{:S(2)}) collective-permute-start(f32[10,32,128]{2,1,0:T(8,128)S(1)} %get-tuple-element.58), channel_id=1, source_target_pairs={{0,28},{1,29},{2,30},{3,31},{4,16},{5,17},{6,18},{7,19},{8,20},{9,... | collective-permute-start | bytes 491528 | tf_op jit(solution)/shard_map/ppermute | solution.py:43
  35.0 11.1 %collective-permute-start.7 = (f32[10,32,128]{2,1,0:T(8,128)S(1)}, f32[10,32,128]{2,1,0:T(8,128)S(1)}, u32[]{:S(2)}, u32[]{:S(2)}) collective-permute-start(f32[10,32,128]{2,1,0:T(8,128)S(1)} %get-tuple-element.60), channel_id=1, source_target_pairs={{0,20},{1,21},{2,22},{3,23},{4,24},{5,25},{6,26},{7,27},{8,28},{9,... | collective-permute-start | bytes 491528 | tf_op jit(solution)/shard_map/ppermute | solution.py:43
  37.6 9.9 %collective-permute-start.6 = (f32[10,32,128]{2,1,0:T(8,128)S(1)}, f32[10,32,128]{2,1,0:T(8,128)S(1)}, u32[]{:S(2)}, u32[]{:S(2)}) collective-permute-start(f32[10,32,128]{2,1,0:T(8,128)S(1)} %get-tuple-element.59), channel_id=1, source_target_pairs={{0,16},{1,17},{2,18},{3,19},{4,20},{5,21},{6,22},{7,23},{8,24},{9,... | collective-permute-start | bytes 491528 | tf_op jit(solution)/shard_map/ppermute | solution.py:43
  40.8 3.7 %collective-permute-start.8 = (f32[5,32,128]{2,1,0:T(8,128)S(1)}, f32[5,32,128]{2,1,0:T(8,128)S(1)}, u32[]{:S(2)}, u32[]{:S(2)}) collective-permute-start(f32[5,32,128]{2,1,0:T(8,128)S(1)} %get-tuple-element.61), channel_id=1, source_target_pairs={{0,12},{1,13},{2,14},{3,15},{4,0},{5,1},{6,2},{7,3},{8,4},{9,5},{1... | collective-permute-start | bytes 245768 | tf_op jit(solution)/shard_map/ppermute | solution.py:43
  41.5 4.6 %collective-permute-start.9 = (f32[5,32,128]{2,1,0:T(8,128)S(1)}, f32[5,32,128]{2,1,0:T(8,128)S(1)}, u32[]{:S(2)}, u32[]{:S(2)}) collective-permute-start(f32[5,32,128]{2,1,0:T(8,128)S(1)} %get-tuple-element.62), channel_id=1, source_target_pairs={{0,4},{1,5},{2,6},{3,7},{4,8},{5,9},{6,10},{7,11},{8,12},{9,13},{1... | collective-permute-start | bytes 245768 | tf_op jit(solution)/shard_map/ppermute | solution.py:43

commit v6 on v5

--- a/solution.py
+++ b/solution.py
@@ -23,7 +23,7 @@
 PIECE = WINDOW // PIECES
 PIECE_ROWS = PIECE * L2
 SPLIT_STEPS = 3
-CHUNK = 15
+CHUNK = 23
 MESH_AXES = ("gx", "gy", "gz")
 
 
@@ -386,47 +386,61 @@
 
 def last_sweep(parts, column, window, tile_ref, delta_ref, stage, sent, local, tau_ref, slots, final):
     deltas = [delta_blocks(delta_ref[:, half * LANES : (half + 1) * LANES]) for half in range(2)]
-    chunks = [[cell_of(ox, oy, oz) for ox, oy in group for oz in range(-2, 3)] for group in stage]
     group_of = lane_index((L2, LANES)) // L2
-
-    def use_image(i, slot):
-        count = len(chunks[i])
+    lines = [
+        (i, place, cell_of(ox, oy, 0))
+        for i, group in enumerate(stage)
+        for place, (ox, oy) in enumerate(group)
+    ]
+    step = stage_lines(stage)
+    chunks = [lines[i : i + step] for i in range(0, len(lines), step)]
+    places = [(at, oz) for at in range(step) for oz in range(-2, 3)]
+
+    def use_image(number, slot):
+        chunk = chunks[number]
         values = []
         for half in range(2):
             lanes = slice(half * LANES, (half + 1) * LANES)
-            for place, cell in enumerate(chunks[i]):
-                value = moved(window, cell, half, slot[place, :, lanes])
+            work = final.at[number % 2, half]
+            for row, (at, oz) in enumerate(places[: 5 * len(chunk)]):
+                if half == 1 and oz == 0:
+                    continue
+                cell = chunk[at][2] + oz
+                value = moved(window, cell, half, slot[row, :, lanes])
                 if cell == CENTRE:
                     value = value + tile_ref[:, lanes]
-                    if half == 0:
-                        tau_ref[...] = value
-                rows = slice(place * L2, (place + 1) * L2)
+                    tau_ref[...] = value
                 high, low = halves(value)
-                final[half, rows, :LANES] = high
-                final[half, rows, LANES:] = low
-            product = jnp.dot(
-                final[half, : count * L2, :], deltas[half], preferred_element_type=f32
-            )
+                work[row * L2 : (row + 1) * L2, :LANES] = high
+                work[row * L2 : (row + 1) * L2, LANES:] = low
+            count = 5 * len(chunk)
+            product = jnp.dot(work[: count * L2, :], deltas[half], preferred_element_type=f32)
             product = product[:, :LANES] + product[:, LANES:]
             values.append(product.reshape(count, L2, LANES))
-        local[i][...] = values[0]
-        for place, cell in enumerate(chunks[i]):
-            oz = cell % 5 - 2
-            value = values[0][place]
+        for row, (at, oz) in enumerate(places[: 5 * len(chunk)]):
+            i, place, _ = chunk[at]
+            value = values[0][row]
+            local[i][place * 5 + oz + 2] = value
             if oz > 0:
-                value = jnp.where(group_of >= DEPTH - oz, values[1][place], value)
+                value = jnp.where(group_of >= DEPTH - oz, values[1][row], value)
             elif oz < 0:
-                value = jnp.where(group_of < -oz, values[1][place], value)
+                value = jnp.where(group_of < -oz, values[1][row], value)
             if oz != 0:
                 value = pltpu.roll(value, oz % DEPTH * L2, 1)
-            sent[i][place] = value
-
-    sweep_over(parts, chunks, column, use_image, slots)
+            sent[i][place * 5 + oz + 2] = value
+
+    cells = [[middle + oz for _, _, middle in chunk for oz in range(-2, 3)] for chunk in chunks]
+    sweep_over(parts, cells, column, use_image, slots)
+
+
+def stage_lines(stage):
+    return 2 if sum(len(group) for group in stage) > 2 else 1
 
 
 def first_kernel(stage, *refs):
     parts, refs = refs[:PIECES], refs[PIECES:]
-    _, _, image_ref, south_ref, north_ref, member_ref, tile_ref, delta_ref = refs[:8]
+    early_column, early_window, image_ref, south_ref, north_ref = refs[:5]
+    member_ref, tile_ref, delta_ref = refs[5:8]
     sent, local = refs[8 : 8 + len(stage)], refs[8 + len(stage) : 8 + 2 * len(stage)]
     column, window, other, slot_a, slot_b, final = refs[8 + 2 * len(stage) :]
     slots = (slot_a, slot_b)
@@ -435,13 +449,20 @@
         ref = south_ref if dy == 0 else north_ref
         return ref[dx % ref.shape[0], slab]
 
+    for cell in early_cells():
+        rows = slice(cell * L2, (cell + 1) * L2)
+        column[rows, :] = early_column[rows, :]
+        rows = slice(cell * 2 * L2, (cell + 1) * 2 * L2)
+        window[rows, :] = early_window[rows, :]
     late = [cell for cell in range(WINDOW) if cell not in early_cells()]
     for cell in late:
         set_window(window, near, member_ref, cell)
     for cell in late:
         set_column(column, window, tile_ref, cell, image_ref[cell])
     source, target = column, other
-    full = [list(range(base, base + CHUNK)) for base in range(0, WINDOW, CHUNK)]
+    full = [
+        list(range(base, min(base + CHUNK, WINDOW))) for base in range(0, WINDOW, CHUNK)
+    ]
     for _ in range(1, ITERS - 1):
 
         def use_image(i, slot, target=target):
@@ -479,8 +500,9 @@
     )
 
 
-def stage_call(kernel, stage, extra_outs, extra_scratch, operands, flops, aliases=()):
-    longest = max(CHUNK, 5 * max(len(group) for group in stage))
+def stage_call(kernel, stage, extra_outs, extra_scratch, operands, flops):
+    lines = stage_lines(stage)
+    longest = max(CHUNK, 5 * lines)
     out_shape = [jax.ShapeDtypeStruct((5 * len(group), L2, LANES), f32) for group in stage] * 2
     out_shape += extra_outs
     return pl.pallas_call(
@@ -490,10 +512,7 @@
         out_specs=tuple(in_vmem(len(out_shape))),
         scratch_shapes=extra_scratch
         + [pltpu.VMEM((longest, L2, 2 * LANES), f32)] * 2
-        + [pltpu.VMEM((2, longest * L2, 2 * LANES), bf16)],
-        input_output_aliases={
-            operand: 2 * len(stage) + i for i, operand in enumerate(aliases)
-        },
+        + [pltpu.VMEM((2, 2, 5 * lines * L2, 2 * LANES), bf16)],
         compiler_params=pltpu.CompilerParams(vmem_limit_bytes=24 * MIB),
         cost_estimate=pl.CostEstimate(flops=flops, bytes_accessed=MIB, transcendentals=0),
     )(*operands)
@@ -510,7 +529,6 @@
         [pltpu.VMEM((ROWS, 4 * LANES), bf16)],
         (*parts, column, window, images, south, north, member, tile, delta),
         2 * 6 * (ITERS - 2) * ROWS * ROWS * LANES,
-        (PIECES, PIECES + 1),
     )
 
 
@@ -682,8 +700,8 @@
 
     table = plane_groups()
     stages = [
+        [shift for shift in table if shift[0] != 0 and shift[1] == 0],
         [shift for shift in table if shift[0] != 0 and shift[1] != 0],
-        [shift for shift in table if shift[0] != 0 and shift[1] == 0],
         [shift for shift in table if shift[0] == 0 and shift[1] != 0],
         [(0, 0)],
     ]

time: 48.8 us -> 47.8 us (0.980)
  Pallas kernels: 28.9 us -> 28 us
    pallas_call x4, Pallas kernels: 17.1 us -> 16.2 us  [stage_call(): pl.pallas_call(functools.partial(kernel, stage), out_shape=tuple(out_shap...]
  transfers between devices with their start and end apart: 10 -> 10, of which waited for: 5 -> 4; matrix products, arithmetic and copies ran while one was open for 0% -> 0% of each run, Pallas kernels for 30% -> 32%
where the time goes in v6:
time: 47.8 us; the launch traced here: 47.5 us
  Pallas kernels  28 us (59%)
  starting transfers between devices  11.4 us (24%)
  waiting for transfers between devices  7.34 us (15%)
  between operations  0.75 us (2%)
    pallas_call x4, Pallas kernels, stage_call(): pl.pallas_call(functools.partial(kernel, stage), out_shape=tuple(out_shap...  16.2 us
    ppermute x10, starting transfers between devices, shifted(): return lax.ppermute(x, MESH_AXES, pairs)  11.4 us
    ppermute x10, waiting for transfers between devices, shifted(): return lax.ppermute(x, MESH_AXES, pairs)  7.34 us
    pallas_call x3, Pallas kernels, split_piece(): pl.pallas_call(functools.partial(split_kernel, piece), out_shape=jax.Shap...  5.98 us
  transfers between devices with their start and end apart: 10, of which 4 were waited for; matrix products, arithmetic and copies ran while one was open for 0% of the time, Pallas kernels for 32%

profile of v6, /device:TPU:0, one launch (start us, length us, event | category | flops | bytes accessed | tf_op | source)
XLA Modules:
  0.0 47.5 jit_solution(12088990109648100956)
XLA Ops:
  0.6 0.9 %packed_own.1.own_ref = f32[40,128]{1,0:T(8,128)S(1)} custom-call(f32[4,1024]{1,0:T(4,128)} %bitcast.19, s32[4,45]{1,0:T(4,128)} %bitcast.21, s32[1,4]{1,0:T(1,128)} %bitcast.22), custom_call_target="tpu_custom_call" | custom-call | tf_op jit(solution)/shard_map/packed_own/pallas_call | solution.py:112
  1.5 5.1 %collective-permute-start.1 = (f32[40,128]{1,0:T(8,128)S(1)}, f32[40,128]{1,0:T(8,128)S(1)}, u32[]{:S(2)}, u32[]{:S(2)}) collective-permute-start(f32[40,128]{1,0:T(8,128)S(1)} %packed_own.1.own_ref), channel_id=1, source_target_pairs={{0,3},{1,0},{2,1},{3,2},{4,7},{5,4},{6,5},{7,6},{8,11},{9,8},{10,9... | collective-permute-start | bytes 61448 | tf_op jit(solution)/shard_map/ppermute | solution.py:43
  6.6 0.0 collective-permute-start
  6.6 2.0 %split_piece.4.refs_1_ = bf16[960,1440]{1,0:T(8,128)(2,1)S(1)} custom-call(f32[1440,1440]{1,0:T(8,128)} %bitcast.14), custom_call_target="tpu_custom_call" | custom-call | flops 1048576 | bytes 2764800 | tf_op jit(solution)/shard_map/split_piece/pallas_call | solution.py:153
  8.6 2.0 %split_piece.3.refs_0_ = bf16[960,1440]{1,0:T(8,128)(2,1)S(1)} custom-call(f32[1440,1440]{1,0:T(8,128)} %bitcast.15), custom_call_target="tpu_custom_call" | custom-call | flops 1048576 | bytes 2764800 | tf_op jit(solution)/shard_map/split_piece/pallas_call | solution.py:153
  10.6 0.0 collective-permute-done.1.above_ref
  10.7 1.6 %collective-permute-done.below_ref = f32[40,128]{1,0:T(8,128)S(1)} collective-permute-done((f32[40,128]{1,0:T(8,128)S(1)}, f32[40,128]{1,0:T(8,128)S(1)}, u32[]{:S(2)}, u32[]{:S(2)}) %collective-permute-start) | collective-permute-done | bytes 20512 | tf_op jit(solution)/shard_map/ppermute | solution.py:43
  12.2 1.5 %collective-permute-start.2 = (f32[3,32,128]{2,1,0:T(8,128)S(1)}, f32[3,32,128]{2,1,0:T(8,128)S(1)}, u32[]{:S(2)}, u32[]{:S(2)}) collective-permute-start(f32[3,32,128]{2,1,0:T(8,128)S(1)} %pad_maximum_fusion.1), channel_id=1, source_target_pairs={{0,16},{1,17},{2,18},{3,19},{4,20},{5,21},{6,22},{7,23},{8,24},{9,... | collective-permute-start | bytes 147464 | tf_op jit(solution)/shard_map/ppermute | solution.py:43
  13.8 0.9 %setup.1 = (f32[45,256]{1,0:T(8,128)S(1)}, f32[32,256]{1,0:T(8,128)S(1)}, f32[32,256]{1,0:T(8,128)S(1)}) custom-call(f32[40,128]{1,0:T(8,128)S(1)} %packed_own.1.own_ref, f32[40,128]{1,0:T(8,128)S(1)} %collective-permute-done.below_ref, f32[40,128]{1,0:T(8,128)S(1)} %collective-permute-done.1.above_ref, f32[4,1024]{1,0:T(4,128)} %table_hbm.1), custom_call_target="tpu_custom_call" | custom-call | tf_op jit(solution)/shard_map/setup/pallas_call | solution.py:211
  14.7 1.6 %collective-permute-done.2 = f32[3,32,128]{2,1,0:T(8,128)S(1)} collective-permute-done((f32[3,32,128]{2,1,0:T(8,128)S(1)}, f32[3,32,128]{2,1,0:T(8,128)S(1)}, u32[]{:S(2)}, u32[]{:S(2)}) %collective-permute-start.2) | collective-permute-done | bytes 49184 | tf_op jit(solution)/shard_map/ppermute | solution.py:43
  16.4 0.1 collective-permute-start.4
  16.5 0.5 %collective-permute-start.3 = (f32[2,3,32,128]{3,2,1,0:T(8,128)S(1)}, f32[2,3,32,128]{3,2,1,0:T(8,128)S(1)}, u32[]{:S(2)}, u32[]{:S(2)}) collective-permute-start(f32[2,3,32,128]{3,2,1,0:T(8,128)S(1)} %pad_maximum_fusion.plane_ref), channel_id=1, source_target_pairs={{0,4},{1,5},{2,6},{3,7},{4,8},{5,9},{6,10},{7,11},{8,12},{9,13},{1... | collective-permute-start | bytes 294920 | tf_op jit(solution)/shard_map/ppermute | solution.py:43
  17.0 2.0 %split_piece.5.refs_2_ = bf16[960,1440]{1,0:T(8,128)(2,1)S(1)} custom-call(f32[1440,1440]{1,0:T(8,128)} %bitcast.16), custom_call_target="tpu_custom_call" | custom-call | flops 1048576 | bytes 2764800 | tf_op jit(solution)/shard_map/split_piece/pallas_call | solution.py:153
  18.9 0.9 %first_images.1.image_ref.refs_5_ = f32[45,32,256]{2,1,0:T(8,128)S(1)} custom-call(bf16[960,1440]{1,0:T(8,128)(2,1)S(1)} %split_piece.3.refs_0_, bf16[960,1440]{1,0:T(8,128)(2,1)S(1)} %split_piece.4.refs_1_, bf16[960,1440]{1,0:T(8,128)(2,1)S(1)} %split_piece.5.refs_2_, f32[32,256]{1,0:T(8,128)S(1)} %get-tuple-element.43.refs_3_.tile_ref.refs_9_.refs_5_), custom_call_target="tpu_custom_call" | custom-call | tf_op jit(solution)/shard_map/first_images/pallas_call | solution.py:258
  19.9 0.5 %early_columns.1 = (bf16[1440,512]{1,0:T(8,128)(2,1)S(1)}, bf16[2880,256]{1,0:T(8,128)(2,1)S(1)}) custom-call(f32[2,3,32,128]{3,2,1,0:T(8,128)S(1)} %pad_maximum_fusion.plane_ref, f32[45,256]{1,0:T(8,128)S(1)} %get-tuple-element.42.member_ref.refs_8_, f32[32,256]{1,0:T(8,128)S(1)} %get-tuple-element.43.refs_3_.tile_ref.refs_9_.refs_5_, ...), custom_call_target="tpu_custom_call" | custom-call | tf_op jit(solution)/shard_map/early_columns/pallas_call | solution.py:355
  20.4 0.0 collective-permute-done.4.refs_7_
  20.4 1.2 %collective-permute-done.3.refs_6_ = f32[2,3,32,128]{3,2,1,0:T(8,128)S(1)} collective-permute-done((f32[2,3,32,128]{3,2,1,0:T(8,128)S(1)}, f32[2,3,32,128]{3,2,1,0:T(8,128)S(1)}, u32[]{:S(2)}, u32[]{:S(2)}) %collective-permute-start.3) | collective-permute-done | bytes 98336 | tf_op jit(solution)/shard_map/ppermute | solution.py:43
  21.6 10.9 %shard_map.68 = (f32[10,32,128]{2,1,0:T(8,128)S(1)}, f32[10,32,128]{2,1,0:T(8,128)S(1)}, bf16[1440,512]{1,0:T(8,128)(2,1)S(1)}, bf16[2880,256]{1,0:T(8,128)(2,1)S(1)}) custom-call(bf16[960,1440]{1,0:T(8,128)(2,1)S(1)} %split_piece.3.refs_0_, bf16[960,1440]{1,0:T(8,128)(2,1)S(1)} %split_piece.4.refs_1_, bf16[960,1440]{1,0:T(8,128)(2,1)S(1)} %split_piece.5.refs_2_, ...), custom_call_target="tpu_custom_call" | custom-call | flops 6370099200 | bytes 1048576 | tf_op jit(solution)/shard_map/pallas_call | solution.py:508
  32.4 1.5 %collective-permute-start.6 = (f32[10,32,128]{2,1,0:T(8,128)S(1)}, f32[10,32,128]{2,1,0:T(8,128)S(1)}, u32[]{:S(2)}, u32[]{:S(2)}) collective-permute-start(f32[10,32,128]{2,1,0:T(8,128)S(1)} %get-tuple-element.59), channel_id=1, source_target_pairs={{0,16},{1,17},{2,18},{3,19},{4,20},{5,21},{6,22},{7,23},{8,24},{9,... | collective-permute-start | bytes 491528 | tf_op jit(solution)/shard_map/ppermute | solution.py:43
  34.0 2.6 %shard_map.70 = (f32[10,32,128]{2,1,0:T(8,128)S(1)}, f32[10,32,128]{2,1,0:T(8,128)S(1)}, f32[10,32,128]{2,1,0:T(8,128)S(1)}, f32[10,32,128]{2,1,0:T(8,128)S(1)}) custom-call(bf16[960,1440]{1,0:T(8,128)(2,1)S(1)} %split_piece.3.refs_0_, bf16[960,1440]{1,0:T(8,128)(2,1)S(1)} %split_piece.4.refs_1_, bf16[960,1440]{1,0:T(8,128)(2,1)S(1)} %split_piece.5.refs_2_, ...), custom_call_target="tpu_custom_call" | custom-call | flops 530841600 | bytes 1048576 | tf_op jit(solution)/shard_map/pallas_call | solution.py:508
  36.5 0.0 collective-permute-start.5
  36.6 1.7 %collective-permute-start.7 = (f32[10,32,128]{2,1,0:T(8,128)S(1)}, f32[10,32,128]{2,1,0:T(8,128)S(1)}, u32[]{:S(2)}, u32[]{:S(2)}) collective-permute-start(f32[10,32,128]{2,1,0:T(8,128)S(1)} %get-tuple-element.60), channel_id=1, source_target_pairs={{0,20},{1,21},{2,22},{3,23},{4,24},{5,25},{6,26},{7,27},{8,28},{9,... | collective-permute-start | bytes 491528 | tf_op jit(solution)/shard_map/ppermute | solution.py:43
  38.3 1.6 %shard_map.71 = (f32[5,32,128]{2,1,0:T(8,128)S(1)}, f32[5,32,128]{2,1,0:T(8,128)S(1)}, f32[5,32,128]{2,1,0:T(8,128)S(1)}, f32[5,32,128]{2,1,0:T(8,128)S(1)}) custom-call(bf16[960,1440]{1,0:T(8,128)(2,1)S(1)} %split_piece.3.refs_0_, bf16[960,1440]{1,0:T(8,128)(2,1)S(1)} %split_piece.4.refs_1_, bf16[960,1440]{1,0:T(8,128)(2,1)S(1)} %split_piece.5.refs_2_, ...), custom_call_target="tpu_custom_call" | custom-call | flops 530841600 | bytes 1048576 | tf_op jit(solution)/shard_map/pallas_call | solution.py:508
  39.9 0.8 %collective-permute-start.8 = (f32[5,32,128]{2,1,0:T(8,128)S(1)}, f32[5,32,128]{2,1,0:T(8,128)S(1)}, u32[]{:S(2)}, u32[]{:S(2)}) collective-permute-start(f32[5,32,128]{2,1,0:T(8,128)S(1)} %get-tuple-element.61), channel_id=1, source_target_pairs={{0,12},{1,13},{2,14},{3,15},{4,0},{5,1},{6,2},{7,3},{8,4},{9,5},{1... | collective-permute-start | bytes 245768 | tf_op jit(solution)/shard_map/ppermute | solution.py:43
  40.7 0.1 collective-permute-start.9
  40.7 1.3 %shard_map.69 = (f32[5,32,128]{2,1,0:T(8,128)S(1)}, f32[5,32,128]{2,1,0:T(8,128)S(1)}, f32[32,128]{1,0:T(8,128)S(1)}) custom-call(bf16[960,1440]{1,0:T(8,128)(2,1)S(1)} %split_piece.3.refs_0_, bf16[960,1440]{1,0:T(8,128)(2,1)S(1)} %split_piece.4.refs_1_, bf16[960,1440]{1,0:T(8,128)(2,1)S(1)} %split_piece.5.refs_2_, ...), custom_call_target="tpu_custom_call" | custom-call | flops 530841600 | bytes 1048576 | tf_op jit(solution)/shard_map/pallas_call | solution.py:508
  42.0 0.9 %turned_tiles.1.refs_1_.refs_5_ = f32[45,32,128]{2,1,0:T(8,128)S(1)} custom-call(f32[10,32,128]{2,1,0:T(8,128)S(1)} %get-tuple-element.50.refs_0_, f32[10,32,128]{2,1,0:T(8,128)S(1)} %get-tuple-element.51.refs_1_, f32[10,32,128]{2,1,0:T(8,128)S(1)} %get-tuple-element.52.refs_2_, f32[5,32,128]{2,1,0:T(8,128)S(1)} %get-tuple-element.53.refs_3_, ...), custom_call_target="tpu_custom_call" | custom-call | flops 1048576 | bytes 2097152 | tf_op jit(solution)/shard_map/turned_tiles/pallas_call | solution.py:584
  42.9 0.7 %near_sums.1 = (f32[48,128]{1,0:T(8,128)S(1)}, f32[4,1024]{1,0:T(4,128)}) custom-call(f32[5,32,128]{2,1,0:T(8,128)S(1)} %get-tuple-element.49.refs_0_, f32[45,32,128]{2,1,0:T(8,128)S(1)} %turned_tiles.1.refs_1_.refs_5_, f32[32,128]{1,0:T(8,128)S(1)} %get-tuple-element.56.refs_2_), custom_call_target="tpu_custom_call" | custom-call | tf_op jit(solution)/shard_map/near_sums/pallas_call | solution.py:613
  43.6 0.0 collective-permute-done.8.refs_3_
  43.6 2.9 %collective-permute-done.9.refs_4_ = f32[5,32,128]{2,1,0:T(8,128)S(1)} collective-permute-done((f32[5,32,128]{2,1,0:T(8,128)S(1)}, f32[5,32,128]{2,1,0:T(8,128)S(1)}, u32[]{:S(2)}, u32[]{:S(2)}) %collective-permute-start.9) | collective-permute-done | bytes 81952 | tf_op jit(solution)/shard_map/ppermute | solution.py:43
  46.5 0.0 collective-permute-done.6.refs_1_
  46.5 0.0 collective-permute-done.5.refs_0_
  46.5 0.0 collective-permute-done.7.refs_2_
  46.5 0.9 %total_sums.1 = f32[4,45]{1,0:T(4,128)} custom-call(f32[10,32,128]{2,1,0:T(8,128)S(1)} %collective-permute-done.5.refs_0_, f32[10,32,128]{2,1,0:T(8,128)S(1)} %collective-permute-done.6.refs_1_, f32[10,32,128]{2,1,0:T(8,128)S(1)} %collective-permute-done.7.refs_2_, f32[5,32,128]{2,1,0:T(8,128)S(1)} %collective-permute-done.8.refs_3_, ...), custom_call_target="tpu_custom_call" | custom-call | tf_op jit(solution)/shard_map/total_sums/pallas_call | solution.py:649
  (5 shorter events, 0.0 us)
Async XLA Ops:
  1.5 9.1 %collective-permute-start.1 = (f32[40,128]{1,0:T(8,128)S(1)}, f32[40,128]{1,0:T(8,128)S(1)}, u32[]{:S(2)}, u32[]{:S(2)}) collective-permute-start(f32[40,128]{1,0:T(8,128)S(1)} %packed_own.1.own_ref), channel_id=1, source_target_pairs={{0,3},{1,0},{2,1},{3,2},{4,7},{5,4},{6,5},{7,6},{8,11},{9,8},{10,9... | collective-permute-start | bytes 61448 | tf_op jit(solution)/shard_map/ppermute | solution.py:43
  6.6 5.6 %collective-permute-start = (f32[40,128]{1,0:T(8,128)S(1)}, f32[40,128]{1,0:T(8,128)S(1)}, u32[]{:S(2)}, u32[]{:S(2)}) collective-permute-start(f32[40,128]{1,0:T(8,128)S(1)} %packed_own.1.own_ref), channel_id=1, source_target_pairs={{0,1},{1,2},{2,3},{3,0},{4,5},{5,6},{6,7},{7,4},{8,9},{9,10},{10,1... | collective-permute-start | bytes 61448 | tf_op jit(solution)/shard_map/ppermute | solution.py:43
  12.2 4.1 %collective-permute-start.2 = (f32[3,32,128]{2,1,0:T(8,128)S(1)}, f32[3,32,128]{2,1,0:T(8,128)S(1)}, u32[]{:S(2)}, u32[]{:S(2)}) collective-permute-start(f32[3,32,128]{2,1,0:T(8,128)S(1)} %pad_maximum_fusion.1), channel_id=1, source_target_pairs={{0,16},{1,17},{2,18},{3,19},{4,20},{5,21},{6,22},{7,23},{8,24},{9,... | collective-permute-start | bytes 147464 | tf_op jit(solution)/shard_map/ppermute | solution.py:43
  16.4 4.0 %collective-permute-start.4 = (f32[2,3,32,128]{3,2,1,0:T(8,128)S(1)}, f32[2,3,32,128]{3,2,1,0:T(8,128)S(1)}, u32[]{:S(2)}, u32[]{:S(2)}) collective-permute-start(f32[2,3,32,128]{3,2,1,0:T(8,128)S(1)} %pad_maximum_fusion.plane_ref), channel_id=1, source_target_pairs={{0,12},{1,13},{2,14},{3,15},{4,0},{5,1},{6,2},{7,3},{8,4},{9,5},{1... | collective-permute-start | bytes 294920 | tf_op jit(solution)/shard_map/ppermute | solution.py:43
  16.5 5.1 %collective-permute-start.3 = (f32[2,3,32,128]{3,2,1,0:T(8,128)S(1)}, f32[2,3,32,128]{3,2,1,0:T(8,128)S(1)}, u32[]{:S(2)}, u32[]{:S(2)}) collective-permute-start(f32[2,3,32,128]{3,2,1,0:T(8,128)S(1)} %pad_maximum_fusion.plane_ref), channel_id=1, source_target_pairs={{0,4},{1,5},{2,6},{3,7},{4,8},{5,9},{6,10},{7,11},{8,12},{9,13},{1... | collective-permute-start | bytes 294920 | tf_op jit(solution)/shard_map/ppermute | solution.py:43
  32.4 14.1 %collective-permute-start.6 = (f32[10,32,128]{2,1,0:T(8,128)S(1)}, f32[10,32,128]{2,1,0:T(8,128)S(1)}, u32[]{:S(2)}, u32[]{:S(2)}) collective-permute-start(f32[10,32,128]{2,1,0:T(8,128)S(1)} %get-tuple-element.59), channel_id=1, source_target_pairs={{0,16},{1,17},{2,18},{3,19},{4,20},{5,21},{6,22},{7,23},{8,24},{9,... | collective-permute-start | bytes 491528 | tf_op jit(solution)/shard_map/ppermute | solution.py:43
  36.5 10.0 %collective-permute-start.5 = (f32[10,32,128]{2,1,0:T(8,128)S(1)}, f32[10,32,128]{2,1,0:T(8,128)S(1)}, u32[]{:S(2)}, u32[]{:S(2)}) collective-permute-start(f32[10,32,128]{2,1,0:T(8,128)S(1)} %get-tuple-element.58), channel_id=1, source_target_pairs={{0,28},{1,29},{2,30},{3,31},{4,16},{5,17},{6,18},{7,19},{8,20},{9,... | collective-permute-start | bytes 491528 | tf_op jit(solution)/shard_map/ppermute | solution.py:43
  36.6 10.0 %collective-permute-start.7 = (f32[10,32,128]{2,1,0:T(8,128)S(1)}, f32[10,32,128]{2,1,0:T(8,128)S(1)}, u32[]{:S(2)}, u32[]{:S(2)}) collective-permute-start(f32[10,32,128]{2,1,0:T(8,128)S(1)} %get-tuple-element.60), channel_id=1, source_target_pairs={{0,20},{1,21},{2,22},{3,23},{4,24},{5,25},{6,26},{7,27},{8,28},{9,... | collective-permute-start | bytes 491528 | tf_op jit(solution)/shard_map/ppermute | solution.py:43
  39.9 3.7 %collective-permute-start.8 = (f32[5,32,128]{2,1,0:T(8,128)S(1)}, f32[5,32,128]{2,1,0:T(8,128)S(1)}, u32[]{:S(2)}, u32[]{:S(2)}) collective-permute-start(f32[5,32,128]{2,1,0:T(8,128)S(1)} %get-tuple-element.61), channel_id=1, source_target_pairs={{0,12},{1,13},{2,14},{3,15},{4,0},{5,1},{6,2},{7,3},{8,4},{9,5},{1... | collective-permute-start | bytes 245768 | tf_op jit(solution)/shard_map/ppermute | solution.py:43
  40.7 5.9 %collective-permute-start.9 = (f32[5,32,128]{2,1,0:T(8,128)S(1)}, f32[5,32,128]{2,1,0:T(8,128)S(1)}, u32[]{:S(2)}, u32[]{:S(2)}) collective-permute-start(f32[5,32,128]{2,1,0:T(8,128)S(1)} %get-tuple-element.62), channel_id=1, source_target_pairs={{0,4},{1,5},{2,6},{3,7},{4,8},{5,9},{6,10},{7,11},{8,12},{9,13},{1... | collective-permute-start | bytes 245768 | tf_op jit(solution)/shard_map/ppermute | solution.py:43

commit v7 on v6

--- a/solution.py
+++ b/solution.py
@@ -19,10 +19,10 @@
 CENTRE = WINDOW // 2
 SUM_ROWS = 48
 PACK_ROWS = L2 + 8
-PIECES = 3
+PIECES = 1
 PIECE = WINDOW // PIECES
 PIECE_ROWS = PIECE * L2
-SPLIT_STEPS = 3
+SPLIT_STEPS = 9
 CHUNK = 23
 MESH_AXES = ("gx", "gy", "gz")
 
@@ -159,7 +159,7 @@
             pltpu.VMEM((SPLIT_STEPS, PIECE_ROWS // SPLIT_STEPS, ROWS), f32),
             pltpu.SemaphoreType.DMA((SPLIT_STEPS,)),
         ],
-        compiler_params=pltpu.CompilerParams(vmem_limit_bytes=8 * MIB),
+        compiler_params=pltpu.CompilerParams(vmem_limit_bytes=12 * MIB),
         cost_estimate=pl.CostEstimate(
             flops=MIB, bytes_accessed=4 * PIECE_ROWS * ROWS, transcendentals=0
         ),
@@ -338,31 +338,41 @@
 
 
 def early_cells():
-    return [cell for cell in range(WINDOW) if cell // 5 % 3 == 1]
-
-
-def early_kernel(plane_ref, member_ref, tile_ref, image_ref, column, window):
+    return [cell for cell in range(WINDOW) if cell // 15 == 1 or cell // 5 % 3 == 1]
+
+
+def near_slabs(own_ref, middle_refs, side_refs):
     def near(dx, dy, slab):
-        return plane_ref[dx % plane_ref.shape[0], slab]
-
+        if dx == 1:
+            return own_ref[slab] if dy == 1 else middle_refs[dy // 2][slab]
+        ref = side_refs[dy]
+        return ref[dx // 2 % ref.shape[0], slab]
+
+    return near
+
+
+def early_kernel(
+    own_ref, south_ref, north_ref, side_ref, member_ref, tile_ref, image_ref, column, window
+):
+    near = near_slabs(own_ref, (south_ref, north_ref), (None, side_ref, None))
     for cell in early_cells():
         set_window(window, near, member_ref, cell)
     for cell in early_cells():
         set_column(column, window, tile_ref, cell, image_ref[cell])
 
 
-def early_columns(plane, member, tile, images):
+def early_columns(*operands):
     return pl.pallas_call(
         early_kernel,
         out_shape=(
             jax.ShapeDtypeStruct((ROWS, 4 * LANES), bf16),
             jax.ShapeDtypeStruct((2 * ROWS, 2 * LANES), bf16),
         ),
-        in_specs=in_vmem(4),
+        in_specs=in_vmem(len(operands)),
         out_specs=tuple(in_vmem(2)),
         compiler_params=pltpu.CompilerParams(vmem_limit_bytes=8 * MIB),
         name="early_columns",
-    )(plane, member, tile, images)
+    )(*operands)
 
 
 def sweep_over(parts, chunks, source, use_image, slots):
@@ -445,10 +455,7 @@
     column, window, other, slot_a, slot_b, final = refs[8 + 2 * len(stage) :]
     slots = (slot_a, slot_b)
 
-    def near(dx, dy, slab):
-        ref = south_ref if dy == 0 else north_ref
-        return ref[dx % ref.shape[0], slab]
-
+    near = near_slabs(None, None, (south_ref, None, north_ref))
     for cell in early_cells():
         rows = slice(cell * L2, (cell + 1) * L2)
         column[rows, :] = early_column[rows, :]
@@ -682,21 +689,20 @@
     structure = structure[0]
 
     below, above = shifted(own, (0, 0, 1)), shifted(own, (0, 0, -1))
-    first, second = split_piece(0, structure), split_piece(1, structure)
+    parts = split_piece(0, structure)
     slabs = jnp.stack([own[:L2], below[:L2], above[:L2]])
-    slabs, structure, first, second = lax.optimization_barrier((slabs, structure, first, second))
-    if lax.axis_size("gx") == 2:
-        sides = [shifted(slabs, (1, 0, 0)), slabs]
-    else:
-        sides = [shifted(slabs, (1, 0, 0)), slabs, shifted(slabs, (-1, 0, 0))]
+    slabs, parts = lax.optimization_barrier((slabs, parts))
+    parts = (parts,)
+    sides = shifted(slabs, (1, 0, 0))[None]
+    if lax.axis_size("gx") > 2:
+        sides = jnp.stack([sides[0], shifted(slabs, (-1, 0, 0))])
+    south, north = shifted(slabs, (0, 1, 0)), shifted(slabs, (0, -1, 0))
     prepared = setup(own, below, above, delta_table)
-    plane = jnp.stack(sides)
-    plane, structure, *prepared = lax.optimization_barrier((plane, structure, *prepared))
+    sides, *prepared = lax.optimization_barrier((sides, *prepared))
     member, delta, tile = prepared
-    south, north = shifted(plane, (0, 1, 0)), shifted(plane, (0, -1, 0))
-    parts = (first, second, split_piece(2, structure))
+    side_south, side_north = shifted(sides, (0, 1, 0)), shifted(sides, (0, -1, 0))
     images = first_images(parts, tile)
-    column, window = early_columns(plane, member, tile, images)
+    column, window = early_columns(slabs, south, north, sides, member, tile, images)
 
     table = plane_groups()
     stages = [
@@ -710,7 +716,7 @@
         groups = [table[shift] for shift in stage]
         if number == 0:
             *tiles, column, window = first_stage(
-                groups, parts, column, window, images, south, north, member, tile, delta
+                groups, parts, column, window, images, side_south, side_north, member, tile, delta
             )
         else:
             tiles = next_stage(groups, parts, column, window, tile, delta)

time: 47.8 us -> 46.8 us (0.979)
  Pallas kernels: 28 us -> 25.8 us
  waiting for transfers between devices: 7.34 us -> 8.18 us
    pallas_call x3 -> x1, Pallas kernels: 5.98 us -> 3.78 us  [split_piece(): pl.pallas_call(functools.partial(split_kernel, piece), out_shape=jax.Shap...]
    ppermute x10 -> x12, waiting for transfers between devices: 7.34 us -> 8.18 us  [shifted(): return lax.ppermute(x, MESH_AXES, pairs)]
    ppermute x10 -> x12, starting transfers between devices: 11.4 us -> 11.7 us  [shifted(): return lax.ppermute(x, MESH_AXES, pairs)]
  transfers between devices with their start and end apart: 10 -> 12, of which waited for: 4 -> 4; matrix products, arithmetic and copies ran while one was open for 0% -> 0% of each run, Pallas kernels for 32% -> 29%
where the time goes in v7:
time: 46.8 us; the launch traced here: 46.4 us
  Pallas kernels  25.8 us (55%)
  starting transfers between devices  11.7 us (25%)
  waiting for transfers between devices  8.18 us (17%)
  between operations  0.74 us (2%)
    pallas_call x4, Pallas kernels, stage_call(): pl.pallas_call(functools.partial(kernel, stage), out_shape=tuple(out_shap...  15.9 us
    ppermute x12, starting transfers between devices, shifted(): return lax.ppermute(x, MESH_AXES, pairs)  11.7 us
    ppermute x12, waiting for transfers between devices, shifted(): return lax.ppermute(x, MESH_AXES, pairs)  8.18 us
    pallas_call x1, Pallas kernels, split_piece(): pl.pallas_call(functools.partial(split_kernel, piece), out_shape=jax.Shap...  3.78 us
    pallas_call x1, Pallas kernels, setup(): pl.pallas_call(setup_kernel, out_shape=(jax.ShapeDtypeStruct((WINDOW, 2 *...  0.94 us
  transfers between devices with their start and end apart: 12, of which 4 were waited for; matrix products, arithmetic and copies ran while one was open for 0% of the time, Pallas kernels for 29%

profile of v7, /device:TPU:0, one launch (start us, length us, event | category | flops | bytes accessed | tf_op | source)
XLA Modules:
  0.0 46.4 jit_solution(5339378484620527628)
XLA Ops:
  0.6 0.9 %packed_own.1.own_ref = f32[40,128]{1,0:T(8,128)S(1)} custom-call(f32[4,1024]{1,0:T(4,128)} %bitcast.17, s32[4,45]{1,0:T(4,128)} %bitcast.19, s32[1,4]{1,0:T(1,128)} %bitcast.20), custom_call_target="tpu_custom_call" | custom-call | tf_op jit(solution)/shard_map/packed_own/pallas_call | solution.py:112
  1.5 5.1 %collective-permute-start.1 = (f32[40,128]{1,0:T(8,128)S(1)}, f32[40,128]{1,0:T(8,128)S(1)}, u32[]{:S(2)}, u32[]{:S(2)}) collective-permute-start(f32[40,128]{1,0:T(8,128)S(1)} %packed_own.1.own_ref), channel_id=1, source_target_pairs={{0,3},{1,0},{2,1},{3,2},{4,7},{5,4},{6,5},{7,6},{8,11},{9,8},{10,9... | collective-permute-start | bytes 61448 | tf_op jit(solution)/shard_map/ppermute | solution.py:43
  6.6 0.0 collective-permute-start
  6.6 3.8 %split_piece.1.refs_0_ = bf16[2880,1440]{1,0:T(8,128)(2,1)S(1)} custom-call(f32[1440,1440]{1,0:T(8,128)} %bitcast.16), custom_call_target="tpu_custom_call" | custom-call | flops 1048576 | bytes 8294400 | tf_op jit(solution)/shard_map/split_piece/pallas_call | solution.py:153
  10.4 0.0 collective-permute-done.1.above_ref
  10.5 1.8 %collective-permute-done.below_ref = f32[40,128]{1,0:T(8,128)S(1)} collective-permute-done((f32[40,128]{1,0:T(8,128)S(1)}, f32[40,128]{1,0:T(8,128)S(1)}, u32[]{:S(2)}, u32[]{:S(2)}) %collective-permute-start) | collective-permute-done | bytes 20512 | tf_op jit(solution)/shard_map/ppermute | solution.py:43
  12.2 1.5 %collective-permute-start.4 = (f32[3,32,128]{2,1,0:T(8,128)S(1)}, f32[3,32,128]{2,1,0:T(8,128)S(1)}, u32[]{:S(2)}, u32[]{:S(2)}) collective-permute-start(f32[3,32,128]{2,1,0:T(8,128)S(1)} %pad_maximum_fusion.own_ref), channel_id=1, source_target_pairs={{0,16},{1,17},{2,18},{3,19},{4,20},{5,21},{6,22},{7,23},{8,24},{9,... | collective-permute-start | bytes 147464 | tf_op jit(solution)/shard_map/ppermute | solution.py:43
  13.8 0.0 collective-permute-start.3
  13.8 0.5 %collective-permute-start.2 = (f32[3,32,128]{2,1,0:T(8,128)S(1)}, f32[3,32,128]{2,1,0:T(8,128)S(1)}, u32[]{:S(2)}, u32[]{:S(2)}) collective-permute-start(f32[3,32,128]{2,1,0:T(8,128)S(1)} %pad_maximum_fusion.own_ref), channel_id=1, source_target_pairs={{0,4},{1,5},{2,6},{3,7},{4,8},{5,9},{6,10},{7,11},{8,12},{9,13},{1... | collective-permute-start | bytes 147464 | tf_op jit(solution)/shard_map/ppermute | solution.py:43
  14.3 0.9 %setup.1 = (f32[45,256]{1,0:T(8,128)S(1)}, f32[32,256]{1,0:T(8,128)S(1)}, f32[32,256]{1,0:T(8,128)S(1)}) custom-call(f32[40,128]{1,0:T(8,128)S(1)} %packed_own.1.own_ref, f32[40,128]{1,0:T(8,128)S(1)} %collective-permute-done.below_ref, f32[40,128]{1,0:T(8,128)S(1)} %collective-permute-done.1.above_ref, f32[4,1024]{1,0:T(4,128)} %table_hbm.1), custom_call_target="tpu_custom_call" | custom-call | tf_op jit(solution)/shard_map/setup/pallas_call | solution.py:211
  15.2 1.1 %collective-permute-done.4 = f32[3,32,128]{2,1,0:T(8,128)S(1)} collective-permute-done((f32[3,32,128]{2,1,0:T(8,128)S(1)}, f32[3,32,128]{2,1,0:T(8,128)S(1)}, u32[]{:S(2)}, u32[]{:S(2)}) %collective-permute-start.4) | collective-permute-done | bytes 49184 | tf_op jit(solution)/shard_map/ppermute | solution.py:43
  16.4 0.2 collective-permute-start.6
  16.5 0.3 collective-permute-start.5
  16.9 0.9 %first_images.1.image_ref.refs_3_ = f32[45,32,256]{2,1,0:T(8,128)S(1)} custom-call(bf16[2880,1440]{1,0:T(8,128)(2,1)S(1)} %split_piece.1.refs_0_, f32[32,256]{1,0:T(8,128)S(1)} %get-tuple-element.37.refs_1_.tile_ref.refs_7_.refs_3_), custom_call_target="tpu_custom_call" | custom-call | tf_op jit(solution)/shard_map/first_images/pallas_call | solution.py:258
  17.8 0.0 collective-permute-done.3.north_ref
  17.8 0.0 collective-permute-done.2.south_ref
  17.8 0.9 %early_columns.1 = (bf16[1440,512]{1,0:T(8,128)(2,1)S(1)}, bf16[2880,256]{1,0:T(8,128)(2,1)S(1)}) custom-call(f32[3,32,128]{2,1,0:T(8,128)S(1)} %pad_maximum_fusion.own_ref, f32[3,32,128]{2,1,0:T(8,128)S(1)} %collective-permute-done.2.south_ref, f32[3,32,128]{2,1,0:T(8,128)S(1)} %collective-permute-done.3.north_ref, f32[1,3,32,128]{3,2,1,0:T(8,128)S(1)} %bitcast.15, ...), custom_call_target="tpu_custom_call" | custom-call | tf_op jit(solution)/shard_map/early_columns/pallas_call | solution.py:365
  18.7 0.0 collective-permute-done.6.refs_5_
  18.7 1.8 %collective-permute-done.5.refs_4_ = f32[1,3,32,128]{3,2,1,0:T(8,128)S(1)} collective-permute-done((f32[1,3,32,128]{3,2,1,0:T(8,128)S(1)}, f32[1,3,32,128]{3,2,1,0:T(8,128)S(1)}, u32[]{:S(2)}, u32[]{:S(2)}) %collective-permute-start.5) | collective-permute-done | bytes 49184 | tf_op jit(solution)/shard_map/ppermute | solution.py:43
  20.5 10.6 %shard_map.68 = (f32[10,32,128]{2,1,0:T(8,128)S(1)}, f32[10,32,128]{2,1,0:T(8,128)S(1)}, bf16[1440,512]{1,0:T(8,128)(2,1)S(1)}, bf16[2880,256]{1,0:T(8,128)(2,1)S(1)}) custom-call(bf16[2880,1440]{1,0:T(8,128)(2,1)S(1)} %split_piece.1.refs_0_, bf16[1440,512]{1,0:T(8,128)(2,1)S(1)} %get-tuple-element.38.refs_1_, ...), custom_call_target="tpu_custom_call" | custom-call | flops 6370099200 | bytes 1048576 | tf_op jit(solution)/shard_map/pallas_call | solution.py:515
  31.1 1.4 %collective-permute-start.8 = (f32[10,32,128]{2,1,0:T(8,128)S(1)}, f32[10,32,128]{2,1,0:T(8,128)S(1)}, u32[]{:S(2)}, u32[]{:S(2)}) collective-permute-start(f32[10,32,128]{2,1,0:T(8,128)S(1)} %get-tuple-element.53), channel_id=1, source_target_pairs={{0,16},{1,17},{2,18},{3,19},{4,20},{5,21},{6,22},{7,23},{8,24},{9,... | collective-permute-start | bytes 491528 | tf_op jit(solution)/shard_map/ppermute | solution.py:43
  32.5 2.6 %shard_map.70 = (f32[10,32,128]{2,1,0:T(8,128)S(1)}, f32[10,32,128]{2,1,0:T(8,128)S(1)}, f32[10,32,128]{2,1,0:T(8,128)S(1)}, f32[10,32,128]{2,1,0:T(8,128)S(1)}) custom-call(bf16[2880,1440]{1,0:T(8,128)(2,1)S(1)} %split_piece.1.refs_0_, bf16[1440,512]{1,0:T(8,128)(2,1)S(1)} %get-tuple-element.41.refs_1_, bf16[2880,256]{1,0:T(8,128)(2,1)S(1)} %get-tuple-element.42.refs_2_, ...), custom_call_target="tpu_custom_call" | custom-call | flops 530841600 | bytes 1048576 | tf_op jit(solution)/shard_map/pallas_call | solution.py:515
  35.0 0.0 collective-permute-start.7
  35.1 1.7 %collective-permute-start.9 = (f32[10,32,128]{2,1,0:T(8,128)S(1)}, f32[10,32,128]{2,1,0:T(8,128)S(1)}, u32[]{:S(2)}, u32[]{:S(2)}) collective-permute-start(f32[10,32,128]{2,1,0:T(8,128)S(1)} %get-tuple-element.54), channel_id=1, source_target_pairs={{0,20},{1,21},{2,22},{3,23},{4,24},{5,25},{6,26},{7,27},{8,28},{9,... | collective-permute-start | bytes 491528 | tf_op jit(solution)/shard_map/ppermute | solution.py:43
  36.8 1.6 %shard_map.71 = (f32[5,32,128]{2,1,0:T(8,128)S(1)}, f32[5,32,128]{2,1,0:T(8,128)S(1)}, f32[5,32,128]{2,1,0:T(8,128)S(1)}, f32[5,32,128]{2,1,0:T(8,128)S(1)}) custom-call(bf16[2880,1440]{1,0:T(8,128)(2,1)S(1)} %split_piece.1.refs_0_, bf16[1440,512]{1,0:T(8,128)(2,1)S(1)} %get-tuple-element.41.refs_1_, bf16[2880,256]{1,0:T(8,128)(2,1)S(1)} %get-tuple-element.42.refs_2_, ...), custom_call_target="tpu_custom_call" | custom-call | flops 530841600 | bytes 1048576 | tf_op jit(solution)/shard_map/pallas_call | solution.py:515
  38.4 0.4 collective-permute-start.10
  38.8 0.4 collective-permute-start.11
  39.2 1.3 %shard_map.69 = (f32[5,32,128]{2,1,0:T(8,128)S(1)}, f32[5,32,128]{2,1,0:T(8,128)S(1)}, f32[32,128]{1,0:T(8,128)S(1)}) custom-call(bf16[2880,1440]{1,0:T(8,128)(2,1)S(1)} %split_piece.1.refs_0_, bf16[1440,512]{1,0:T(8,128)(2,1)S(1)} %get-tuple-element.41.refs_1_, bf16[2880,256]{1,0:T(8,128)(2,1)S(1)} %get-tuple-element.42.refs_2_, ...), custom_call_target="tpu_custom_call" | custom-call | flops 530841600 | bytes 1048576 | tf_op jit(solution)/shard_map/pallas_call | solution.py:515
  40.5 0.9 %turned_tiles.1.refs_1_.refs_5_ = f32[45,32,128]{2,1,0:T(8,128)S(1)} custom-call(f32[10,32,128]{2,1,0:T(8,128)S(1)} %get-tuple-element.44.refs_0_, f32[10,32,128]{2,1,0:T(8,128)S(1)} %get-tuple-element.45.refs_1_, f32[10,32,128]{2,1,0:T(8,128)S(1)} %get-tuple-element.46.refs_2_, f32[5,32,128]{2,1,0:T(8,128)S(1)} %get-tuple-element.47.refs_3_, ...), custom_call_target="tpu_custom_call" | custom-call | flops 1048576 | bytes 2097152 | tf_op jit(solution)/shard_map/turned_tiles/pallas_call | solution.py:591
  41.3 0.7 %near_sums.1 = (f32[48,128]{1,0:T(8,128)S(1)}, f32[4,1024]{1,0:T(4,128)}) custom-call(f32[5,32,128]{2,1,0:T(8,128)S(1)} %get-tuple-element.43.refs_0_, f32[45,32,128]{2,1,0:T(8,128)S(1)} %turned_tiles.1.refs_1_.refs_5_, f32[32,128]{1,0:T(8,128)S(1)} %get-tuple-element.50.refs_2_), custom_call_target="tpu_custom_call" | custom-call | tf_op jit(solution)/shard_map/near_sums/pallas_call | solution.py:620
  42.1 0.0 collective-permute-done.10.refs_3_
  42.1 3.5 %collective-permute-done.11.refs_4_ = f32[5,32,128]{2,1,0:T(8,128)S(1)} collective-permute-done((f32[5,32,128]{2,1,0:T(8,128)S(1)}, f32[5,32,128]{2,1,0:T(8,128)S(1)}, u32[]{:S(2)}, u32[]{:S(2)}) %collective-permute-start.11) | collective-permute-done | bytes 81952 | tf_op jit(solution)/shard_map/ppermute | solution.py:43
  45.5 0.0 collective-permute-done.8.refs_1_
  45.5 0.0 collective-permute-done.7.refs_0_
  45.5 0.0 collective-permute-done.9.refs_2_
  45.5 0.9 %total_sums.1 = f32[4,45]{1,0:T(4,128)} custom-call(f32[10,32,128]{2,1,0:T(8,128)S(1)} %collective-permute-done.7.refs_0_, f32[10,32,128]{2,1,0:T(8,128)S(1)} %collective-permute-done.8.refs_1_, f32[10,32,128]{2,1,0:T(8,128)S(1)} %collective-permute-done.9.refs_2_, f32[5,32,128]{2,1,0:T(8,128)S(1)} %collective-permute-done.10.refs_3_, ...), custom_call_target="tpu_custom_call" | custom-call | tf_op jit(solution)/shard_map/total_sums/pallas_call | solution.py:656
  (4 shorter events, 0.0 us)
Async XLA Ops:
  1.5 8.9 %collective-permute-start.1 = (f32[40,128]{1,0:T(8,128)S(1)}, f32[40,128]{1,0:T(8,128)S(1)}, u32[]{:S(2)}, u32[]{:S(2)}) collective-permute-start(f32[40,128]{1,0:T(8,128)S(1)} %packed_own.1.own_ref), channel_id=1, source_target_pairs={{0,3},{1,0},{2,1},{3,2},{4,7},{5,4},{6,5},{7,6},{8,11},{9,8},{10,9... | collective-permute-start | bytes 61448 | tf_op jit(solution)/shard_map/ppermute | solution.py:43
  6.6 5.6 %collective-permute-start = (f32[40,128]{1,0:T(8,128)S(1)}, f32[40,128]{1,0:T(8,128)S(1)}, u32[]{:S(2)}, u32[]{:S(2)}) collective-permute-start(f32[40,128]{1,0:T(8,128)S(1)} %packed_own.1.own_ref), channel_id=1, source_target_pairs={{0,1},{1,2},{2,3},{3,0},{4,5},{5,6},{6,7},{7,4},{8,9},{9,10},{10,1... | collective-permute-start | bytes 61448 | tf_op jit(solution)/shard_map/ppermute | solution.py:43
  12.2 4.1 %collective-permute-start.4 = (f32[3,32,128]{2,1,0:T(8,128)S(1)}, f32[3,32,128]{2,1,0:T(8,128)S(1)}, u32[]{:S(2)}, u32[]{:S(2)}) collective-permute-start(f32[3,32,128]{2,1,0:T(8,128)S(1)} %pad_maximum_fusion.own_ref), channel_id=1, source_target_pairs={{0,16},{1,17},{2,18},{3,19},{4,20},{5,21},{6,22},{7,23},{8,24},{9,... | collective-permute-start | bytes 147464 | tf_op jit(solution)/shard_map/ppermute | solution.py:43
  13.8 4.0 %collective-permute-start.3 = (f32[3,32,128]{2,1,0:T(8,128)S(1)}, f32[3,32,128]{2,1,0:T(8,128)S(1)}, u32[]{:S(2)}, u32[]{:S(2)}) collective-permute-start(f32[3,32,128]{2,1,0:T(8,128)S(1)} %pad_maximum_fusion.own_ref), channel_id=1, source_target_pairs={{0,12},{1,13},{2,14},{3,15},{4,0},{5,1},{6,2},{7,3},{8,4},{9,5},{1... | collective-permute-start | bytes 147464 | tf_op jit(solution)/shard_map/ppermute | solution.py:43
  13.8 4.0 %collective-permute-start.2 = (f32[3,32,128]{2,1,0:T(8,128)S(1)}, f32[3,32,128]{2,1,0:T(8,128)S(1)}, u32[]{:S(2)}, u32[]{:S(2)}) collective-permute-start(f32[3,32,128]{2,1,0:T(8,128)S(1)} %pad_maximum_fusion.own_ref), channel_id=1, source_target_pairs={{0,4},{1,5},{2,6},{3,7},{4,8},{5,9},{6,10},{7,11},{8,12},{9,13},{1... | collective-permute-start | bytes 147464 | tf_op jit(solution)/shard_map/ppermute | solution.py:43
  16.4 2.3 %collective-permute-start.6 = (f32[1,3,32,128]{3,2,1,0:T(8,128)S(1)}, f32[1,3,32,128]{3,2,1,0:T(8,128)S(1)}, u32[]{:S(2)}, u32[]{:S(2)}) collective-permute-start(f32[1,3,32,128]{3,2,1,0:T(8,128)S(1)} %bitcast.13), channel_id=1, source_target_pairs={{0,12},{1,13},{2,14},{3,15},{4,0},{5,1},{6,2},{7,3},{8,4},{9,5},{1... | collective-permute-start | bytes 147464 | tf_op jit(solution)/shard_map/ppermute | solution.py:43
  16.5 4.0 %collective-permute-start.5 = (f32[1,3,32,128]{3,2,1,0:T(8,128)S(1)}, f32[1,3,32,128]{3,2,1,0:T(8,128)S(1)}, u32[]{:S(2)}, u32[]{:S(2)}) collective-permute-start(f32[1,3,32,128]{3,2,1,0:T(8,128)S(1)} %bitcast.14), channel_id=1, source_target_pairs={{0,4},{1,5},{2,6},{3,7},{4,8},{5,9},{6,10},{7,11},{8,12},{9,13},{1... | collective-permute-start | bytes 147464 | tf_op jit(solution)/shard_map/ppermute | solution.py:43
  31.1 14.4 %collective-permute-start.8 = (f32[10,32,128]{2,1,0:T(8,128)S(1)}, f32[10,32,128]{2,1,0:T(8,128)S(1)}, u32[]{:S(2)}, u32[]{:S(2)}) collective-permute-start(f32[10,32,128]{2,1,0:T(8,128)S(1)} %get-tuple-element.53), channel_id=1, source_target_pairs={{0,16},{1,17},{2,18},{3,19},{4,20},{5,21},{6,22},{7,23},{8,24},{9,... | collective-permute-start | bytes 491528 | tf_op jit(solution)/shard_map/ppermute | solution.py:43
  35.0 10.5 %collective-permute-start.7 = (f32[10,32,128]{2,1,0:T(8,128)S(1)}, f32[10,32,128]{2,1,0:T(8,128)S(1)}, u32[]{:S(2)}, u32[]{:S(2)}) collective-permute-start(f32[10,32,128]{2,1,0:T(8,128)S(1)} %get-tuple-element.52), channel_id=1, source_target_pairs={{0,28},{1,29},{2,30},{3,31},{4,16},{5,17},{6,18},{7,19},{8,20},{9,... | collective-permute-start | bytes 491528 | tf_op jit(solution)/shard_map/ppermute | solution.py:43
  35.1 10.5 %collective-permute-start.9 = (f32[10,32,128]{2,1,0:T(8,128)S(1)}, f32[10,32,128]{2,1,0:T(8,128)S(1)}, u32[]{:S(2)}, u32[]{:S(2)}) collective-permute-start(f32[10,32,128]{2,1,0:T(8,128)S(1)} %get-tuple-element.54), channel_id=1, source_target_pairs={{0,20},{1,21},{2,22},{3,23},{4,24},{5,25},{6,26},{7,27},{8,28},{9,... | collective-permute-start | bytes 491528 | tf_op jit(solution)/shard_map/ppermute | solution.py:43
  38.4 3.7 %collective-permute-start.10 = (f32[5,32,128]{2,1,0:T(8,128)S(1)}, f32[5,32,128]{2,1,0:T(8,128)S(1)}, u32[]{:S(2)}, u32[]{:S(2)}) collective-permute-start(f32[5,32,128]{2,1,0:T(8,128)S(1)} %get-tuple-element.55), channel_id=1, source_target_pairs={{0,12},{1,13},{2,14},{3,15},{4,0},{5,1},{6,2},{7,3},{8,4},{9,5},{1... | collective-permute-start | bytes 245768 | tf_op jit(solution)/shard_map/ppermute | solution.py:43
  38.8 6.7 %collective-permute-start.11 = (f32[5,32,128]{2,1,0:T(8,128)S(1)}, f32[5,32,128]{2,1,0:T(8,128)S(1)}, u32[]{:S(2)}, u32[]{:S(2)}) collective-permute-start(f32[5,32,128]{2,1,0:T(8,128)S(1)} %get-tuple-element.56), channel_id=1, source_target_pairs={{0,4},{1,5},{2,6},{3,7},{4,8},{5,9},{6,10},{7,11},{8,12},{9,13},{1... | collective-permute-start | bytes 245768 | tf_op jit(solution)/shard_map/ppermute | solution.py:43
